TPU v7x, 32 devices: a whole 2x2x4 slice. The times are simulated.
32 devices in a mesh: grp: 2 (over x), row: 16 (over z, y, core).
Axes of the slice: x: 2, y: 2, z: 4, core: 2. Of those that a mesh axis runs over, the one named last changes fastest.
Arguments:
- features: bfloat16 [64, 128, 384], P(('grp', 'row')), parts along dimension 0, may hold values from -6 to 6
- decay_rate: float32 [4, 6, 64, 128], P(None, None, ('grp', 'row')), parts along dimension 2, may hold values from 0 to 2
- input_proj: float32 [4, 16, 64, 128], P(None, None, ('grp', 'row')), parts along dimension 2, may hold values from -1 to 1
- read_proj: float32 [4, 16, 64, 128], P(None, None, ('grp', 'row')), parts along dimension 2, may hold values from -1 to 1
- skip_gain: float32 [384], replicated, may hold values from 0.5 to 1.5
- out_weight: bfloat16 [384, 384], replicated, may hold values from -0.3125 to 0.3125
- out_cotangent: bfloat16 [64, 128, 384], P(('grp', 'row')), parts along dimension 0, may hold values from -6 to 6
Outputs:
- grad_features: bfloat16 [64, 128, 384], P(('grp', 'row')), parts along dimension 0
- grad_rate: float32 [4, 6, 64, 128], P(None, None, ('grp', 'row')), parts along dimension 2
- grad_input: float32 [4, 16, 64, 128], P(None, None, ('grp', 'row')), parts along dimension 2
- grad_read: float32 [4, 16, 64, 128], P(None, None, ('grp', 'row')), parts along dimension 2
- grad_skip: float32 [768], P('grp'), parts along dimension 0
- grad_out_weight: float32 [768, 384], P('grp'), parts along dimension 0
There are 2 independent parts, one for each index of `grp`. A program takes and returns all parts, laid end to end along the dimension named above; an argument that names none is the same for every part. Nothing has to cross between parts.
All inputs are finite; a program needn't handle non-finite values.
Results may differ from a plain program's by a relative error of at most 0.0065.
Values may be sent and summed in bfloat16 or wider, within the bound.
No kernel may reach another device: no remote copies, remote signals or barrier semaphores. Data moves between devices by JAX's collectives and lax.ppermute only.
A program may use at most 64 MiB of HBM per device.

v0:
```python
import functools

import jax
import jax.numpy as jnp
from jax import lax
from jax.experimental import pallas as pl
from jax.experimental.pallas import tpu as pltpu
from jax.sharding import PartitionSpec as P

F32 = jnp.float32
BF16 = jnp.bfloat16
HI = lax.Precision.HIGHEST
LANES = 128
FAR = -1e30


def iota(shape, dim):
    return lax.broadcasted_iota(jnp.int32, shape, dim)


def nt(a, b):
    return lax.dot_general(a, b, (((1,), (1,)), ((), ())), preferred_element_type=F32)


def nn(a, b):
    return jnp.dot(a, b, preferred_element_type=F32)


def tn(a, b):
    return lax.dot_general(a, b, (((0,), (0,)), ((), ())), preferred_element_type=F32)


def split_index(index, sizes):
    parts = []
    for size in reversed(sizes):
        if size & (size - 1) == 0:
            parts.append(index & (size - 1))
            index = index >> (size.bit_length() - 1)
        else:
            parts.append(lax.rem(index, size))
            index = lax.div(index, size)
    return parts[::-1]


def one_hot_rows(count, source_of):
    wanted = source_of(iota((count, 1), 0))
    return (wanted == iota((count, count), 1)).astype(F32).astype(BF16)


class Slots:
    def __init__(self, heads, states):
        self.heads = heads
        self.states = states
        self.inputs = (0, states)
        self.reads = (2 * states, 3 * states)
        pad = -(-heads // 8) * 8
        self.pad = pad
        self.rates = (4 * states, 4 * states + pad)
        self.lows = (4 * states + 2 * pad, 4 * states + 3 * pad)
        self.used = 4 * states + 2 * pad


def scan_block(feats, grads, rows, rates, slots, line, small_ref, row_slice):
    block = feats.shape[0]
    heads = slots.heads
    head_size = feats.shape[1] // heads
    per_group = LANES // head_size
    at_t, at_u = iota((block, block), 0), iota((block, block), 1)
    below, above = at_t > at_u, at_t < at_u
    same = None
    if line < block:
        (line_t, _), (line_u, _) = (
            split_index(at_t, (block // line, line)),
            split_index(at_u, (block // line, line)),
        )
        same = line_t == line_u

    def within(mask):
        return mask if same is None else mask & same

    ends = within(at_t <= at_u).astype(F32)
    starts = within(at_t >= at_u).astype(F32)
    sums = (
        -jnp.dot(rates[0], ends, precision=HI, preferred_element_type=F32),
        -jnp.dot(rates[1], starts, precision=HI, preferred_element_type=F32),
    )
    columns = jnp.transpose(jnp.concatenate(sums, axis=0))
    in_b = [rows[at : at + slots.states].astype(BF16) for at in slots.inputs]
    out_c = [rows[at : at + slots.states].astype(BF16) for at in slots.reads]
    score_down, score_up = tn(out_c[0], in_b[0]), tn(out_c[1], in_b[1])
    scores = jnp.where(
        below, score_down, jnp.where(above, score_up, score_down + score_up)
    )
    lane = iota((block, LANES), 1)
    grad_scores = jnp.zeros((block, block), F32)
    out_parts, grad_parts = [], []
    lane_pad = iota((block, LANES), 1)
    row_sums = jnp.zeros((block, LANES), F32)
    row_at = iota((2 * slots.pad, block), 0)
    col_sums = jnp.zeros((2 * slots.pad, block), F32)
    for group in range(heads // per_group):
        span = slice(group * LANES, (group + 1) * LANES)
        feat_group, grad_group = feats[:, span], grads[:, span]
        mixes, feat_own, grad_own = [], [], []
        for member in range(per_group):
            head = group * per_group + member
            mine = (lane >= member * head_size) & (lane < (member + 1) * head_size)
            feat_head = jnp.where(mine, feat_group, jnp.zeros_like(feat_group))
            grad_head = jnp.where(mine, grad_group, jnp.zeros_like(grad_group))
            up = slots.pad + head
            spread = jnp.where(
                below,
                columns[:, head : head + 1] - sums[0][head : head + 1],
                columns[:, up : up + 1] - sums[1][head : head + 1],
            )
            if same is not None:
                spread = jnp.where(same, spread, FAR)
            kernel = jnp.exp(spread)
            mix = kernel * scores
            grad_mix = nt(grad_group, feat_head)
            grad_scores = grad_scores + kernel * grad_mix
            flow = mix * grad_mix
            flow_down = jnp.where(below, flow, 0.0)
            row_down = jnp.sum(flow_down, axis=1, keepdims=True)
            row_all = jnp.sum(flow, axis=1, keepdims=True)
            col_down = jnp.sum(flow_down, axis=0, keepdims=True)
            col_all = jnp.sum(flow, axis=0, keepdims=True)
            row_sums = jnp.where(lane_pad == head, row_down, row_sums)
            row_sums = jnp.where(lane_pad == up, row_all - row_down, row_sums)
            col_sums = jnp.where(row_at == head, col_down, col_sums)
            col_sums = jnp.where(row_at == up, col_all - col_down, col_sums)
            mixes.append(mix.astype(BF16))
            feat_own.append(feat_head)
            grad_own.append(grad_head)
        out_parts.append(
            nn(jnp.concatenate(mixes, axis=1), jnp.concatenate(feat_own, axis=0))
        )
        grad_parts.append(
            tn(jnp.concatenate(mixes, axis=0), jnp.concatenate(grad_own, axis=0))
        )
    change = col_sums - jnp.transpose(row_sums)[: 2 * slots.pad]
    grad_down = within(at_t >= at_u)
    grad_up = within(at_t <= at_u)
    score_grads = (
        jnp.where(grad_down, grad_scores, 0.0).astype(BF16),
        jnp.where(grad_up, grad_scores, 0.0).astype(BF16),
    )
    for way in (0, 1):
        small_ref[slots.inputs[way] : slots.inputs[way] + slots.states, row_slice] = nn(
            out_c[way], score_grads[way]
        )
        small_ref[slots.reads[way] : slots.reads[way] + slots.states, row_slice] = nt(
            in_b[way], score_grads[way]
        )
        part = change[way * slots.pad : (way + 1) * slots.pad]
        reach = starts if way == 0 else ends
        small_ref[slots.rates[way] : slots.rates[way] + slots.pad, row_slice] = jnp.dot(
            part, reach, precision=HI, preferred_element_type=F32
        )
    return jnp.concatenate(out_parts, axis=1), jnp.concatenate(grad_parts, axis=1)


def pack_kernel(slots, ranks, feat_ref, cot_ref, rate_ref, input_ref, read_ref, out_ref, rows_ref):
    tile_rows, columns, width = feat_ref.shape
    model = cot_ref.shape[2]
    tokens = tile_rows * columns
    narrow = columns // ranks

    def source(at):
        rank, row, column = split_index(at, (ranks, tile_rows, narrow))
        return row * columns + rank * narrow + column

    order = one_hot_rows(tokens, source)
    out_ref[:, :width] = nn(order, feat_ref[...].reshape(tokens, width)).astype(BF16)
    out_ref[:, width : width + model] = nn(order, cot_ref[...].reshape(tokens, model)).astype(BF16)
    rows_ref[...] = jnp.zeros_like(rows_ref)
    for way in (0, 1):
        for row in range(tile_rows):
            span = slice(row * columns, (row + 1) * columns)
            at = slots.inputs[way]
            rows_ref[at : at + slots.states, span] = input_ref[2 + way, :, row, :]
            at = slots.reads[way]
            rows_ref[at : at + slots.states, span] = read_ref[2 + way, :, row, :]
            at = slots.rates[way]
            rate = rate_ref[2 + way, :, row, :]
            rows_ref[at : at + slots.heads, span] = rate
            at = slots.lows[way]
            rows_ref[at : at + slots.heads, span] = rate - rate.astype(BF16).astype(F32)
    out_ref[:, width + model :] = nt(order, rows_ref[...].astype(BF16)).astype(BF16)


def rows_kernel(
    slots, chunk, feat_ref, cot_ref, weight_ref, skip_ref, rate_ref, input_ref, read_ref,
    gx_ref, small_ref, part_ref, skip_out_ref, rows_ref,
):
    tile_rows, columns, width = feat_ref.shape
    tokens = tile_rows * columns
    skip = skip_ref[...]
    rows_ref[...] = jnp.zeros_like(rows_ref)
    partial = jnp.zeros(part_ref.shape, F32)
    skip_part = jnp.zeros((1, width), F32)
    for row in range(tile_rows):
        feats, cots = feat_ref[row], cot_ref[row]
        grads = nt(cots, weight_ref[...]).astype(BF16)
        for way in (0, 1):
            at = slots.inputs[way]
            rows_ref[at : at + slots.states, :] = input_ref[way, :, row, :]
            at = slots.reads[way]
            rows_ref[at : at + slots.states, :] = read_ref[way, :, row, :]
            at = slots.rates[way]
            rows_ref[at : at + slots.heads, :] = rate_ref[way, :, row, :]
        rates = [rows_ref[at : at + slots.pad, :] for at in slots.rates]
        outs, gx = scan_block(
            feats, grads, rows_ref, rates, slots, columns, small_ref,
            slice(row * columns, (row + 1) * columns),
        )
        feat_f32, grad_f32 = feats.astype(F32), grads.astype(F32)
        across = (outs + skip * feat_f32).astype(BF16)
        partial = partial + tn(across, cots)
        gx_ref[row * columns : (row + 1) * columns, :] = gx + skip * grad_f32
        skip_part = skip_part + jnp.sum(feat_f32 * grad_f32, axis=0, keepdims=True)
    part_ref[...] = partial
    if chunk is None:
        skip_out_ref[...] = skip_part
    else:
        high = skip_part.astype(BF16).astype(F32)
        piece = width // chunk
        lane_of = iota((chunk, width), 1)
        start = iota((chunk, width), 0) * piece
        owned = (lane_of >= start) & (lane_of < start + piece)
        spread = jnp.concatenate(
            [jnp.where(owned, high, 0.0), jnp.where(owned, skip_part - high, 0.0)], axis=1
        ).astype(BF16)
        skip_out_ref[...] = nn(spread, skip_places(slots, width, piece))


def skip_places(slots, width, piece):
    place = lax.rem(iota((width, 1), 0), piece) + slots.used
    lane = iota((width, LANES), 1)
    high, low = place == lane, place + piece == lane
    return jnp.concatenate([high.astype(F32), low.astype(F32)], axis=0).astype(BF16)


def cols_kernel(
    slots, ranks, tile_rows, chunk, recv_ref, weight_ref, part_ref, skip_ref,
    back_ref, sum_ref, small_ref,
):
    tokens = recv_ref.shape[0]
    width, model = weight_ref.shape
    line = ranks * tile_rows
    narrow = tokens // line
    block = max(line, min(LANES, tokens))

    def source(at):
        column, rank, row = split_index(at, (narrow, ranks, tile_rows))
        return rank * (tile_rows * narrow) + row * narrow + column

    def source_back(at):
        rank, row, column = split_index(at, (ranks, tile_rows, narrow))
        return column * line + rank * tile_rows + row

    order = one_hot_rows(tokens, source)
    feats = nn(order, recv_ref[:, :width]).astype(BF16)
    cots = nn(order, recv_ref[:, width : width + model]).astype(BF16)
    params = nn(order, recv_ref[:, width + model :])
    grads = nt(cots, weight_ref[...]).astype(BF16)
    small_ref[...] = jnp.zeros_like(small_ref)
    outs, gxs = [], []
    for at in range(0, tokens, block):
        span = slice(at, at + block)
        rows = jnp.transpose(params[span])
        rates = [
            rows[hi : hi + slots.pad] + rows[lo : lo + slots.pad]
            for hi, lo in zip(slots.rates, slots.lows)
        ]
        out, gx = scan_block(
            feats[span], grads[span], rows, rates, slots, line, small_ref, span
        )
        outs.append(out.astype(BF16))
        gxs.append(gx.astype(BF16))
    sum_ref[...] = (part_ref[...] + tn(jnp.concatenate(outs, axis=0), cots)).astype(BF16)
    order_back = one_hot_rows(tokens, source_back)
    back_ref[:, :width] = nn(order_back, jnp.concatenate(gxs, axis=0)).astype(BF16)
    smalls = nt(order_back, small_ref[...].astype(BF16))
    if chunk is not None:
        skip = skip_ref[...]
        smalls = smalls + jnp.concatenate([skip] * ranks, axis=0)
    back_ref[:, width:] = smalls.astype(BF16)


def sum_kernel(ranks, parts_ref, out_ref):
    rows = parts_ref.shape[0] // ranks
    total = parts_ref[:rows, :].astype(F32)
    for rank in range(1, ranks):
        total = total + parts_ref[rank * rows : (rank + 1) * rows, :].astype(F32)
    out_ref[...] = total.astype(BF16)


def finish_kernel(
    slots, ranks, chunk, back_ref, gx_ref, small_ref,
    feat_out, rate_out, input_out, read_out, *skip_out,
):
    tile_rows, columns, width = feat_out.shape
    tokens = tile_rows * columns
    narrow = columns // ranks

    def source(at):
        row, rank, column = split_index(at, (tile_rows, ranks, narrow))
        return rank * (tile_rows * narrow) + row * narrow + column

    order = one_hot_rows(tokens, source)
    total = gx_ref[...] + nn(order, back_ref[:, :width])
    feat_out[...] = total.astype(BF16).reshape(tile_rows, columns, width)
    smalls = nn(order, back_ref[:, width:])
    for row in range(tile_rows):
        span = slice(row * columns, (row + 1) * columns)
        rows = jnp.transpose(smalls[span])
        for way in (0, 1):
            at = slots.inputs[way]
            input_out[way, :, row, :] = small_ref[at : at + slots.states, span]
            input_out[2 + way, :, row, :] = rows[at : at + slots.states]
            at = slots.reads[way]
            read_out[way, :, row, :] = small_ref[at : at + slots.states, span]
            read_out[2 + way, :, row, :] = rows[at : at + slots.states]
            at = slots.rates[way]
            rate_out[way, :, row, :] = small_ref[at : at + slots.heads, span]
            rate_out[2 + way, :, row, :] = rows[at : at + slots.heads]
    if chunk is not None:
        piece = width // chunk
        gathered = back_ref[:chunk, width:].astype(F32)
        for rank in range(1, ranks):
            gathered = gathered + back_ref[rank * chunk : (rank + 1) * chunk, width:].astype(F32)
        places = skip_places(slots, width, piece).astype(F32)
        places = places[:width] + places[width:]
        spread = lax.dot_general(
            gathered, places, (((1,), (1,)), ((), ())), precision=HI, preferred_element_type=F32
        )
        lane_of = iota((chunk, width), 1)
        start = iota((chunk, width), 0) * piece
        owned = (lane_of >= start) & (lane_of < start + piece)
        skip_out[0][...] = jnp.sum(jnp.where(owned, spread, 0.0), axis=0, keepdims=True)


def widen_kernel(in_ref, out_ref):
    out_ref[...] = in_ref[...].astype(F32)


def call(kernel, name, out_shape, operands, scratch=(), flops=0, moved=0):
    return pl.pallas_call(
        kernel,
        name=name,
        out_shape=out_shape,
        scratch_shapes=list(scratch),
        cost_estimate=pl.CostEstimate(flops=flops, bytes_accessed=moved, transcendentals=0),
    )(*operands)


def local(ranks, features, decay_rate, input_proj, read_proj, skip_gain, out_weight, out_cotangent):
    tile_rows, columns, width = features.shape
    model = out_cotangent.shape[2]
    heads, states = decay_rate.shape[1], input_proj.shape[1]
    slots = Slots(heads, states)
    tokens = tile_rows * columns
    chunk = tokens // ranks
    room = chunk * (LANES - slots.used)
    if chunk % 8 or width % chunk or 2 * width > room:
        chunk = None
    shape = jax.ShapeDtypeStruct

    def exchange(array):
        return lax.all_to_all(array, "row", split_axis=0, concat_axis=0, tiled=True)

    packed = call(
        functools.partial(pack_kernel, slots, ranks), "pack",
        shape((tokens, width + model + LANES), BF16),
        (features, out_cotangent, decay_rate, input_proj, read_proj),
        [pltpu.VMEM((LANES, tokens), F32)],
        flops=2 * tokens * tokens * (width + model), moved=4 * tokens * (width + model),
    )
    received = exchange(packed)
    skip_shape = (1, width) if chunk is None else (chunk, LANES)
    gx_rows, small_rows, partial, skip_part = call(
        functools.partial(rows_kernel, slots, chunk), "rows",
        (
            shape((tokens, width), F32),
            shape((LANES, tokens), F32),
            shape((width, model), F32),
            shape(skip_shape, F32),
        ),
        (
            features, out_cotangent, out_weight, skip_gain.reshape(1, width),
            decay_rate, input_proj, read_proj,
        ),
        [pltpu.VMEM((LANES, columns), F32)],
        flops=2 * tokens * width * (2 * model + 3 * columns), moved=8 * tokens * width,
    )
    back, weight_sum = call(
        functools.partial(cols_kernel, slots, ranks, tile_rows, chunk), "cols",
        (shape((tokens, width + LANES), BF16), shape((width, model), BF16)),
        (received, out_weight, partial, skip_part),
        [pltpu.VMEM((LANES, tokens), F32)],
        flops=2 * tokens * width * (2 * model + 3 * columns), moved=8 * tokens * width,
    )
    weight_parts = exchange(weight_sum)
    returned = exchange(back)
    own = call(
        functools.partial(sum_kernel, ranks), "sum",
        shape((width // ranks, model), BF16), (weight_parts,),
        flops=width * model, moved=2 * width * model,
    )
    gathered = exchange(jnp.tile(own, (ranks, 1)))
    outs = [
        shape(features.shape, BF16),
        shape(decay_rate.shape, F32),
        shape(input_proj.shape, F32),
        shape(read_proj.shape, F32),
    ]
    if chunk is not None:
        outs.append(shape((1, width), F32))
    done = call(
        functools.partial(finish_kernel, slots, ranks, chunk), "finish",
        tuple(outs), (returned, gx_rows, small_rows),
        flops=2 * tokens * tokens * width, moved=8 * tokens * width,
    )
    grad_weight = call(
        widen_kernel, "widen", shape((width, model), F32), (gathered,),
        flops=width * model, moved=6 * width * model,
    )
    if chunk is None:
        grad_skip = lax.psum(skip_part, "row").reshape(width)
    else:
        grad_skip = done[4].reshape(width)
    return (*done[:4], grad_skip, grad_weight)


def solution(mesh):
    in_specs = (
        P(("grp", "row"), None, None),
        P(None, None, ("grp", "row"), None),
        P(None, None, ("grp", "row"), None),
        P(None, None, ("grp", "row"), None),
        P(),
        P(),
        P(("grp", "row"), None, None),
    )
    out_specs = (
        P(("grp", "row"), None, None),
        P(None, None, ("grp", "row"), None),
        P(None, None, ("grp", "row"), None),
        P(None, None, ("grp", "row"), None),
        P("grp"),
        P("grp", None),
    )
    body = functools.partial(local, mesh.shape["row"])
    return jax.shard_map(body, mesh=mesh, in_specs=in_specs, out_specs=out_specs, check_vma=False)
```

profile of v0, /device:TPU:0, one launch (start us, length us, event | category | flops | bytes accessed | tf_op | source)
XLA Modules:
  0.0 76.0 jit_solution(4228875843256713385)
XLA Ops:
  0.6 2.2 %pack.1 = bf16[256,896]{1,0:T(8,128)(2,1)} custom-call(bf16[2,128,384]{2,1,0:T(8,128)(2,1)} %feat_ref.3, bf16[2,128,384]{2,1,0:T(8,128)(2,1)} %cot_ref.3, f32[4,6,2,128]{3,2,1,0:T(2,128)} %rate_ref.3, f32[4,16,2,128]{3,2,1,0:T(2,128)} %input_ref.3, f32[4,16,2,128]{3,2,1,0:T(2,128)} %read_ref.3), custom_call_target="tpu_custom_call" | custom-call | flops 100663296 | bytes 786432 | tf_op jit(solution)/shard_map/pack/pallas_call | solution.py:349
  2.8 0.0 copy-start.3
  2.8 7.5 %all-to-all-start = ((bf16[16,16,896]{2,1,0:T(8,128)(2,1)}), bf16[16,16,896]{2,1,0:T(8,128)(2,1)S(1)}, u32[]{:S(2)}, u32[]{:S(2)}) async-start(bf16[16,16,896]{2,1,0:T(8,128)(2,1)} %bitcast.7), calls=%async_computation | async-start | bytes 917504 | tf_op jit(solution)/shard_map/all_to_all | solution.py:371
  10.4 0.0 copy-done.3
  10.4 0.6 reshape.31.skip_ref
  11.0 5.1 %rows.1 = (f32[256,384]{1,0:T(8,128)}, f32[128,256]{1,0:T(8,128)}, f32[384,384]{1,0:T(8,128)}, f32[16,128]{1,0:T(8,128)}) custom-call(bf16[2,128,384]{2,1,0:T(8,128)(2,1)} %feat_ref.3, bf16[2,128,384]{2,1,0:T(8,128)(2,1)} %cot_ref.3, bf16[384,384]{1,0:T(8,128)(2,1)} %weight_ref.3, f32[1,384]{1,0:T(1,128)} %reshape.31.skip_ref, f32[4,6,2,128]{3,2,1,0:T(2,128)} %rate_ref.3, ...), custom_call_target="tpu_custom_call" | custom-call | flops 226492416 | bytes 786432 | tf_op jit(solution)/shard_map/rows/pallas_call | solution.py:349
  16.0 7.6 %all-to-all-done = bf16[16,16,896]{2,1,0:T(8,128)(2,1)S(1)} async-done(((bf16[16,16,896]{2,1,0:T(8,128)(2,1)}), bf16[16,16,896]{2,1,0:T(8,128)(2,1)S(1)}, u32[]{:S(2)}, u32[]{:S(2)}) %all-to-all-start) | async-done | bytes 458784 | tf_op jit(solution)/shard_map/all_to_all | solution.py:371
  23.6 0.0 copy-start
  23.6 0.8 %copy-done = bf16[16,16,896]{2,1,0:T(8,128)(2,1)} copy-done((bf16[16,16,896]{2,1,0:T(8,128)(2,1)}, bf16[16,16,896]{2,1,0:T(8,128)(2,1)S(1)}, u32[]{:S(2)}) %copy-start) | copy-done | bytes 458776
  24.4 5.3 %cols.1 = (bf16[256,512]{1,0:T(8,128)(2,1)}, bf16[384,384]{1,0:T(8,128)(2,1)}) custom-call(bf16[256,896]{1,0:T(8,128)(2,1)} %bitcast.8, bf16[384,384]{1,0:T(8,128)(2,1)} %weight_ref.3, f32[384,384]{1,0:T(8,128)} %get-tuple-element.17.part_ref, f32[16,128]{1,0:T(8,128)} %get-tuple-element.18.skip_ref), custom_call_target="tpu_custom_call" | custom-call | flops 226492416 | bytes 786432 | tf_op jit(solution)/shard_map/cols/pallas_call | solution.py:349
  29.7 14.7 %all_to_all.41 = bf16[16,24,384]{2,1,0:T(8,128)(2,1)} all-to-all(bf16[16,24,384]{2,1,0:T(8,128)(2,1)} %bitcast.12), channel_id=1, replica_groups=mesh['grp'=2,'row'=16] {'row'}, dimensions={0} | all-to-all | bytes 589824 | tf_op jit(solution)/shard_map/all_to_all | solution.py:371
  44.4 3.5 %all-to-all-start.1 = ((bf16[16,16,512]{2,1,0:T(8,128)(2,1)}), bf16[16,16,512]{2,1,0:T(8,128)(2,1)S(1)}, u32[]{:S(2)}, u32[]{:S(2)}) async-start(bf16[16,16,512]{2,1,0:T(8,128)(2,1)} %bitcast.2), calls=%async_computation.1 | async-start | bytes 524288 | tf_op jit(solution)/shard_map/all_to_all | solution.py:371
  47.9 1.6 %sum.1 = bf16[24,384]{1,0:T(8,128)(2,1)} custom-call(bf16[384,384]{1,0:T(8,128)(2,1)} %bitcast.10), custom_call_target="tpu_custom_call" | custom-call | flops 147456 | bytes 294912 | tf_op jit(solution)/shard_map/sum/pallas_call | solution.py:349
  49.6 8.4 %all-to-all-done.1 = bf16[16,16,512]{2,1,0:T(8,128)(2,1)S(1)} async-done(((bf16[16,16,512]{2,1,0:T(8,128)(2,1)}), bf16[16,16,512]{2,1,0:T(8,128)(2,1)S(1)}, u32[]{:S(2)}, u32[]{:S(2)}) %all-to-all-start.1) | async-done | bytes 262176 | tf_op jit(solution)/shard_map/all_to_all | solution.py:371
  57.9 0.0 copy-start.2
  57.9 1.5 %tile.2 = bf16[16,24,384]{2,1,0:T(8,128)(2,1)} broadcast(bf16[24,384]{1,0:T(8,128)(2,1)} %sum.1), dimensions={1,2} | broadcast | bytes 313344 | tf_op jit(solution)/shard_map/tile | solution.py:411
  59.4 0.0 copy-done.2
  59.4 3.5 %all-to-all-start.3 = ((bf16[16,24,384]{2,1,0:T(8,128)(2,1)}), bf16[16,24,384]{2,1,0:T(8,128)(2,1)S(1)}, u32[]{:S(2)}, u32[]{:S(2)}) async-start(bf16[16,24,384]{2,1,0:T(8,128)(2,1)} %tile.2), calls=%async_computation.3 | async-start | bytes 589824 | tf_op jit(solution)/shard_map/all_to_all | solution.py:371
  62.9 2.2 %finish.1 = (bf16[2,128,384]{2,1,0:T(8,128)(2,1)}, f32[4,6,2,128]{3,2,1,0:T(2,128)}, f32[4,16,2,128]{3,2,1,0:T(2,128)}, f32[4,16,2,128]{3,2,1,0:T(2,128)}, f32[1,384]{1,0:T(1,128)}) custom-call(bf16[256,512]{1,0:T(8,128)(2,1)} %bitcast.11, f32[256,384]{1,0:T(8,128)} %get-tuple-element.20.gx_ref, f32[128,256]{1,0:T(8,128)} %get-tuple-element.21.small_ref), custom_call_target="tpu_custom_call" | custom-call | flops 50331648 | bytes 786432 | tf_op jit(solution)/shard_map/finish/pallas_call | solution.py:349
  65.2 0.0 copy-start.4
  65.2 0.7 copy-done.4
  65.8 0.6 reduce
  66.4 7.0 %all-to-all-done.3 = bf16[16,24,384]{2,1,0:T(8,128)(2,1)S(1)} async-done(((bf16[16,24,384]{2,1,0:T(8,128)(2,1)}), bf16[16,24,384]{2,1,0:T(8,128)(2,1)S(1)}, u32[]{:S(2)}, u32[]{:S(2)}) %all-to-all-start.3) | async-done | bytes 294944 | tf_op jit(solution)/shard_map/all_to_all | solution.py:371
  73.4 0.0 copy-start.1
  73.4 0.7 copy-done.1
  74.1 1.8 %widen.1 = f32[384,384]{1,0:T(8,128)} custom-call(bf16[384,384]{1,0:T(8,128)(2,1)} %bitcast.9), custom_call_target="tpu_custom_call" | custom-call | flops 147456 | bytes 884736 | tf_op jit(solution)/shard_map/widen/pallas_call | solution.py:349
Async XLA Ops:
  2.8 7.6 %copy-start.3 = (f32[384]{0:T(512)S(1)}, f32[384]{0:T(512)}, u32[]{:S(2)}) copy-start(f32[384]{0:T(512)} %param.11) | copy-start | bytes 4612
  2.8 20.8 %all-to-all-start = ((bf16[16,16,896]{2,1,0:T(8,128)(2,1)}), bf16[16,16,896]{2,1,0:T(8,128)(2,1)S(1)}, u32[]{:S(2)}, u32[]{:S(2)}) async-start(bf16[16,16,896]{2,1,0:T(8,128)(2,1)} %bitcast.7), calls=%async_computation | async-start | bytes 917504 | tf_op jit(solution)/shard_map/all_to_all | solution.py:371
  23.6 0.8 %copy-start = (bf16[16,16,896]{2,1,0:T(8,128)(2,1)}, bf16[16,16,896]{2,1,0:T(8,128)(2,1)S(1)}, u32[]{:S(2)}) copy-start(bf16[16,16,896]{2,1,0:T(8,128)(2,1)S(1)} %all-to-all-done) | copy-start | bytes 1376260
  44.4 13.5 %all-to-all-start.1 = ((bf16[16,16,512]{2,1,0:T(8,128)(2,1)}), bf16[16,16,512]{2,1,0:T(8,128)(2,1)S(1)}, u32[]{:S(2)}, u32[]{:S(2)}) async-start(bf16[16,16,512]{2,1,0:T(8,128)(2,1)} %bitcast.2), calls=%async_computation.1 | async-start | bytes 524288 | tf_op jit(solution)/shard_map/all_to_all | solution.py:371
  57.9 1.5 %copy-start.2 = (bf16[16,16,512]{2,1,0:T(8,128)(2,1)}, bf16[16,16,512]{2,1,0:T(8,128)(2,1)S(1)}, u32[]{:S(2)}) copy-start(bf16[16,16,512]{2,1,0:T(8,128)(2,1)S(1)} %all-to-all-done.1) | copy-start | bytes 786436
  59.4 14.1 %all-to-all-start.3 = ((bf16[16,24,384]{2,1,0:T(8,128)(2,1)}), bf16[16,24,384]{2,1,0:T(8,128)(2,1)S(1)}, u32[]{:S(2)}, u32[]{:S(2)}) async-start(bf16[16,24,384]{2,1,0:T(8,128)(2,1)} %tile.2), calls=%async_computation.3 | async-start | bytes 589824 | tf_op jit(solution)/shard_map/all_to_all | solution.py:371
  65.2 0.7 copy-start.4
  73.4 0.7 copy-start.1
where the time goes:
time: 76.7 us; the launch traced here: 76 us
  waiting for transfers between devices  22.9 us (30%)
  Pallas kernels  18.2 us (24%)
  blocking collectives  14.7 us (19%)
  starting transfers between devices  14.6 us (19%)
  local copies, waits for them, and re-layouts  4.19 us (5%)
    all_to_all x3, waiting for transfers between devices, exchange(): return lax.all_to_all(array, 'row', split_axis=0, concat_axis=0, tiled=True)  22.9 us
    pallas_call x6, Pallas kernels, call(): pl.pallas_call(kernel, name=name, out_shape=out_shape, scratch_shapes=lis...  18.2 us
    all_to_all x1, blocking collectives, exchange(): return lax.all_to_all(array, 'row', split_axis=0, concat_axis=0, tiled=True)  14.7 us
    all_to_all x3, starting transfers between devices, exchange(): return lax.all_to_all(array, 'row', split_axis=0, concat_axis=0, tiled=True)  14.6 us
    unnamed x10, local copies, waits for them, and re-layouts  2.16 us
  transfers between devices with their start and end apart: 3, of which 3 were waited for; matrix products, arithmetic and copies ran while one was open for 2% of the time, Pallas kernels for 12%

commit v1 on v0

v1 whole, which is shorter than its diff:
```python
import functools

import jax
import jax.numpy as jnp
from jax import lax
from jax.experimental import pallas as pl
from jax.experimental.pallas import tpu as pltpu
from jax.sharding import PartitionSpec as P

F32 = jnp.float32
BF16 = jnp.bfloat16
HI = lax.Precision.HIGHEST
LANES = 128
FAR = -1e30
VMEM_GRANT = 16 << 20


def iota(shape, dim):
    return lax.broadcasted_iota(jnp.int32, shape, dim)


def nt(a, b):
    return lax.dot_general(a, b, (((1,), (1,)), ((), ())), preferred_element_type=F32)


def nn(a, b):
    return jnp.dot(a, b, preferred_element_type=F32)


def tn(a, b):
    return lax.dot_general(a, b, (((0,), (0,)), ((), ())), preferred_element_type=F32)


def split_index(index, sizes):
    parts = []
    for size in reversed(sizes):
        if size & (size - 1) == 0:
            parts.append(index & (size - 1))
            index = index >> (size.bit_length() - 1)
        else:
            parts.append(lax.rem(index, size))
            index = lax.div(index, size)
    return parts[::-1]


def one_hot_rows(count, source_of):
    wanted = source_of(iota((count, 1), 0))
    return (wanted == iota((count, count), 1)).astype(F32).astype(BF16)


class Slots:
    def __init__(self, heads, states):
        self.heads = heads
        self.states = states
        self.inputs = (0, states)
        self.reads = (2 * states, 3 * states)
        pad = -(-heads // 8) * 8
        self.pad = pad
        self.rates = (4 * states, 4 * states + pad)
        self.lows = (4 * states + 2 * pad, 4 * states + 3 * pad)
        self.used = 4 * states + 2 * pad


class Lines:
    def __init__(self, rows, rates, slots, line, block):
        at_t, at_u = iota((block, block), 0), iota((block, block), 1)
        self.below, self.above = at_t > at_u, at_t < at_u
        self.same = None
        if line < block:
            line_t = split_index(at_t, (block // line, line))[0]
            line_u = split_index(at_u, (block // line, line))[0]
            self.same = line_t == line_u
        self.till = self.within(at_t <= at_u)
        self.since = self.within(at_t >= at_u)
        self.sums = (
            -jnp.dot(rates[0], self.till.astype(F32), precision=HI, preferred_element_type=F32),
            -jnp.dot(rates[1], self.since.astype(F32), precision=HI, preferred_element_type=F32),
        )
        self.columns = jnp.transpose(jnp.concatenate(self.sums, axis=0))
        self.inputs = [rows[at : at + slots.states].astype(BF16) for at in slots.inputs]
        self.reads = [rows[at : at + slots.states].astype(BF16) for at in slots.reads]
        down, up = (tn(self.reads[way], self.inputs[way]) for way in (0, 1))
        self.scores = jnp.where(self.below, down, jnp.where(self.above, up, down + up))
        self.pad = slots.pad

    def within(self, mask):
        return mask if self.same is None else mask & self.same

    def kernel(self, head):
        up = self.pad + head
        spread = jnp.where(
            self.below,
            self.columns[:, head : head + 1] - self.sums[0][head : head + 1],
            self.columns[:, up : up + 1] - self.sums[1][head : head + 1],
        )
        if self.same is not None:
            spread = jnp.where(self.same, spread, FAR)
        return jnp.exp(spread)


def head_mask(block, head_size, member):
    lane = iota((block, LANES), 1)
    return (lane >= member * head_size) & (lane < (member + 1) * head_size)


def scan_block(feats, grads, lines, slots, small_ref, row_slice, forward, backward):
    block = feats.shape[0]
    heads = slots.heads
    head_size = feats.shape[1] // heads
    per_group = LANES // head_size
    below = lines.below
    grad_scores = jnp.zeros((block, block), F32)
    out_parts, grad_parts = [], []
    lane_pad = iota((block, LANES), 1)
    row_sums = jnp.zeros((block, LANES), F32)
    row_at = iota((2 * slots.pad, block), 0)
    col_sums = jnp.zeros((2 * slots.pad, block), F32)
    for group in range(heads // per_group):
        span = slice(group * LANES, (group + 1) * LANES)
        feat_group = feats[:, span]
        grad_group = grads[:, span] if backward else None
        mixes, feat_own, grad_own = [], [], []
        for member in range(per_group):
            head = group * per_group + member
            up = slots.pad + head
            mine = head_mask(block, head_size, member)
            feat_head = jnp.where(mine, feat_group, jnp.zeros_like(feat_group))
            kernel = lines.kernel(head)
            mix = kernel * lines.scores
            mixes.append(mix.astype(BF16))
            feat_own.append(feat_head)
            if not backward:
                continue
            grad_own.append(jnp.where(mine, grad_group, jnp.zeros_like(grad_group)))
            grad_mix = nt(grad_group, feat_head)
            grad_scores = grad_scores + kernel * grad_mix
            flow = mix * grad_mix
            flow_down = jnp.where(below, flow, 0.0)
            row_down = jnp.sum(flow_down, axis=1, keepdims=True)
            row_all = jnp.sum(flow, axis=1, keepdims=True)
            col_down = jnp.sum(flow_down, axis=0, keepdims=True)
            col_all = jnp.sum(flow, axis=0, keepdims=True)
            row_sums = jnp.where(lane_pad == head, row_down, row_sums)
            row_sums = jnp.where(lane_pad == up, row_all - row_down, row_sums)
            col_sums = jnp.where(row_at == head, col_down, col_sums)
            col_sums = jnp.where(row_at == up, col_all - col_down, col_sums)
        if forward:
            out_parts.append(
                nn(jnp.concatenate(mixes, axis=1), jnp.concatenate(feat_own, axis=0))
            )
        if backward:
            grad_parts.append(
                tn(jnp.concatenate(mixes, axis=0), jnp.concatenate(grad_own, axis=0))
            )
    out = jnp.concatenate(out_parts, axis=1) if forward else None
    if not backward:
        return out, None
    change = col_sums - jnp.transpose(row_sums)[: 2 * slots.pad]
    reach = (lines.since, lines.till)
    for way in (0, 1):
        score_grad = jnp.where(reach[way], grad_scores, 0.0).astype(BF16)
        at = slots.inputs[way]
        small_ref[at : at + slots.states, row_slice] = nn(lines.reads[way], score_grad)
        at = slots.reads[way]
        small_ref[at : at + slots.states, row_slice] = nt(lines.inputs[way], score_grad)
        at = slots.rates[way]
        part = change[way * slots.pad : (way + 1) * slots.pad]
        small_ref[at : at + slots.pad, row_slice] = jnp.dot(
            part, reach[way].astype(F32), precision=HI, preferred_element_type=F32
        )
    return out, jnp.concatenate(grad_parts, axis=1)


def pack_kernel(slots, ranks, feat_ref, cot_ref, rate_ref, input_ref, read_ref, out_ref, rows_ref):
    tile_rows, columns, width = feat_ref.shape
    model = cot_ref.shape[2]
    tokens = tile_rows * columns
    narrow = columns // ranks

    def source(at):
        rank, row, column = split_index(at, (ranks, tile_rows, narrow))
        return row * columns + rank * narrow + column

    order = one_hot_rows(tokens, source)
    out_ref[:, :width] = nn(order, feat_ref[...].reshape(tokens, width)).astype(BF16)
    out_ref[:, width : width + model] = nn(order, cot_ref[...].reshape(tokens, model)).astype(BF16)
    rows_ref[...] = jnp.zeros_like(rows_ref)
    for way in (0, 1):
        for row in range(tile_rows):
            span = slice(row * columns, (row + 1) * columns)
            at = slots.inputs[way]
            rows_ref[at : at + slots.states, span] = input_ref[2 + way, :, row, :]
            at = slots.reads[way]
            rows_ref[at : at + slots.states, span] = read_ref[2 + way, :, row, :]
            at = slots.rates[way]
            rate = rate_ref[2 + way, :, row, :]
            rows_ref[at : at + slots.heads, span] = rate
            at = slots.lows[way]
            rows_ref[at : at + slots.heads, span] = rate - rate.astype(BF16).astype(F32)
    out_ref[:, width + model :] = nt(order, rows_ref[...].astype(BF16)).astype(BF16)


def rows_kernel(
    slots, chunk, feat_ref, cot_ref, weight_ref, skip_ref, rate_ref, input_ref, read_ref,
    gx_ref, small_ref, part_ref, skip_out_ref, rows_ref,
):
    tile_rows, columns, width = feat_ref.shape
    tokens = tile_rows * columns
    skip = skip_ref[...]
    rows_ref[...] = jnp.zeros_like(rows_ref)
    partial = jnp.zeros(part_ref.shape, F32)
    skip_part = jnp.zeros((1, width), F32)
    for row in range(tile_rows):
        feats, cots = feat_ref[row], cot_ref[row]
        grads = nt(cots, weight_ref[...]).astype(BF16)
        for way in (0, 1):
            at = slots.inputs[way]
            rows_ref[at : at + slots.states, :] = input_ref[way, :, row, :]
            at = slots.reads[way]
            rows_ref[at : at + slots.states, :] = read_ref[way, :, row, :]
            at = slots.rates[way]
            rows_ref[at : at + slots.heads, :] = rate_ref[way, :, row, :]
        rates = [rows_ref[at : at + slots.pad, :] for at in slots.rates]
        lines = Lines(rows_ref, rates, slots, columns, columns)
        outs, gx = scan_block(
            feats, grads, lines, slots, small_ref,
            slice(row * columns, (row + 1) * columns), True, True,
        )
        feat_f32, grad_f32 = feats.astype(F32), grads.astype(F32)
        across = (outs + skip * feat_f32).astype(BF16)
        partial = partial + tn(across, cots)
        gx_ref[row * columns : (row + 1) * columns, :] = gx + skip * grad_f32
        skip_part = skip_part + jnp.sum(feat_f32 * grad_f32, axis=0, keepdims=True)
    part_ref[...] = partial
    if chunk is None:
        skip_out_ref[...] = skip_part
    else:
        high = skip_part.astype(BF16).astype(F32)
        piece = width // chunk
        lane_of = iota((chunk, width), 1)
        start = iota((chunk, width), 0) * piece
        owned = (lane_of >= start) & (lane_of < start + piece)
        spread = jnp.concatenate(
            [jnp.where(owned, high, 0.0), jnp.where(owned, skip_part - high, 0.0)], axis=1
        ).astype(BF16)
        skip_out_ref[...] = nn(spread, skip_places(slots, width, piece))


def skip_places(slots, width, piece):
    place = lax.rem(iota((width, 1), 0), piece) + slots.used
    lane = iota((width, LANES), 1)
    high, low = place == lane, place + piece == lane
    return jnp.concatenate([high.astype(F32), low.astype(F32)], axis=0).astype(BF16)


class Columns:
    def __init__(self, slots, ranks, tile_rows, width, model, recv_ref):
        tokens = recv_ref.shape[0]
        self.line = ranks * tile_rows
        narrow = tokens // self.line
        self.block = max(self.line, min(LANES, tokens))
        self.slots = slots

        def source(at):
            column, rank, row = split_index(at, (narrow, ranks, tile_rows))
            return rank * (tile_rows * narrow) + row * narrow + column

        def source_back(at):
            rank, row, column = split_index(at, (ranks, tile_rows, narrow))
            return column * self.line + rank * tile_rows + row

        order = one_hot_rows(tokens, source)
        self.source_back = source_back
        self.feats = nn(order, recv_ref[:, :width]).astype(BF16)
        self.cots = nn(order, recv_ref[:, width : width + model]).astype(BF16)
        self.params = nn(order, recv_ref[:, width + model :])
        self.spans = [slice(at, at + self.block) for at in range(0, tokens, self.block)]

    def lines(self, span):
        slots = self.slots
        rows = jnp.transpose(self.params[span])
        rates = [
            rows[hi : hi + slots.pad] + rows[lo : lo + slots.pad]
            for hi, lo in zip(slots.rates, slots.lows)
        ]
        return Lines(rows, rates, slots, self.line, self.block)


def forward_kernel(slots, ranks, tile_rows, recv_ref, part_ref, sum_ref):
    width, model = part_ref.shape
    cols = Columns(slots, ranks, tile_rows, width, model, recv_ref)
    outs = [
        scan_block(cols.feats[span], None, cols.lines(span), slots, None, None, True, False)[0]
        for span in cols.spans
    ]
    down = jnp.concatenate(outs, axis=0).astype(BF16)
    sum_ref[...] = (part_ref[...] + tn(down, cols.cots)).astype(BF16)


def backward_kernel(
    slots, ranks, tile_rows, chunk, recv_ref, weight_ref, skip_ref, back_ref, small_ref
):
    width, model = weight_ref.shape
    cols = Columns(slots, ranks, tile_rows, width, model, recv_ref)
    grads = nt(cols.cots, weight_ref[...]).astype(BF16)
    small_ref[...] = jnp.zeros_like(small_ref)
    gxs = [
        scan_block(
            cols.feats[span], grads[span], cols.lines(span), slots, small_ref, span, False, True
        )[1].astype(BF16)
        for span in cols.spans
    ]
    order_back = one_hot_rows(recv_ref.shape[0], cols.source_back)
    back_ref[:, :width] = nn(order_back, jnp.concatenate(gxs, axis=0)).astype(BF16)
    smalls = nt(order_back, small_ref[...].astype(BF16))
    if chunk is not None:
        smalls = smalls + jnp.concatenate([skip_ref[...]] * ranks, axis=0)
    back_ref[:, width:] = smalls.astype(BF16)


def strip(array):
    return [array[:, at : at + LANES] for at in range(0, array.shape[1], LANES)]


def sum_kernel(ranks, parts_ref, back_ref, out_ref):
    rows = parts_ref.shape[0] // ranks
    total = parts_ref[:rows, :].astype(F32)
    for rank in range(1, ranks):
        total = total + parts_ref[rank * rows : (rank + 1) * rows, :].astype(F32)
    own = total.astype(BF16)
    tokens = back_ref.shape[0] // ranks
    for rank in range(ranks):
        at = 0
        pieces = strip(back_ref[rank * tokens : (rank + 1) * tokens, :]) + strip(own)
        for piece in pieces:
            out_ref[rank, at : at + piece.shape[0], :] = piece
            at += piece.shape[0]


def finish_kernel(
    slots, ranks, chunk, recv_ref, gx_ref, small_ref,
    feat_out, rate_out, input_out, read_out, weight_out, *skip_out,
):
    tile_rows, columns, width = feat_out.shape
    tokens = tile_rows * columns
    narrow = columns // ranks
    group = tokens // ranks
    model = weight_out.shape[1]
    rows = weight_out.shape[0] // ranks
    backs = width // LANES + 1

    for rank in range(ranks):
        at = backs * group
        for lane in range(0, model, LANES):
            weight_out[rank * rows : (rank + 1) * rows, lane : lane + LANES] = recv_ref[
                rank, at : at + rows, :
            ].astype(F32)
            at += rows

    def source(at):
        row, rank, column = split_index(at, (tile_rows, ranks, narrow))
        return rank * group + row * narrow + column

    order = one_hot_rows(tokens, source)
    back = [
        jnp.concatenate(
            [recv_ref[rank, part * group : (part + 1) * group, :] for rank in range(ranks)], axis=0
        )
        for part in range(backs)
    ]
    for part in range(backs - 1):
        lane = slice(part * LANES, (part + 1) * LANES)
        total = gx_ref[:, lane] + nn(order, back[part])
        feat_out[:, :, lane] = total.astype(BF16).reshape(tile_rows, columns, LANES)
    smalls = nn(order, back[-1])
    for row in range(tile_rows):
        span = slice(row * columns, (row + 1) * columns)
        held = jnp.transpose(smalls[span])
        for way in (0, 1):
            at = slots.inputs[way]
            input_out[way, :, row, :] = small_ref[at : at + slots.states, span]
            input_out[2 + way, :, row, :] = held[at : at + slots.states]
            at = slots.reads[way]
            read_out[way, :, row, :] = small_ref[at : at + slots.states, span]
            read_out[2 + way, :, row, :] = held[at : at + slots.states]
            at = slots.rates[way]
            rate_out[way, :, row, :] = small_ref[at : at + slots.heads, span]
            rate_out[2 + way, :, row, :] = held[at : at + slots.heads]
    if chunk is not None:
        piece = width // chunk
        gathered = back[-1][:chunk].astype(F32)
        for rank in range(1, ranks):
            gathered = gathered + back[-1][rank * chunk : (rank + 1) * chunk].astype(F32)
        places = skip_places(slots, width, piece).astype(F32)
        places = places[:width] + places[width:]
        spread = lax.dot_general(
            gathered, places, (((1,), (1,)), ((), ())), precision=HI, preferred_element_type=F32
        )
        lane_of = iota((chunk, width), 1)
        start = iota((chunk, width), 0) * piece
        owned = (lane_of >= start) & (lane_of < start + piece)
        skip_out[0][...] = jnp.sum(jnp.where(owned, spread, 0.0), axis=0)


def call(kernel, name, out_shape, operands, scratch=(), flops=0, moved=0, grant=VMEM_GRANT):
    return pl.pallas_call(
        kernel,
        name=name,
        out_shape=out_shape,
        in_specs=[pl.BlockSpec(memory_space=pltpu.VMEM)] * len(operands),
        out_specs=jax.tree.map(lambda leaf: pl.BlockSpec(memory_space=pltpu.VMEM), out_shape),
        scratch_shapes=list(scratch),
        compiler_params=pltpu.CompilerParams(vmem_limit_bytes=grant),
        cost_estimate=pl.CostEstimate(flops=flops, bytes_accessed=moved, transcendentals=0),
    )(*operands)


def local(ranks, features, decay_rate, input_proj, read_proj, skip_gain, out_weight, out_cotangent):
    tile_rows, columns, width = features.shape
    model = out_cotangent.shape[2]
    heads, states = decay_rate.shape[1], input_proj.shape[1]
    slots = Slots(heads, states)
    tokens = tile_rows * columns
    chunk = tokens // ranks
    room = chunk * (LANES - slots.used)
    if chunk % 8 or width % chunk or 2 * width > room:
        chunk = None
    shape = jax.ShapeDtypeStruct

    def exchange(array):
        return lax.all_to_all(array, "row", split_axis=0, concat_axis=0, tiled=True)

    packed = call(
        functools.partial(pack_kernel, slots, ranks), "pack",
        shape((tokens, width + model + LANES), BF16),
        (features, out_cotangent, decay_rate, input_proj, read_proj),
        [pltpu.VMEM((LANES, tokens), F32)],
        flops=2 * tokens * tokens * (width + model), moved=4 * tokens * (width + model), grant=None,
    )
    received = exchange(packed)
    skip_shape = (1, width) if chunk is None else (chunk, LANES)
    gx_rows, small_rows, partial, skip_part = call(
        functools.partial(rows_kernel, slots, chunk), "rows",
        (
            shape((tokens, width), F32),
            shape((LANES, tokens), F32),
            shape((width, model), F32),
            shape(skip_shape, F32),
        ),
        (
            features, out_cotangent, out_weight, skip_gain.reshape(1, width),
            decay_rate, input_proj, read_proj,
        ),
        [pltpu.VMEM((LANES, columns), F32)],
        flops=2 * tokens * width * (2 * model + 3 * columns), moved=8 * tokens * width,
    )
    weight_sum = call(
        functools.partial(forward_kernel, slots, ranks, tile_rows), "forward",
        shape((width, model), BF16), (received, partial),
        flops=2 * tokens * width * (2 * model + columns), moved=8 * tokens * width,
    )
    weight_parts = exchange(weight_sum)
    back = call(
        functools.partial(backward_kernel, slots, ranks, tile_rows, chunk), "backward",
        shape((tokens, width + LANES), BF16), (received, out_weight, skip_part),
        [pltpu.VMEM((LANES, tokens), F32)],
        flops=2 * tokens * width * (2 * model + 3 * columns), moved=8 * tokens * width,
    )
    group = tokens // ranks
    chunk_rows = (width // LANES + 1) * group + (model // LANES) * (width // ranks)
    last = call(
        functools.partial(sum_kernel, ranks), "sum",
        shape((ranks, chunk_rows, LANES), BF16), (weight_parts, back),
        flops=width * model, moved=2 * width * model,
    )
    returned = exchange(last)
    outs = [
        shape(features.shape, BF16),
        shape(decay_rate.shape, F32),
        shape(input_proj.shape, F32),
        shape(read_proj.shape, F32),
        shape((width, model), F32),
    ]
    if chunk is not None:
        outs.append(shape((width,), F32))
    done = call(
        functools.partial(finish_kernel, slots, ranks, chunk), "finish",
        tuple(outs), (returned, gx_rows, small_rows),
        flops=2 * tokens * tokens * width, moved=8 * tokens * width,
    )
    if chunk is None:
        grad_skip = lax.psum(skip_part, "row").reshape(width)
    else:
        grad_skip = done[5]
    return (*done[:4], grad_skip, done[4])


def solution(mesh):
    in_specs = (
        P(("grp", "row"), None, None),
        P(None, None, ("grp", "row"), None),
        P(None, None, ("grp", "row"), None),
        P(None, None, ("grp", "row"), None),
        P(),
        P(),
        P(("grp", "row"), None, None),
    )
    out_specs = (
        P(("grp", "row"), None, None),
        P(None, None, ("grp", "row"), None),
        P(None, None, ("grp", "row"), None),
        P(None, None, ("grp", "row"), None),
        P("grp"),
        P("grp", None),
    )
    body = functools.partial(local, mesh.shape["row"])
    return jax.shard_map(body, mesh=mesh, in_specs=in_specs, out_specs=out_specs, check_vma=False)
```

time: 76.7 us -> 62.1 us (0.81)
  waiting for transfers between devices: 22.9 us -> 17.3 us
  Pallas kernels: 18.2 us -> 12.8 us
  blocking collectives: 14.7 us -> 19.5 us
  local copies, waits for them, and re-layouts: 4.19 us -> 0.04 us
  starting transfers between devices: 14.6 us -> 11.4 us
    all_to_all x3 -> x2, waiting for transfers between devices: 22.9 us -> 17.3 us  [exchange(): return lax.all_to_all(array, 'row', split_axis=0, concat_axis=0, tiled=True)]
    pallas_call x6, Pallas kernels: 18.2 us -> 12.8 us  [call(): pl.pallas_call(kernel, name=name, out_shape=out_shape, in_specs=[pl.Block...]
    all_to_all x1, blocking collectives: 14.7 us -> 19.5 us  [exchange(): return lax.all_to_all(array, 'row', split_axis=0, concat_axis=0, tiled=True)]
    all_to_all x3 -> x2, starting transfers between devices: 14.6 us -> 11.4 us  [exchange(): return lax.all_to_all(array, 'row', split_axis=0, concat_axis=0, tiled=True)]
    unnamed x10 -> x14, local copies, waits for them, and re-layouts: 2.16 us -> 0.03 us
    another operation x1 -> x0, local copies, waits for them, and re-layouts: 1.46 us -> none  [local(): gathered = exchange(jnp.tile(own, (ranks, 1)))]
  transfers between devices with their start and end apart: 3 -> 2, of which waited for: 3 -> 2; matrix products, arithmetic and copies ran while one was open for 2% -> 0% of each run, Pallas kernels for 12% -> 10%
where the time goes in v1:
time: 62.1 us; the launch traced here: 61.8 us
  blocking collectives  19.5 us (31%)
  waiting for transfers between devices  17.3 us (28%)
  Pallas kernels  12.8 us (21%)
  starting transfers between devices  11.4 us (18%)
  between operations  0.75 us (1%)
    all_to_all x1, blocking collectives, exchange(): return lax.all_to_all(array, 'row', split_axis=0, concat_axis=0, tiled=True)  19.5 us
    all_to_all x2, waiting for transfers between devices, exchange(): return lax.all_to_all(array, 'row', split_axis=0, concat_axis=0, tiled=True)  17.3 us
    pallas_call x6, Pallas kernels, call(): pl.pallas_call(kernel, name=name, out_shape=out_shape, in_specs=[pl.Block...  12.8 us
    all_to_all x2, starting transfers between devices, exchange(): return lax.all_to_all(array, 'row', split_axis=0, concat_axis=0, tiled=True)  11.4 us
  transfers between devices with their start and end apart: 2, of which 2 were waited for; matrix products, arithmetic and copies ran while one was open for 0% of the time, Pallas kernels for 10%

profile of v1, /device:TPU:0, one launch (start us, length us, event | category | flops | bytes accessed | tf_op | source)
XLA Modules:
  0.0 61.8 jit_solution(4553881045265872321)
XLA Ops:
  0.6 2.2 %pack.1 = bf16[256,896]{1,0:T(8,128)(2,1)} custom-call(bf16[2,128,384]{2,1,0:T(8,128)(2,1)} %feat_ref.3, bf16[2,128,384]{2,1,0:T(8,128)(2,1)} %cot_ref.3, f32[4,6,2,128]{3,2,1,0:T(2,128)} %rate_ref.3, f32[4,16,2,128]{3,2,1,0:T(2,128)} %input_ref.3, f32[4,16,2,128]{3,2,1,0:T(2,128)} %read_ref.3), custom_call_target="tpu_custom_call" | custom-call | flops 100663296 | bytes 786432 | tf_op jit(solution)/shard_map/pack/pallas_call | solution.py:406
  2.8 0.0 copy-start.6
  2.8 0.0 copy-start
  2.8 0.0 copy-start.1
  2.8 0.0 copy-start.2
  2.9 0.0 copy-start.3
  2.9 0.0 copy-start.4
  2.9 0.0 copy-start.5
  2.9 7.6 %all-to-all-start = ((bf16[16,16,896]{2,1,0:T(8,128)(2,1)}), bf16[16,16,896]{2,1,0:T(8,128)(2,1)S(1)}, u32[]{:S(2)}, u32[]{:S(2)}) async-start(bf16[16,16,896]{2,1,0:T(8,128)(2,1)} %bitcast.7), calls=%async_computation | async-start | bytes 917504 | tf_op jit(solution)/shard_map/all_to_all | solution.py:431
  10.5 0.0 copy-done.6
  10.5 0.0 copy-done
  10.5 0.0 copy-done.1
  10.5 0.0 copy-done.2
  10.5 0.0 copy-done.3
  10.5 0.0 copy-done.4
  10.5 0.0 copy-done.5
  10.5 3.0 %rows.1 = (f32[256,384]{1,0:T(8,128)S(1)}, f32[128,256]{1,0:T(8,128)S(1)}, f32[384,384]{1,0:T(8,128)S(1)}, f32[16,128]{1,0:T(8,128)S(1)}) custom-call(bf16[2,128,384]{2,1,0:T(8,128)(2,1)S(1)} %copy-done.1, bf16[2,128,384]{2,1,0:T(8,128)(2,1)S(1)} %copy-done.2, bf16[384,384]{1,0:T(8,128)(2,1)S(1)} %copy-done, f32[1,384]{1,0:T(1,128)S(1)} %reshape.19.skip_ref, ...), custom_call_target="tpu_custom_call" | custom-call | flops 226492416 | bytes 786432 | tf_op jit(solution)/shard_map/rows/pallas_call | solution.py:406
  13.6 10.1 %all-to-all-done = bf16[16,16,896]{2,1,0:T(8,128)(2,1)S(1)} async-done(((bf16[16,16,896]{2,1,0:T(8,128)(2,1)}), bf16[16,16,896]{2,1,0:T(8,128)(2,1)S(1)}, u32[]{:S(2)}, u32[]{:S(2)}) %all-to-all-start) | async-done | bytes 458784 | tf_op jit(solution)/shard_map/all_to_all | solution.py:431
  23.7 2.8 %forward.1 = bf16[384,384]{1,0:T(8,128)(2,1)} custom-call(bf16[256,896]{1,0:T(8,128)(2,1)S(1)} %bitcast.4, f32[384,384]{1,0:T(8,128)S(1)} %get-tuple-element.16.part_ref), custom_call_target="tpu_custom_call" | custom-call | flops 176160768 | bytes 786432 | tf_op jit(solution)/shard_map/forward/pallas_call | solution.py:406
  26.5 3.8 %all-to-all-start.1 = ((bf16[16,24,384]{2,1,0:T(8,128)(2,1)}), bf16[16,24,384]{2,1,0:T(8,128)(2,1)S(1)}, u32[]{:S(2)}, u32[]{:S(2)}) async-start(bf16[16,24,384]{2,1,0:T(8,128)(2,1)} %bitcast.2), calls=%async_computation.1 | async-start | bytes 589824 | tf_op jit(solution)/shard_map/all_to_all | solution.py:431
  30.3 3.3 %backward.1.back_ref = bf16[256,512]{1,0:T(8,128)(2,1)S(1)} custom-call(bf16[256,896]{1,0:T(8,128)(2,1)S(1)} %bitcast.5, bf16[384,384]{1,0:T(8,128)(2,1)S(1)} %copy-done, f32[16,128]{1,0:T(8,128)S(1)} %get-tuple-element.17.skip_ref), custom_call_target="tpu_custom_call" | custom-call | flops 226492416 | bytes 786432 | tf_op jit(solution)/shard_map/backward/pallas_call | solution.py:406
  33.6 7.3 %all-to-all-done.1 = bf16[16,24,384]{2,1,0:T(8,128)(2,1)S(1)} async-done(((bf16[16,24,384]{2,1,0:T(8,128)(2,1)}), bf16[16,24,384]{2,1,0:T(8,128)(2,1)S(1)}, u32[]{:S(2)}, u32[]{:S(2)}) %all-to-all-start.1) | async-done | bytes 294944 | tf_op jit(solution)/shard_map/all_to_all | solution.py:431
  40.8 0.1 sum.1
  40.9 19.5 %all_to_all.27.recv_ref = bf16[16,136,128]{2,1,0:T(8,128)(2,1)S(1)} all-to-all(bf16[16,136,128]{2,1,0:T(8,128)(2,1)S(1)} %sum.1), channel_id=1, replica_groups=mesh['grp'=2,'row'=16] {'row'}, dimensions={0} | all-to-all | bytes 1114112 | tf_op jit(solution)/shard_map/all_to_all | solution.py:431
  60.4 1.4 %finish.1 = (bf16[2,128,384]{2,1,0:T(8,128)(2,1)}, f32[4,6,2,128]{3,2,1,0:T(2,128)}, f32[4,16,2,128]{3,2,1,0:T(2,128)}, f32[4,16,2,128]{3,2,1,0:T(2,128)}, f32[384,384]{1,0:T(8,128)}, /*index=5*/f32[384]{0:T(512)}) custom-call(bf16[16,136,128]{2,1,0:T(8,128)(2,1)S(1)} %all_to_all.27.recv_ref, f32[256,384]{1,0:T(8,128)S(1)} %get-tuple-element.18.gx_ref, ...), custom_call_target="tpu_custom_call" | custom-call | flops 50331648 | bytes 786432 | tf_op jit(solution)/shard_map/finish/pallas_call | solution.py:406
  (1 shorter events, 0.0 us)
Async XLA Ops:
  2.8 7.6 %copy-start.6 = (f32[384]{0:T(512)S(1)}, f32[384]{0:T(512)}, u32[]{:S(2)}) copy-start(f32[384]{0:T(512)} %param.11) | copy-start | bytes 4612
  2.8 7.6 %copy-start = (bf16[384,384]{1,0:T(8,128)(2,1)S(1)}, bf16[384,384]{1,0:T(8,128)(2,1)}, u32[]{:S(2)}) copy-start(bf16[384,384]{1,0:T(8,128)(2,1)} %weight_ref.3) | copy-start | bytes 884740
  2.8 7.6 %copy-start.1 = (bf16[2,128,384]{2,1,0:T(8,128)(2,1)S(1)}, bf16[2,128,384]{2,1,0:T(8,128)(2,1)}, u32[]{:S(2)}) copy-start(bf16[2,128,384]{2,1,0:T(8,128)(2,1)} %feat_ref.3) | copy-start | bytes 589828
  2.8 7.7 %copy-start.2 = (bf16[2,128,384]{2,1,0:T(8,128)(2,1)S(1)}, bf16[2,128,384]{2,1,0:T(8,128)(2,1)}, u32[]{:S(2)}) copy-start(bf16[2,128,384]{2,1,0:T(8,128)(2,1)} %cot_ref.3) | copy-start | bytes 589828
  2.9 7.7 %copy-start.3 = (f32[4,16,2,128]{3,2,1,0:T(2,128)S(1)}, f32[4,16,2,128]{3,2,1,0:T(2,128)}, u32[]{:S(2)}) copy-start(f32[4,16,2,128]{3,2,1,0:T(2,128)} %input_ref.3) | copy-start | bytes 196612
  2.9 7.7 %copy-start.4 = (f32[4,16,2,128]{3,2,1,0:T(2,128)S(1)}, f32[4,16,2,128]{3,2,1,0:T(2,128)}, u32[]{:S(2)}) copy-start(f32[4,16,2,128]{3,2,1,0:T(2,128)} %read_ref.3) | copy-start | bytes 196612
  2.9 7.7 %copy-start.5 = (f32[4,6,2,128]{3,2,1,0:T(2,128)S(1)}, f32[4,6,2,128]{3,2,1,0:T(2,128)}, u32[]{:S(2)}) copy-start(f32[4,6,2,128]{3,2,1,0:T(2,128)} %rate_ref.3) | copy-start | bytes 73732
  2.9 20.8 %all-to-all-start = ((bf16[16,16,896]{2,1,0:T(8,128)(2,1)}), bf16[16,16,896]{2,1,0:T(8,128)(2,1)S(1)}, u32[]{:S(2)}, u32[]{:S(2)}) async-start(bf16[16,16,896]{2,1,0:T(8,128)(2,1)} %bitcast.7), calls=%async_computation | async-start | bytes 917504 | tf_op jit(solution)/shard_map/all_to_all | solution.py:431
  26.5 14.3 %all-to-all-start.1 = ((bf16[16,24,384]{2,1,0:T(8,128)(2,1)}), bf16[16,24,384]{2,1,0:T(8,128)(2,1)S(1)}, u32[]{:S(2)}, u32[]{:S(2)}) async-start(bf16[16,24,384]{2,1,0:T(8,128)(2,1)} %bitcast.2), calls=%async_computation.1 | async-start | bytes 589824 | tf_op jit(solution)/shard_map/all_to_all | solution.py:431

commit v2 on v1

--- a/solution.py
+++ b/solution.py
@@ -171,19 +171,18 @@
     return out, jnp.concatenate(grad_parts, axis=1)
 
 
+def by_rank(array, ranks):
+    narrow = array[0].shape[0] // ranks
+    return [
+        jnp.concatenate([row[rank * narrow : (rank + 1) * narrow] for row in array], axis=0)
+        for rank in range(ranks)
+    ]
+
+
 def pack_kernel(slots, ranks, feat_ref, cot_ref, rate_ref, input_ref, read_ref, out_ref, rows_ref):
     tile_rows, columns, width = feat_ref.shape
     model = cot_ref.shape[2]
-    tokens = tile_rows * columns
-    narrow = columns // ranks
-
-    def source(at):
-        rank, row, column = split_index(at, (ranks, tile_rows, narrow))
-        return row * columns + rank * narrow + column
-
-    order = one_hot_rows(tokens, source)
-    out_ref[:, :width] = nn(order, feat_ref[...].reshape(tokens, width)).astype(BF16)
-    out_ref[:, width : width + model] = nn(order, cot_ref[...].reshape(tokens, model)).astype(BF16)
+    group = tile_rows * columns // ranks
     rows_ref[...] = jnp.zeros_like(rows_ref)
     for way in (0, 1):
         for row in range(tile_rows):
@@ -197,7 +196,22 @@
             rows_ref[at : at + slots.heads, span] = rate
             at = slots.lows[way]
             rows_ref[at : at + slots.heads, span] = rate - rate.astype(BF16).astype(F32)
-    out_ref[:, width + model :] = nt(order, rows_ref[...].astype(BF16)).astype(BF16)
+    values = [
+        (0, [feat_ref[row].astype(F32) for row in range(tile_rows)]),
+        (width, [cot_ref[row].astype(F32) for row in range(tile_rows)]),
+        (
+            width + model,
+            [
+                jnp.transpose(rows_ref[:, row * columns : (row + 1) * columns])
+                for row in range(tile_rows)
+            ],
+        ),
+    ]
+    for lane, array in values:
+        for rank, piece in enumerate(by_rank(array, ranks)):
+            out_ref[rank * group : (rank + 1) * group, lane : lane + piece.shape[1]] = (
+                piece.astype(BF16)
+            )
 
 
 def rows_kernel(
@@ -322,60 +336,92 @@
     return [array[:, at : at + LANES] for at in range(0, array.shape[1], LANES)]
 
 
+class Halves:
+    def __init__(self, rows, model):
+        self.unit = 8 if rows % 8 == 0 else rows
+        steps = rows // self.unit
+        self.places = [
+            (at * self.unit, lane) for lane in range(0, model, LANES) for at in range(steps)
+        ]
+        self.count = -(-len(self.places) // 2)
+        self.size = self.count * self.unit
+
+    def of(self, index):
+        return divmod(index, self.count)
+
+
 def sum_kernel(ranks, parts_ref, back_ref, out_ref):
-    rows = parts_ref.shape[0] // ranks
+    rows, model = parts_ref.shape[0] // ranks, parts_ref.shape[1]
     total = parts_ref[:rows, :].astype(F32)
     for rank in range(1, ranks):
         total = total + parts_ref[rank * rows : (rank + 1) * rows, :].astype(F32)
-    own = total.astype(BF16)
     tokens = back_ref.shape[0] // ranks
+    halves = Halves(rows, model)
+    unit = halves.unit
+    blocks = [
+        total[at : at + unit, lane : lane + LANES].astype(BF16) for at, lane in halves.places
+    ]
+    blocks += [jnp.zeros_like(blocks[0])] * (2 * halves.count - len(blocks))
     for rank in range(ranks):
         at = 0
-        pieces = strip(back_ref[rank * tokens : (rank + 1) * tokens, :]) + strip(own)
-        for piece in pieces:
-            out_ref[rank, at : at + piece.shape[0], :] = piece
-            at += piece.shape[0]
+        for piece in strip(back_ref[rank * tokens : (rank + 1) * tokens, :]):
+            out_ref[rank, at : at + tokens, :] = piece
+            at += tokens
+        half = rank % 2
+        for piece in blocks[half * halves.count : (half + 1) * halves.count]:
+            out_ref[rank, at : at + unit, :] = piece
+            at += unit
+
+
+def half_kernel(recv_ref, out_ref):
+    size = out_ref.shape[1]
+    out_ref[...] = recv_ref[:, recv_ref.shape[1] - size :, :]
+
+
+def weight_kernel(mine_ref, theirs_ref, out_ref):
+    ranks = mine_ref.shape[0]
+    width, model = out_ref.shape
+    rows = width // ranks
+    halves = Halves(rows, model)
+    unit = halves.unit
+    even = lax.rem(lax.axis_index("row"), 2) == 0
+    mine, theirs = mine_ref[...].astype(F32), theirs_ref[...].astype(F32)
+    pair = (jnp.where(even, mine, theirs), jnp.where(even, theirs, mine))
+    for rank in range(ranks):
+        for index, (at, lane) in enumerate(halves.places):
+            half, step = halves.of(index)
+            out_ref[rank * rows + at : rank * rows + at + unit, lane : lane + LANES] = pair[half][
+                rank, step * unit : (step + 1) * unit, :
+            ]
 
 
 def finish_kernel(
     slots, ranks, chunk, recv_ref, gx_ref, small_ref,
-    feat_out, rate_out, input_out, read_out, weight_out, *skip_out,
+    feat_out, rate_out, input_out, read_out, *skip_out,
 ):
     tile_rows, columns, width = feat_out.shape
-    tokens = tile_rows * columns
     narrow = columns // ranks
-    group = tokens // ranks
-    model = weight_out.shape[1]
-    rows = weight_out.shape[0] // ranks
-    backs = width // LANES + 1
-
-    for rank in range(ranks):
-        at = backs * group
-        for lane in range(0, model, LANES):
-            weight_out[rank * rows : (rank + 1) * rows, lane : lane + LANES] = recv_ref[
-                rank, at : at + rows, :
-            ].astype(F32)
-            at += rows
-
-    def source(at):
-        row, rank, column = split_index(at, (tile_rows, ranks, narrow))
-        return rank * group + row * narrow + column
-
-    order = one_hot_rows(tokens, source)
-    back = [
-        jnp.concatenate(
-            [recv_ref[rank, part * group : (part + 1) * group, :] for rank in range(ranks)], axis=0
+    group = tile_rows * narrow
+    lanes = width // LANES
+
+    def part_of(part):
+        return recv_ref[:, part * group : (part + 1) * group, :].astype(F32)
+
+    def row_of(array, row):
+        return jnp.concatenate(
+            [array[rank, row * narrow : (row + 1) * narrow] for rank in range(ranks)], axis=0
         )
-        for part in range(backs)
-    ]
-    for part in range(backs - 1):
+
+    for part in range(lanes):
         lane = slice(part * LANES, (part + 1) * LANES)
-        total = gx_ref[:, lane] + nn(order, back[part])
-        feat_out[:, :, lane] = total.astype(BF16).reshape(tile_rows, columns, LANES)
-    smalls = nn(order, back[-1])
+        back = part_of(part)
+        for row in range(tile_rows):
+            span = slice(row * columns, (row + 1) * columns)
+            feat_out[row, :, lane] = (gx_ref[span, lane] + row_of(back, row)).astype(BF16)
+    back = part_of(lanes)
     for row in range(tile_rows):
         span = slice(row * columns, (row + 1) * columns)
-        held = jnp.transpose(smalls[span])
+        held = jnp.transpose(row_of(back, row))
         for way in (0, 1):
             at = slots.inputs[way]
             input_out[way, :, row, :] = small_ref[at : at + slots.states, span]
@@ -388,9 +434,7 @@
             rate_out[2 + way, :, row, :] = held[at : at + slots.heads]
     if chunk is not None:
         piece = width // chunk
-        gathered = back[-1][:chunk].astype(F32)
-        for rank in range(1, ranks):
-            gathered = gathered + back[-1][rank * chunk : (rank + 1) * chunk].astype(F32)
+        gathered = jnp.sum(back, axis=0)
         places = skip_places(slots, width, piece).astype(F32)
         places = places[:width] + places[width:]
         spread = lax.dot_general(
@@ -467,19 +511,23 @@
         flops=2 * tokens * width * (2 * model + 3 * columns), moved=8 * tokens * width,
     )
     group = tokens // ranks
-    chunk_rows = (width // LANES + 1) * group + (model // LANES) * (width // ranks)
+    size = Halves(width // ranks, model).size
     last = call(
         functools.partial(sum_kernel, ranks), "sum",
-        shape((ranks, chunk_rows, LANES), BF16), (weight_parts, back),
+        shape((ranks, (width // LANES + 1) * group + size, LANES), BF16), (weight_parts, back),
         flops=width * model, moved=2 * width * model,
     )
     returned = exchange(last)
+    mine = call(
+        half_kernel, "half", shape((ranks, size, LANES), BF16), (returned,),
+        flops=width * model, moved=2 * width * model,
+    )
+    theirs = lax.ppermute(mine, "row", [(rank, rank ^ 1) for rank in range(ranks)])
     outs = [
         shape(features.shape, BF16),
         shape(decay_rate.shape, F32),
         shape(input_proj.shape, F32),
         shape(read_proj.shape, F32),
-        shape((width, model), F32),
     ]
     if chunk is not None:
         outs.append(shape((width,), F32))
@@ -488,11 +536,15 @@
         tuple(outs), (returned, gx_rows, small_rows),
         flops=2 * tokens * tokens * width, moved=8 * tokens * width,
     )
+    grad_weight = call(
+        weight_kernel, "weight", shape((width, model), F32), (mine, theirs),
+        flops=width * model, moved=6 * width * model,
+    )
     if chunk is None:
         grad_skip = lax.psum(skip_part, "row").reshape(width)
     else:
-        grad_skip = done[5]
-    return (*done[:4], grad_skip, done[4])
+        grad_skip = done[4]
+    return (*done[:4], grad_skip, grad_weight)
 
 
 def solution(mesh):

time: 62.1 us -> 58.9 us (0.948)
  blocking collectives: 19.5 us -> 15.5 us
    all_to_all x1, blocking collectives: 19.5 us -> 15.5 us  [exchange(): return lax.all_to_all(array, 'row', split_axis=0, concat_axis=0, tiled=True)]
    pallas_call x6 -> x8, Pallas kernels: 12.8 us -> 13.2 us  [call(): pl.pallas_call(kernel, name=name, out_shape=out_shape, in_specs=[pl.Block...]
  transfers between devices with their start and end apart: 2 -> 3, of which waited for: 2 -> 3; matrix products, arithmetic and copies ran while one was open for 0% -> 0% of each run, Pallas kernels for 10% -> 13%
where the time goes in v2:
time: 58.9 us; the launch traced here: 58.6 us
  waiting for transfers between devices  17.5 us (30%)
  blocking collectives  15.5 us (26%)
  Pallas kernels  13.2 us (22%)
  starting transfers between devices  11.5 us (20%)
  between operations  0.76 us (1%)
    all_to_all x2, waiting for transfers between devices, exchange(): return lax.all_to_all(array, 'row', split_axis=0, concat_axis=0, tiled=True)  17.3 us
    all_to_all x1, blocking collectives, exchange(): return lax.all_to_all(array, 'row', split_axis=0, concat_axis=0, tiled=True)  15.5 us
    pallas_call x8, Pallas kernels, call(): pl.pallas_call(kernel, name=name, out_shape=out_shape, in_specs=[pl.Block...  13.2 us
    all_to_all x2, starting transfers between devices, exchange(): return lax.all_to_all(array, 'row', split_axis=0, concat_axis=0, tiled=True)  11.4 us
  transfers between devices with their start and end apart: 3, of which 3 were waited for; matrix products, arithmetic and copies ran while one was open for 0% of the time, Pallas kernels for 13%

profile of v2, /device:TPU:0, one launch (start us, length us, event | category | flops | bytes accessed | tf_op | source)
XLA Modules:
  0.0 58.6 jit_solution(4968069712999734656)
XLA Ops:
  0.6 2.0 %pack.1 = bf16[256,896]{1,0:T(8,128)(2,1)} custom-call(bf16[2,128,384]{2,1,0:T(8,128)(2,1)} %feat_ref.3, bf16[2,128,384]{2,1,0:T(8,128)(2,1)} %cot_ref.3, f32[4,6,2,128]{3,2,1,0:T(2,128)} %rate_ref.3, f32[4,16,2,128]{3,2,1,0:T(2,128)} %input_ref.3, f32[4,16,2,128]{3,2,1,0:T(2,128)} %read_ref.3), custom_call_target="tpu_custom_call" | custom-call | flops 100663296 | bytes 786432 | tf_op jit(solution)/shard_map/pack/pallas_call | solution.py:450
  2.6 0.0 copy-start.6
  2.6 0.0 copy-start
  2.6 0.0 copy-start.1
  2.6 0.0 copy-start.2
  2.6 0.0 copy-start.3
  2.7 0.0 copy-start.4
  2.7 0.0 copy-start.5
  2.7 7.6 %all-to-all-start = ((bf16[16,16,896]{2,1,0:T(8,128)(2,1)}), bf16[16,16,896]{2,1,0:T(8,128)(2,1)S(1)}, u32[]{:S(2)}, u32[]{:S(2)}) async-start(bf16[16,16,896]{2,1,0:T(8,128)(2,1)} %bitcast.7), calls=%async_computation | async-start | bytes 917504 | tf_op jit(solution)/shard_map/all_to_all | solution.py:475
  10.2 0.0 copy-done.6
  10.3 0.0 copy-done
  10.3 0.0 copy-done.1
  10.3 0.0 copy-done.2
  10.3 0.0 copy-done.3
  10.3 0.0 copy-done.4
  10.3 0.0 copy-done.5
  10.3 3.0 %rows.1 = (f32[256,384]{1,0:T(8,128)S(1)}, f32[128,256]{1,0:T(8,128)S(1)}, f32[384,384]{1,0:T(8,128)S(1)}, f32[16,128]{1,0:T(8,128)S(1)}) custom-call(bf16[2,128,384]{2,1,0:T(8,128)(2,1)S(1)} %copy-done.1, bf16[2,128,384]{2,1,0:T(8,128)(2,1)S(1)} %copy-done.2, bf16[384,384]{1,0:T(8,128)(2,1)S(1)} %copy-done, f32[1,384]{1,0:T(1,128)S(1)} %reshape.19.skip_ref, ...), custom_call_target="tpu_custom_call" | custom-call | flops 226492416 | bytes 786432 | tf_op jit(solution)/shard_map/rows/pallas_call | solution.py:450
  13.4 10.1 %all-to-all-done = bf16[16,16,896]{2,1,0:T(8,128)(2,1)S(1)} async-done(((bf16[16,16,896]{2,1,0:T(8,128)(2,1)}), bf16[16,16,896]{2,1,0:T(8,128)(2,1)S(1)}, u32[]{:S(2)}, u32[]{:S(2)}) %all-to-all-start) | async-done | bytes 458784 | tf_op jit(solution)/shard_map/all_to_all | solution.py:475
  23.5 2.8 %forward.1 = bf16[384,384]{1,0:T(8,128)(2,1)} custom-call(bf16[256,896]{1,0:T(8,128)(2,1)S(1)} %bitcast.4, f32[384,384]{1,0:T(8,128)S(1)} %get-tuple-element.15.part_ref), custom_call_target="tpu_custom_call" | custom-call | flops 176160768 | bytes 786432 | tf_op jit(solution)/shard_map/forward/pallas_call | solution.py:450
  26.3 3.8 %all-to-all-start.1 = ((bf16[16,24,384]{2,1,0:T(8,128)(2,1)}), bf16[16,24,384]{2,1,0:T(8,128)(2,1)S(1)}, u32[]{:S(2)}, u32[]{:S(2)}) async-start(bf16[16,24,384]{2,1,0:T(8,128)(2,1)} %bitcast.2), calls=%async_computation.1 | async-start | bytes 589824 | tf_op jit(solution)/shard_map/all_to_all | solution.py:475
  30.1 3.3 %backward.1.back_ref = bf16[256,512]{1,0:T(8,128)(2,1)S(1)} custom-call(bf16[256,896]{1,0:T(8,128)(2,1)S(1)} %bitcast.5, bf16[384,384]{1,0:T(8,128)(2,1)S(1)} %copy-done, f32[16,128]{1,0:T(8,128)S(1)} %get-tuple-element.16.skip_ref), custom_call_target="tpu_custom_call" | custom-call | flops 226492416 | bytes 786432 | tf_op jit(solution)/shard_map/backward/pallas_call | solution.py:450
  33.4 7.3 %all-to-all-done.1 = bf16[16,24,384]{2,1,0:T(8,128)(2,1)S(1)} async-done(((bf16[16,24,384]{2,1,0:T(8,128)(2,1)}), bf16[16,24,384]{2,1,0:T(8,128)(2,1)S(1)}, u32[]{:S(2)}, u32[]{:S(2)}) %all-to-all-start.1) | async-done | bytes 294944 | tf_op jit(solution)/shard_map/all_to_all | solution.py:475
  40.6 0.1 sum.1
  40.7 15.5 %all_to_all.27.recv_ref = bf16[16,104,128]{2,1,0:T(8,128)(2,1)S(1)} all-to-all(bf16[16,104,128]{2,1,0:T(8,128)(2,1)S(1)} %sum.1), channel_id=1, replica_groups=mesh['grp'=2,'row'=16] {'row'}, dimensions={0} | all-to-all | bytes 851968 | tf_op jit(solution)/shard_map/all_to_all | solution.py:475
  56.2 0.2 collective-permute-start
  56.4 1.1 %finish.1 = (bf16[2,128,384]{2,1,0:T(8,128)(2,1)}, f32[4,6,2,128]{3,2,1,0:T(2,128)}, f32[4,16,2,128]{3,2,1,0:T(2,128)}, f32[4,16,2,128]{3,2,1,0:T(2,128)}, f32[384]{0:T(512)}) custom-call(bf16[16,104,128]{2,1,0:T(8,128)(2,1)S(1)} %all_to_all.27.recv_ref, f32[256,384]{1,0:T(8,128)S(1)} %get-tuple-element.17.gx_ref, f32[128,256]{1,0:T(8,128)S(1)} %get-tuple-element.18.small_ref), custom_call_target="tpu_custom_call" | custom-call | flops 50331648 | bytes 786432 | tf_op jit(solution)/shard_map/finish/pallas_call | solution.py:450
  57.5 0.2 collective-permute-done.theirs_ref
  57.7 0.9 %weight.1 = f32[384,384]{1,0:T(8,128)} custom-call(bf16[16,40,128]{2,1,0:T(8,128)(2,1)S(1)} %half.1.mine_ref, bf16[16,40,128]{2,1,0:T(8,128)(2,1)S(1)} %collective-permute-done.theirs_ref), custom_call_target="tpu_custom_call" | custom-call | flops 147456 | bytes 884736 | tf_op jit(solution)/shard_map/weight/pallas_call | solution.py:450
  (2 shorter events, 0.0 us)
Async XLA Ops:
  2.6 7.6 %copy-start.6 = (f32[384]{0:T(512)S(1)}, f32[384]{0:T(512)}, u32[]{:S(2)}) copy-start(f32[384]{0:T(512)} %param.11) | copy-start | bytes 4612
  2.6 7.6 %copy-start = (bf16[384,384]{1,0:T(8,128)(2,1)S(1)}, bf16[384,384]{1,0:T(8,128)(2,1)}, u32[]{:S(2)}) copy-start(bf16[384,384]{1,0:T(8,128)(2,1)} %weight_ref.3) | copy-start | bytes 884740
  2.6 7.6 %copy-start.1 = (bf16[2,128,384]{2,1,0:T(8,128)(2,1)S(1)}, bf16[2,128,384]{2,1,0:T(8,128)(2,1)}, u32[]{:S(2)}) copy-start(bf16[2,128,384]{2,1,0:T(8,128)(2,1)} %feat_ref.3) | copy-start | bytes 589828
  2.6 7.7 %copy-start.2 = (bf16[2,128,384]{2,1,0:T(8,128)(2,1)S(1)}, bf16[2,128,384]{2,1,0:T(8,128)(2,1)}, u32[]{:S(2)}) copy-start(bf16[2,128,384]{2,1,0:T(8,128)(2,1)} %cot_ref.3) | copy-start | bytes 589828
  2.6 7.7 %copy-start.3 = (f32[4,16,2,128]{3,2,1,0:T(2,128)S(1)}, f32[4,16,2,128]{3,2,1,0:T(2,128)}, u32[]{:S(2)}) copy-start(f32[4,16,2,128]{3,2,1,0:T(2,128)} %input_ref.3) | copy-start | bytes 196612
  2.7 7.7 %copy-start.4 = (f32[4,16,2,128]{3,2,1,0:T(2,128)S(1)}, f32[4,16,2,128]{3,2,1,0:T(2,128)}, u32[]{:S(2)}) copy-start(f32[4,16,2,128]{3,2,1,0:T(2,128)} %read_ref.3) | copy-start | bytes 196612
  2.7 7.7 %copy-start.5 = (f32[4,6,2,128]{3,2,1,0:T(2,128)S(1)}, f32[4,6,2,128]{3,2,1,0:T(2,128)}, u32[]{:S(2)}) copy-start(f32[4,6,2,128]{3,2,1,0:T(2,128)} %rate_ref.3) | copy-start | bytes 73732
  2.7 20.8 %all-to-all-start = ((bf16[16,16,896]{2,1,0:T(8,128)(2,1)}), bf16[16,16,896]{2,1,0:T(8,128)(2,1)S(1)}, u32[]{:S(2)}, u32[]{:S(2)}) async-start(bf16[16,16,896]{2,1,0:T(8,128)(2,1)} %bitcast.7), calls=%async_computation | async-start | bytes 917504 | tf_op jit(solution)/shard_map/all_to_all | solution.py:475
  26.3 14.3 %all-to-all-start.1 = ((bf16[16,24,384]{2,1,0:T(8,128)(2,1)}), bf16[16,24,384]{2,1,0:T(8,128)(2,1)S(1)}, u32[]{:S(2)}, u32[]{:S(2)}) async-start(bf16[16,24,384]{2,1,0:T(8,128)(2,1)} %bitcast.2), calls=%async_computation.1 | async-start | bytes 589824 | tf_op jit(solution)/shard_map/all_to_all | solution.py:475
  56.2 1.5 %collective-permute-start = (bf16[16,40,128]{2,1,0:T(8,128)(2,1)S(1)}, bf16[16,40,128]{2,1,0:T(8,128)(2,1)S(1)}, u32[]{:S(2)}, u32[]{:S(2)}) collective-permute-start(bf16[16,40,128]{2,1,0:T(8,128)(2,1)S(1)} %half.1.mine_ref), channel_id=1, source_target_pairs={{0,1},{1,0},{2,3},{3,2},{4,5},{5,4},{6,7},{7,6},{8,9},{9,8},{10,11... | collective-permute-start | bytes 491528 | tf_op jit(solution)/shard_map/ppermute | solution.py:525

commit v3 on v2

--- a/solution.py
+++ b/solution.py
@@ -215,9 +215,11 @@
 
 
 def rows_kernel(
-    slots, chunk, feat_ref, cot_ref, weight_ref, skip_ref, rate_ref, input_ref, read_ref,
-    gx_ref, small_ref, part_ref, skip_out_ref, rows_ref,
+    slots, chunk, tables, feat_ref, cot_ref, weight_ref, skip_ref, rate_ref, input_ref, read_ref,
+    gx_ref, small_ref, part_ref, skip_out_ref, *refs,
 ):
+    *table_refs, rows_ref = refs
+    tables.fill(table_refs)
     tile_rows, columns, width = feat_ref.shape
     tokens = tile_rows * columns
     skip = skip_ref[...]
@@ -261,138 +263,349 @@
 
 
 def skip_places(slots, width, piece):
-    place = lax.rem(iota((width, 1), 0), piece) + slots.used
+    at = iota((width, 1), 0)
+    whole = ((at.astype(F32) + 0.5) * (1.0 / piece)).astype(jnp.int32)
+    place = at - whole * piece + slots.used
     lane = iota((width, LANES), 1)
     high, low = place == lane, place + piece == lane
     return jnp.concatenate([high.astype(F32), low.astype(F32)], axis=0).astype(BF16)
 
 
-class Columns:
-    def __init__(self, slots, ranks, tile_rows, width, model, recv_ref):
-        tokens = recv_ref.shape[0]
-        self.line = ranks * tile_rows
-        narrow = tokens // self.line
-        self.block = max(self.line, min(LANES, tokens))
-        self.slots = slots
-
-        def source(at):
-            column, rank, row = split_index(at, (narrow, ranks, tile_rows))
-            return rank * (tile_rows * narrow) + row * narrow + column
-
-        def source_back(at):
-            rank, row, column = split_index(at, (ranks, tile_rows, narrow))
-            return column * self.line + rank * tile_rows + row
-
-        order = one_hot_rows(tokens, source)
-        self.source_back = source_back
-        self.feats = nn(order, recv_ref[:, :width]).astype(BF16)
-        self.cots = nn(order, recv_ref[:, width : width + model]).astype(BF16)
-        self.params = nn(order, recv_ref[:, width + model :])
-        self.spans = [slice(at, at + self.block) for at in range(0, tokens, self.block)]
-
-    def lines(self, span):
-        slots = self.slots
-        rows = jnp.transpose(self.params[span])
-        rates = [
-            rows[hi : hi + slots.pad] + rows[lo : lo + slots.pad]
-            for hi, lo in zip(slots.rates, slots.lows)
+def ordered_by_column(ranks, tile_rows, tokens):
+    line = ranks * tile_rows
+    narrow = tokens // line
+
+    def source(at):
+        column, rank, row = split_index(at, (narrow, ranks, tile_rows))
+        return rank * (tile_rows * narrow) + row * narrow + column
+
+    return one_hot_rows(tokens, source)
+
+
+def ordered_by_rank(ranks, tile_rows, tokens):
+    line = ranks * tile_rows
+    narrow = tokens // line
+
+    def source(at):
+        rank, row, column = split_index(at, (ranks, tile_rows, narrow))
+        return column * line + rank * tile_rows + row
+
+    return one_hot_rows(tokens, source)
+
+
+def blocks_of(line, tokens):
+    block = max(line, min(LANES, tokens))
+    return block, [slice(at, at + block) for at in range(0, tokens, block)]
+
+
+def long_lines(params, span, slots, line, block):
+    rows = jnp.transpose(params[span].astype(F32))
+    rates = [
+        rows[hi : hi + slots.pad] + rows[lo : lo + slots.pad]
+        for hi, lo in zip(slots.rates, slots.lows)
+    ]
+    return Lines(rows, rates, slots, line, block)
+
+
+def halves_of(array):
+    high = array.astype(BF16)
+    return high, (array - high.astype(F32)).astype(BF16)
+
+
+def reach_of(line, block):
+    at_t, at_u = iota((block, block), 0), iota((block, block), 1)
+    same = split_index(at_t, (block // line, line))[0] == (
+        split_index(at_u, (block // line, line))[0]
+    )
+    return same, (same & (at_t >= at_u), same & (at_t <= at_u))
+
+
+class Tables:
+    def __init__(self, slots, ranks, tile_rows, tokens, width):
+        line = ranks * tile_rows
+        block = blocks_of(line, tokens)[0]
+        self.slots, self.ranks, self.tile_rows = slots, ranks, tile_rows
+        self.tokens, self.width, self.line, self.block = tokens, width, line, block
+        self.shapes = [(tokens, tokens)] * 2
+        if line <= LONGEST_SHORT:
+            self.shapes += [(2 * block, block), (2 * LANES, 2 * width), (4 * width, LANES)]
+
+    def fill(self, refs):
+        slots, width, block = self.slots, self.width, self.block
+        size = width // slots.heads
+        refs[0][...] = ordered_by_column(self.ranks, self.tile_rows, self.tokens)
+        refs[1][...] = ordered_by_rank(self.ranks, self.tile_rows, self.tokens)
+        if self.line > LONGEST_SHORT:
+            return
+        same, reach = reach_of(self.line, block)
+        half = jnp.where(same, 0.5, 0.0)
+        for way in (0, 1):
+            refs[2][way * block : (way + 1) * block, :] = (
+                reach[way].astype(F32) - half
+            ).astype(BF16)
+            at = iota((LANES, width), 0)
+            head = split_index(iota((LANES, width), 1), (slots.heads, size))[0]
+            spread = (at == head + slots.rates[way]).astype(F32).astype(BF16)
+            lanes = slice(way * width, (way + 1) * width)
+            refs[3][:LANES, lanes] = spread
+            refs[3][LANES:, lanes] = spread
+            at = iota((width, LANES), 1)
+            head = split_index(iota((width, LANES), 0), (slots.heads, size))[0]
+            gather = (at == head + slots.rates[way]).astype(F32).astype(BF16)
+            refs[4][way * width : (way + 1) * width, :] = gather
+            refs[4][(2 + way) * width : (3 + way) * width, :] = gather
+
+
+class ShortLines:
+    def __init__(self, params, slots, line, block, spans, width, tables):
+        self.slots, self.spans, self.block = slots, spans, block
+        self.tables = tables
+        self.reach = reach_of(line, block)[1]
+        tokens = params.shape[0]
+        lane = iota((tokens, LANES), 1)
+        states = slots.states
+        ways = tables[2][...]
+        sums = [nn(ways, params[span]) for span in spans]
+        low_up = lane >= slots.lows[1]
+        self.up_lane = ((lane >= slots.rates[1]) & (lane < slots.lows[0])) | low_up
+        sums = jnp.where(
+            self.up_lane,
+            jnp.concatenate([both[block:] for both in sums], axis=0),
+            jnp.concatenate([both[:block] for both in sums], axis=0),
+        )
+        wide = params.astype(F32)
+        turned = pltpu.roll(wide, LANES - slots.reads[0], 1)
+        first, second = lane < states, (lane >= states) & (lane < 2 * states)
+        self.inputs = [jnp.where(mask, wide, 0.0).astype(BF16) for mask in (first, second)]
+        self.reads = [jnp.where(mask, turned, 0.0).astype(BF16) for mask in (first, second)]
+        scores = [
+            nt(jnp.concatenate([read[span] for read in self.reads], axis=0), params[span])
+            for span in spans
         ]
-        return Lines(rows, rates, slots, self.line, self.block)
-
-
-def forward_kernel(slots, ranks, tile_rows, recv_ref, part_ref, sum_ref):
+        self.scores = [
+            [
+                jnp.where(self.reach[way], both[way * block : (way + 1) * block], 0.0).astype(BF16)
+                for both in scores
+            ]
+            for way in (0, 1)
+        ]
+        sums = sums + pltpu.roll(sums, LANES - (slots.lows[0] - slots.rates[0]), 1)
+        rated = (lane >= slots.rates[0]) & (lane < slots.lows[0])
+        sums = jnp.where(rated, sums, 0.0)
+        spread = tables[3][...]
+
+        def widen(narrow):
+            wide = nn(jnp.concatenate(halves_of(narrow), axis=1), spread)
+            return wide[:, :width], wide[:, width:]
+
+        self.losses, self.gains = widen(jnp.exp(sums)), widen(jnp.exp(-sums))
+
+    def per_block(self, way, product, right):
+        return jnp.concatenate(
+            [
+                product(score, right[span])
+                for score, span in zip(self.scores[way], self.spans)
+            ],
+            axis=0,
+        )
+
+    def values(self, feats):
+        wide = feats.astype(F32)
+        self.lost = [(wide * loss).astype(BF16) for loss in self.losses]
+        self.mixed = [self.per_block(way, nn, self.lost[way]) for way in (0, 1)]
+
+    def forward(self, feats):
+        self.values(feats)
+        return self.gains[0] * self.mixed[0] + self.gains[1] * self.mixed[1]
+
+    def backward(self, feats, grads):
+        self.values(feats)
+        slots, spans = self.slots, self.spans
+        wide = grads.astype(F32)
+        gained = [(wide * gain).astype(BF16) for gain in self.gains]
+        back = [self.per_block(way, tn, gained[way]) for way in (0, 1)]
+        gx = self.losses[0] * back[0] + self.losses[1] * back[1]
+        score_grads = [
+            [
+                jnp.where(
+                    self.reach[way], nt(gained[way][span], self.lost[way][span]), 0.0
+                ).astype(BF16)
+                for way in (0, 1)
+            ]
+            for span in spans
+        ]
+        change = jnp.concatenate(
+            [
+                self.lost[way].astype(F32) * back[way] - gained[way].astype(F32) * self.mixed[way]
+                for way in (0, 1)
+            ],
+            axis=1,
+        )
+        heads = nn(jnp.concatenate(halves_of(change), axis=1), self.tables[4][...])
+        read_grads = [
+            nn(
+                jnp.concatenate(score_grads[at], axis=1),
+                jnp.concatenate([part[span] for part in self.inputs], axis=0),
+            )
+            for at, span in enumerate(spans)
+        ]
+        input_grads = [
+            tn(
+                jnp.concatenate(score_grads[at], axis=0),
+                jnp.concatenate([part[span] for part in self.reads], axis=0),
+            )
+            for at, span in enumerate(spans)
+        ]
+        since, till = (mask.astype(F32).astype(BF16) for mask in self.reach)
+        both = jnp.concatenate(
+            [jnp.concatenate([till, till], axis=1), jnp.concatenate([since, since], axis=1)], axis=0
+        )
+        high, low = halves_of(heads)
+        reached = [
+            nn(both, jnp.concatenate([high[span], low[span]], axis=0)) for span in spans
+        ]
+        rates = jnp.where(
+            self.up_lane,
+            jnp.concatenate([pair[self.block :] for pair in reached], axis=0),
+            jnp.concatenate([pair[: self.block] for pair in reached], axis=0),
+        )
+        smalls = jnp.concatenate(input_grads, axis=0) + pltpu.roll(
+            jnp.concatenate(read_grads, axis=0), slots.reads[0], 1
+        )
+        lane = iota(smalls.shape, 1)
+        return gx, jnp.where(lane >= slots.rates[0], rates, smalls)
+
+
+LONGEST_SHORT = 64
+
+
+def forward_kernel(slots, ranks, tile_rows, recv_ref, part_ref, *refs):
+    *tables, mine_ref, other_ref, order_ref = refs
     width, model = part_ref.shape
-    cols = Columns(slots, ranks, tile_rows, width, model, recv_ref)
-    outs = [
-        scan_block(cols.feats[span], None, cols.lines(span), slots, None, None, True, False)[0]
-        for span in cols.spans
-    ]
-    down = jnp.concatenate(outs, axis=0).astype(BF16)
-    sum_ref[...] = (part_ref[...] + tn(down, cols.cots)).astype(BF16)
-
-
-def backward_kernel(
-    slots, ranks, tile_rows, chunk, recv_ref, weight_ref, skip_ref, back_ref, small_ref
-):
+    tokens = recv_ref.shape[0]
+    line = ranks * tile_rows
+    block, spans = blocks_of(line, tokens)
+    order = tables[0][...]
+    params = nn(order, recv_ref[:, width + model :]).astype(BF16)
+    feats = nn(order, recv_ref[:, :width]).astype(BF16)
+    cots = nn(order, recv_ref[:, width : width + model]).astype(BF16)
+    order_ref[:, width + model :] = params
+    order_ref[:, :width] = feats
+    order_ref[:, width : width + model] = cots
+    if line <= LONGEST_SHORT:
+        lines = ShortLines(params, slots, line, block, spans, width, tables)
+        down = lines.forward(feats).astype(BF16)
+    else:
+        outs = []
+        for span in spans:
+            lines = long_lines(params, span, slots, line, block)
+            outs.append(scan_block(feats[span], None, lines, slots, None, None, True, False)[0])
+        down = jnp.concatenate(outs, axis=0).astype(BF16)
+    total = part_ref[...] + tn(down, cots)
+    even = lax.rem(lax.axis_index("row"), 2) == 0
+    half = width // 2
+    mine_ref[...] = jnp.where(even, total[:half], total[half:])
+    other_ref[...] = jnp.where(even, total[half:], total[:half]).astype(BF16)
+
+
+def backward_kernel(slots, ranks, tile_rows, chunk, order_ref, weight_ref, skip_ref, *refs):
+    *tables, back_ref, small_ref = refs
     width, model = weight_ref.shape
-    cols = Columns(slots, ranks, tile_rows, width, model, recv_ref)
-    grads = nt(cols.cots, weight_ref[...]).astype(BF16)
-    small_ref[...] = jnp.zeros_like(small_ref)
-    gxs = [
-        scan_block(
-            cols.feats[span], grads[span], cols.lines(span), slots, small_ref, span, False, True
-        )[1].astype(BF16)
-        for span in cols.spans
-    ]
-    order_back = one_hot_rows(recv_ref.shape[0], cols.source_back)
-    back_ref[:, :width] = nn(order_back, jnp.concatenate(gxs, axis=0)).astype(BF16)
-    smalls = nt(order_back, small_ref[...].astype(BF16))
+    tokens = order_ref.shape[0]
+    line = ranks * tile_rows
+    block, spans = blocks_of(line, tokens)
+    params = order_ref[:, width + model :]
+    feats = order_ref[:, :width]
+    grads = nt(order_ref[:, width : width + model], weight_ref[...]).astype(BF16)
+    if line <= LONGEST_SHORT:
+        lines = ShortLines(params, slots, line, block, spans, width, tables)
+        gx, small = lines.backward(feats, grads)
+        gx, small = gx.astype(BF16), small.astype(BF16)
+    else:
+        small_ref[...] = jnp.zeros_like(small_ref)
+        gxs = []
+        for span in spans:
+            lines = long_lines(params, span, slots, line, block)
+            gxs.append(
+                scan_block(feats[span], grads[span], lines, slots, small_ref, span, False, True)[1]
+            )
+        gx = jnp.concatenate(gxs, axis=0).astype(BF16)
+        small = jnp.transpose(small_ref[...]).astype(BF16)
+    order_back = tables[1][...]
+    back_ref[:, :width] = nn(order_back, gx).astype(BF16)
+    small = nn(order_back, small)
     if chunk is not None:
-        smalls = smalls + jnp.concatenate([skip_ref[...]] * ranks, axis=0)
-    back_ref[:, width:] = smalls.astype(BF16)
+        small = small + jnp.concatenate([skip_ref[...]] * ranks, axis=0)
+    back_ref[:, width:] = small.astype(BF16)
 
 
 def strip(array):
     return [array[:, at : at + LANES] for at in range(0, array.shape[1], LANES)]
 
 
-class Halves:
-    def __init__(self, rows, model):
-        self.unit = 8 if rows % 8 == 0 else rows
+class Tiles:
+    def __init__(self, rows, model, ranks):
+        self.unit = 8
         steps = rows // self.unit
         self.places = [
             (at * self.unit, lane) for lane in range(0, model, LANES) for at in range(steps)
         ]
-        self.count = -(-len(self.places) // 2)
-        self.size = self.count * self.unit
-
-    def of(self, index):
-        return divmod(index, self.count)
-
-
-def sum_kernel(ranks, parts_ref, back_ref, out_ref):
-    rows, model = parts_ref.shape[0] // ranks, parts_ref.shape[1]
-    total = parts_ref[:rows, :].astype(F32)
-    for rank in range(1, ranks):
-        total = total + parts_ref[rank * rows : (rank + 1) * rows, :].astype(F32)
+        count = len(self.places)
+        self.starts = [count * rank // ranks for rank in range(ranks + 1)]
+        self.size = self.unit * -(-count // ranks)
+
+    def of(self, rank):
+        return self.places[self.starts[rank] : self.starts[rank + 1]]
+
+
+def merge_kernel(ranks, mine_ref, theirs_ref, back_ref, out_ref):
+    total = mine_ref[...] + theirs_ref[...].astype(F32)
     tokens = back_ref.shape[0] // ranks
-    halves = Halves(rows, model)
-    unit = halves.unit
-    blocks = [
-        total[at : at + unit, lane : lane + LANES].astype(BF16) for at, lane in halves.places
-    ]
-    blocks += [jnp.zeros_like(blocks[0])] * (2 * halves.count - len(blocks))
+    tiles = Tiles(*mine_ref.shape, ranks)
+    unit = tiles.unit
     for rank in range(ranks):
         at = 0
         for piece in strip(back_ref[rank * tokens : (rank + 1) * tokens, :]):
             out_ref[rank, at : at + tokens, :] = piece
             at += tokens
-        half = rank % 2
-        for piece in blocks[half * halves.count : (half + 1) * halves.count]:
-            out_ref[rank, at : at + unit, :] = piece
+        end = at + tiles.size
+        for row, lane in tiles.of(rank):
+            out_ref[rank, at : at + unit, :] = total[row : row + unit, lane : lane + LANES].astype(
+                BF16
+            )
             at += unit
-
-
-def half_kernel(recv_ref, out_ref):
-    size = out_ref.shape[1]
-    out_ref[...] = recv_ref[:, recv_ref.shape[1] - size :, :]
+        while at < end:
+            out_ref[rank, at : at + unit, :] = jnp.zeros((unit, LANES), BF16)
+            at += unit
+
+
+def sum_kernel(recv_ref, out_ref):
+    ranks, size = out_ref.shape[:2]
+    own = slice(recv_ref.shape[1] - size, recv_ref.shape[1])
+    for half in (0, 1):
+        total = recv_ref[half, own, :].astype(F32)
+        for rank in range(half + 2, ranks, 2):
+            total = total + recv_ref[rank, own, :].astype(F32)
+        total = total.astype(BF16)
+        for rank in range(half, ranks, 2):
+            out_ref[rank] = total
 
 
 def weight_kernel(mine_ref, theirs_ref, out_ref):
     ranks = mine_ref.shape[0]
     width, model = out_ref.shape
-    rows = width // ranks
-    halves = Halves(rows, model)
-    unit = halves.unit
+    tiles = Tiles(width // 2, model, ranks)
+    unit = tiles.unit
     even = lax.rem(lax.axis_index("row"), 2) == 0
     mine, theirs = mine_ref[...].astype(F32), theirs_ref[...].astype(F32)
     pair = (jnp.where(even, mine, theirs), jnp.where(even, theirs, mine))
-    for rank in range(ranks):
-        for index, (at, lane) in enumerate(halves.places):
-            half, step = halves.of(index)
-            out_ref[rank * rows + at : rank * rows + at + unit, lane : lane + LANES] = pair[half][
-                rank, step * unit : (step + 1) * unit, :
-            ]
+    for half in (0, 1):
+        for rank in range(ranks):
+            for step, (row, lane) in enumerate(tiles.of(rank)):
+                row += half * (width // 2)
+                out_ref[row : row + unit, lane : lane + LANES] = pair[half][
+                    rank, step * unit : (step + 1) * unit, :
+                ]
 
 
 def finish_kernel(
@@ -435,11 +648,10 @@
     if chunk is not None:
         piece = width // chunk
         gathered = jnp.sum(back, axis=0)
-        places = skip_places(slots, width, piece).astype(F32)
+        places = skip_places(slots, width, piece)
         places = places[:width] + places[width:]
-        spread = lax.dot_general(
-            gathered, places, (((1,), (1,)), ((), ())), precision=HI, preferred_element_type=F32
-        )
+        high, low = halves_of(gathered)
+        spread = nt(high, places) + nt(low, places)
         lane_of = iota((chunk, width), 1)
         start = iota((chunk, width), 0) * piece
         owned = (lane_of >= start) & (lane_of < start + piece)
@@ -483,13 +695,15 @@
     )
     received = exchange(packed)
     skip_shape = (1, width) if chunk is None else (chunk, LANES)
-    gx_rows, small_rows, partial, skip_part = call(
-        functools.partial(rows_kernel, slots, chunk), "rows",
+    tables = Tables(slots, ranks, tile_rows, tokens, width)
+    gx_rows, small_rows, partial, skip_part, *table = call(
+        functools.partial(rows_kernel, slots, chunk, tables), "rows",
         (
             shape((tokens, width), F32),
             shape((LANES, tokens), F32),
             shape((width, model), F32),
             shape(skip_shape, F32),
+            *(shape(sizes, BF16) for sizes in tables.shapes),
         ),
         (
             features, out_cotangent, out_weight, skip_gain.reshape(1, width),
@@ -498,31 +712,40 @@
         [pltpu.VMEM((LANES, columns), F32)],
         flops=2 * tokens * width * (2 * model + 3 * columns), moved=8 * tokens * width,
     )
-    weight_sum = call(
+    half = width // 2
+    partners = [(rank, rank ^ 1) for rank in range(ranks)]
+    mine, other, ordered = call(
         functools.partial(forward_kernel, slots, ranks, tile_rows), "forward",
-        shape((width, model), BF16), (received, partial),
+        (
+            shape((half, model), F32),
+            shape((half, model), BF16),
+            shape(received.shape, BF16),
+        ),
+        (received, partial, *table),
         flops=2 * tokens * width * (2 * model + columns), moved=8 * tokens * width,
     )
-    weight_parts = exchange(weight_sum)
+    theirs = lax.ppermute(other, "row", partners)
     back = call(
         functools.partial(backward_kernel, slots, ranks, tile_rows, chunk), "backward",
-        shape((tokens, width + LANES), BF16), (received, out_weight, skip_part),
+        shape((tokens, width + LANES), BF16), (ordered, out_weight, skip_part, *table),
         [pltpu.VMEM((LANES, tokens), F32)],
         flops=2 * tokens * width * (2 * model + 3 * columns), moved=8 * tokens * width,
     )
     group = tokens // ranks
-    size = Halves(width // ranks, model).size
-    last = call(
-        functools.partial(sum_kernel, ranks), "sum",
-        shape((ranks, (width // LANES + 1) * group + size, LANES), BF16), (weight_parts, back),
+    size = Tiles(half, model, ranks).size
+    merged = call(
+        functools.partial(merge_kernel, ranks), "merge",
+        shape((ranks, (width // LANES + 1) * group + size, LANES), BF16), (mine, theirs, back),
         flops=width * model, moved=2 * width * model,
     )
-    returned = exchange(last)
-    mine = call(
-        half_kernel, "half", shape((ranks, size, LANES), BF16), (returned,),
+    returned = exchange(merged)
+    summed = call(
+        sum_kernel, "sum", shape((ranks, size, LANES), BF16), (returned,),
         flops=width * model, moved=2 * width * model,
     )
-    theirs = lax.ppermute(mine, "row", [(rank, rank ^ 1) for rank in range(ranks)])
+    held = exchange(summed)
+    swapped = lax.ppermute(held, "row", partners)
+    returned, held = lax.optimization_barrier((returned, held))
     outs = [
         shape(features.shape, BF16),
         shape(decay_rate.shape, F32),
@@ -537,7 +760,7 @@
         flops=2 * tokens * tokens * width, moved=8 * tokens * width,
     )
     grad_weight = call(
-        weight_kernel, "weight", shape((width, model), F32), (mine, theirs),
+        weight_kernel, "weight", shape((width, model), F32), (held, swapped),
         flops=width * model, moved=6 * width * model,
     )
     if chunk is None:

time: 58.9 us -> 57.8 us (0.981)
  blocking collectives: 15.5 us -> 28.4 us
  waiting for transfers between devices: 17.5 us -> 10.3 us
  starting transfers between devices: 11.5 us -> 7.74 us
  Pallas kernels: 13.2 us -> 10.2 us
    all_to_all x1 -> x2, blocking collectives: 15.5 us -> 28.4 us  [exchange(): return lax.all_to_all(array, 'row', split_axis=0, concat_axis=0, tiled=True)]
    all_to_all x2 -> x1, waiting for transfers between devices: 17.3 us -> 9.87 us  [exchange(): return lax.all_to_all(array, 'row', split_axis=0, concat_axis=0, tiled=True)]
    all_to_all x2 -> x1, starting transfers between devices: 11.4 us -> 7.56 us  [exchange(): return lax.all_to_all(array, 'row', split_axis=0, concat_axis=0, tiled=True)]
    pallas_call x8, Pallas kernels: 13.2 us -> 10.2 us  [call(): pl.pallas_call(kernel, name=name, out_shape=out_shape, in_specs=[pl.Block...]
  transfers between devices with their start and end apart: 3 -> 3, of which waited for: 3 -> 2; matrix products, arithmetic and copies ran while one was open for 0% -> 0% of each run, Pallas kernels for 13% -> 11%
where the time goes in v3:
time: 57.8 us; the launch traced here: 57.5 us
  blocking collectives  28.4 us (49%)
  waiting for transfers between devices  10.3 us (18%)
  Pallas kernels  10.2 us (18%)
  starting transfers between devices  7.74 us (13%)
  between operations  0.77 us (1%)
    all_to_all x2, blocking collectives, exchange(): return lax.all_to_all(array, 'row', split_axis=0, concat_axis=0, tiled=True)  28.4 us
    pallas_call x8, Pallas kernels, call(): pl.pallas_call(kernel, name=name, out_shape=out_shape, in_specs=[pl.Block...  10.2 us
    all_to_all x1, waiting for transfers between devices, exchange(): return lax.all_to_all(array, 'row', split_axis=0, concat_axis=0, tiled=True)  9.87 us
    all_to_all x1, starting transfers between devices, exchange(): return lax.all_to_all(array, 'row', split_axis=0, concat_axis=0, tiled=True)  7.56 us
  transfers between devices with their start and end apart: 3, of which 2 were waited for; matrix products, arithmetic and copies ran while one was open for 0% of the time, Pallas kernels for 11%

profile of v3, /device:TPU:0, one launch (start us, length us, event | category | flops | bytes accessed | tf_op | source)
XLA Modules:
  0.0 57.5 jit_solution(13781739654583138675)
XLA Ops:
  0.6 2.0 %pack.1 = bf16[256,896]{1,0:T(8,128)(2,1)} custom-call(bf16[2,128,384]{2,1,0:T(8,128)(2,1)} %feat_ref.3, bf16[2,128,384]{2,1,0:T(8,128)(2,1)} %cot_ref.3, f32[4,6,2,128]{3,2,1,0:T(2,128)} %rate_ref.3, f32[4,16,2,128]{3,2,1,0:T(2,128)} %input_ref.3, f32[4,16,2,128]{3,2,1,0:T(2,128)} %read_ref.3), custom_call_target="tpu_custom_call" | custom-call | flops 100663296 | bytes 786432 | tf_op jit(solution)/shard_map/pack/pallas_call | solution.py:662
  2.6 0.0 copy-start.6
  2.6 0.0 copy-start
  2.6 0.0 copy-start.1
  2.6 0.0 copy-start.2
  2.6 0.0 copy-start.3
  2.7 0.0 copy-start.4
  2.7 0.0 copy-start.5
  2.7 7.6 %all-to-all-start = ((bf16[16,16,896]{2,1,0:T(8,128)(2,1)}), bf16[16,16,896]{2,1,0:T(8,128)(2,1)S(1)}, u32[]{:S(2)}, u32[]{:S(2)}) async-start(bf16[16,16,896]{2,1,0:T(8,128)(2,1)} %bitcast.3), calls=%async_computation | async-start | bytes 917504 | tf_op jit(solution)/shard_map/all_to_all | solution.py:687
  10.2 0.0 copy-done.6
  10.3 0.0 copy-done
  10.3 0.0 copy-done.1
  10.3 0.0 copy-done.2
  10.3 0.0 copy-done.3
  10.3 0.0 copy-done.4
  10.3 0.0 copy-done.5
  10.3 3.3 %rows.1 = (f32[256,384]{1,0:T(8,128)S(1)}, f32[128,256]{1,0:T(8,128)S(1)}, f32[384,384]{1,0:T(8,128)S(1)}, f32[16,128]{1,0:T(8,128)S(1)}, bf16[256,256]{1,0:T(8,...) custom-call(bf16[2,128,384]{2,1,0:T(8,128)(2,1)S(1)} %copy-done.1, ...), custom_call_target="tpu_custom_call" | custom-call | flops 226492416 | bytes 786432 | tf_op jit(solution)/shard_map/rows/pallas_call | solution.py:662
  13.6 9.9 %all-to-all-done = bf16[16,16,896]{2,1,0:T(8,128)(2,1)S(1)} async-done(((bf16[16,16,896]{2,1,0:T(8,128)(2,1)}), bf16[16,16,896]{2,1,0:T(8,128)(2,1)S(1)}, u32[]{:S(2)}, u32[]{:S(2)}) %all-to-all-start) | async-done | bytes 458784 | tf_op jit(solution)/shard_map/all_to_all | solution.py:687
  23.5 1.2 %forward.1 = (f32[192,384]{1,0:T(8,128)S(1)}, bf16[192,384]{1,0:T(8,128)(2,1)S(1)}, bf16[256,896]{1,0:T(8,128)(2,1)S(1)}) custom-call(bf16[256,896]{1,0:T(8,128)(2,1)S(1)} %bitcast.2, f32[384,384]{1,0:T(8,128)S(1)} %get-tuple-element.25.part_ref, bf16[256,256]{1,0:T(8,128)(2,1)S(1)} %get-tuple-element.26.refs_0_, ...), custom_call_target="tpu_custom_call" | custom-call | flops 176160768 | bytes 786432 | tf_op jit(solution)/shard_map/forward/pallas_call | solution.py:662
  24.6 0.2 collective-permute-start
  24.8 1.9 %backward.1.back_ref = bf16[256,512]{1,0:T(8,128)(2,1)S(1)} custom-call(bf16[256,896]{1,0:T(8,128)(2,1)S(1)} %get-tuple-element.33.order_ref, bf16[384,384]{1,0:T(8,128)(2,1)S(1)} %copy-done, f32[16,128]{1,0:T(8,128)S(1)} %get-tuple-element.34.skip_ref, bf16[256,256]{1,0:T(8,128)(2,1)S(1)} %get-tuple-element.26.refs_0_, ...), custom_call_target="tpu_custom_call" | custom-call | flops 226492416 | bytes 786432 | tf_op jit(solution)/shard_map/backward/pallas_call | solution.py:662
  26.7 0.0 collective-permute-done.theirs_ref
  26.7 0.1 merge.1
  26.8 16.6 %all_to_all.21.recv_ref = bf16[16,104,128]{2,1,0:T(8,128)(2,1)S(1)} all-to-all(bf16[16,104,128]{2,1,0:T(8,128)(2,1)S(1)} %merge.1), channel_id=1, replica_groups=mesh['grp'=2,'row'=16] {'row'}, dimensions={0} | all-to-all | bytes 851968 | tf_op jit(solution)/shard_map/all_to_all | solution.py:687
  43.4 11.8 %all_to_all.22.mine_ref = bf16[16,40,128]{2,1,0:T(8,128)(2,1)S(1)} all-to-all(bf16[16,40,128]{2,1,0:T(8,128)(2,1)S(1)} %sum.1), channel_id=1, replica_groups=mesh['grp'=2,'row'=16] {'row'}, dimensions={0} | all-to-all | bytes 327680 | tf_op jit(solution)/shard_map/all_to_all | solution.py:687
  55.2 0.0 collective-permute-start.1
  55.2 1.0 %finish.1 = (bf16[2,128,384]{2,1,0:T(8,128)(2,1)}, f32[4,6,2,128]{3,2,1,0:T(2,128)}, f32[4,16,2,128]{3,2,1,0:T(2,128)}, f32[4,16,2,128]{3,2,1,0:T(2,128)}, f32[384]{0:T(512)}) custom-call(bf16[16,104,128]{2,1,0:T(8,128)(2,1)S(1)} %all_to_all.21.recv_ref, f32[256,384]{1,0:T(8,128)S(1)} %get-tuple-element.36.gx_ref, f32[128,256]{1,0:T(8,128)S(1)} %get-tuple-element.37.small_ref), custom_call_target="tpu_custom_call" | custom-call | flops 50331648 | bytes 786432 | tf_op jit(solution)/shard_map/finish/pallas_call | solution.py:662
  56.2 0.4 collective-permute-done.1.theirs_ref
  56.6 0.9 %weight.1 = f32[384,384]{1,0:T(8,128)} custom-call(bf16[16,40,128]{2,1,0:T(8,128)(2,1)S(1)} %all_to_all.22.mine_ref, bf16[16,40,128]{2,1,0:T(8,128)(2,1)S(1)} %collective-permute-done.1.theirs_ref), custom_call_target="tpu_custom_call" | custom-call | flops 147456 | bytes 884736 | tf_op jit(solution)/shard_map/weight/pallas_call | solution.py:662
  (2 shorter events, 0.0 us)
Async XLA Ops:
  2.6 7.6 %copy-start.6 = (f32[384]{0:T(512)S(1)}, f32[384]{0:T(512)}, u32[]{:S(2)}) copy-start(f32[384]{0:T(512)} %param.11) | copy-start | bytes 4612
  2.6 7.6 %copy-start = (bf16[384,384]{1,0:T(8,128)(2,1)S(1)}, bf16[384,384]{1,0:T(8,128)(2,1)}, u32[]{:S(2)}) copy-start(bf16[384,384]{1,0:T(8,128)(2,1)} %weight_ref.3) | copy-start | bytes 884740
  2.6 7.6 %copy-start.1 = (bf16[2,128,384]{2,1,0:T(8,128)(2,1)S(1)}, bf16[2,128,384]{2,1,0:T(8,128)(2,1)}, u32[]{:S(2)}) copy-start(bf16[2,128,384]{2,1,0:T(8,128)(2,1)} %feat_ref.3) | copy-start | bytes 589828
  2.6 7.7 %copy-start.2 = (bf16[2,128,384]{2,1,0:T(8,128)(2,1)S(1)}, bf16[2,128,384]{2,1,0:T(8,128)(2,1)}, u32[]{:S(2)}) copy-start(bf16[2,128,384]{2,1,0:T(8,128)(2,1)} %cot_ref.3) | copy-start | bytes 589828
  2.6 7.7 %copy-start.3 = (f32[4,16,2,128]{3,2,1,0:T(2,128)S(1)}, f32[4,16,2,128]{3,2,1,0:T(2,128)}, u32[]{:S(2)}) copy-start(f32[4,16,2,128]{3,2,1,0:T(2,128)} %input_ref.3) | copy-start | bytes 196612
  2.7 7.7 %copy-start.4 = (f32[4,16,2,128]{3,2,1,0:T(2,128)S(1)}, f32[4,16,2,128]{3,2,1,0:T(2,128)}, u32[]{:S(2)}) copy-start(f32[4,16,2,128]{3,2,1,0:T(2,128)} %read_ref.3) | copy-start | bytes 196612
  2.7 7.7 %copy-start.5 = (f32[4,6,2,128]{3,2,1,0:T(2,128)S(1)}, f32[4,6,2,128]{3,2,1,0:T(2,128)}, u32[]{:S(2)}) copy-start(f32[4,6,2,128]{3,2,1,0:T(2,128)} %rate_ref.3) | copy-start | bytes 73732
  2.7 20.8 %all-to-all-start = ((bf16[16,16,896]{2,1,0:T(8,128)(2,1)}), bf16[16,16,896]{2,1,0:T(8,128)(2,1)S(1)}, u32[]{:S(2)}, u32[]{:S(2)}) async-start(bf16[16,16,896]{2,1,0:T(8,128)(2,1)} %bitcast.3), calls=%async_computation | async-start | bytes 917504 | tf_op jit(solution)/shard_map/all_to_all | solution.py:687
  24.6 2.0 %collective-permute-start = (bf16[192,384]{1,0:T(8,128)(2,1)S(1)}, bf16[192,384]{1,0:T(8,128)(2,1)S(1)}, u32[]{:S(2)}, u32[]{:S(2)}) collective-permute-start(bf16[192,384]{1,0:T(8,128)(2,1)S(1)} %get-tuple-element.32), channel_id=1, source_target_pairs={{0,1},{1,0},{2,3},{3,2},{4,5},{5,4},{6,7},{7,6},{8,9},{9,8},{10,11... | collective-permute-start | bytes 442376 | tf_op jit(solution)/shard_map/ppermute | solution.py:727
  55.2 1.4 %collective-permute-start.1 = (bf16[16,40,128]{2,1,0:T(8,128)(2,1)S(1)}, bf16[16,40,128]{2,1,0:T(8,128)(2,1)S(1)}, u32[]{:S(2)}, u32[]{:S(2)}) collective-permute-start(bf16[16,40,128]{2,1,0:T(8,128)(2,1)S(1)} %all_to_all.22.mine_ref), channel_id=1, source_target_pairs={{0,1},{1,0},{2,3},{3,2},{4,5},{5,4},{6,7},{7,6},{8,9},{9,8},{10,11... | collective-permute-start | bytes 491528 | tf_op jit(solution)/shard_map/ppermute | solution.py:747

commit v4 on v3

--- a/solution.py
+++ b/solution.py
@@ -41,11 +41,6 @@
             parts.append(lax.rem(index, size))
             index = lax.div(index, size)
     return parts[::-1]
-
-
-def one_hot_rows(count, source_of):
-    wanted = source_of(iota((count, 1), 0))
-    return (wanted == iota((count, count), 1)).astype(F32).astype(BF16)
 
 
 class Slots:
@@ -62,14 +57,14 @@
 
 
 class Lines:
-    def __init__(self, rows, rates, slots, line, block):
+    def __init__(self, rows, rates, slots, lines, block):
         at_t, at_u = iota((block, block), 0), iota((block, block), 1)
+        self.same = None
+        if lines > 1:
+            at_t, line_t = split_index(at_t, (block // lines, lines))
+            at_u, line_u = split_index(at_u, (block // lines, lines))
+            self.same = line_t == line_u
         self.below, self.above = at_t > at_u, at_t < at_u
-        self.same = None
-        if line < block:
-            line_t = split_index(at_t, (block // line, line))[0]
-            line_u = split_index(at_u, (block // line, line))[0]
-            self.same = line_t == line_u
         self.till = self.within(at_t <= at_u)
         self.since = self.within(at_t >= at_u)
         self.sums = (
@@ -237,7 +232,7 @@
             at = slots.rates[way]
             rows_ref[at : at + slots.heads, :] = rate_ref[way, :, row, :]
         rates = [rows_ref[at : at + slots.pad, :] for at in slots.rates]
-        lines = Lines(rows_ref, rates, slots, columns, columns)
+        lines = Lines(rows_ref, rates, slots, 1, columns)
         outs, gx = scan_block(
             feats, grads, lines, slots, small_ref,
             slice(row * columns, (row + 1) * columns), True, True,
@@ -271,40 +266,13 @@
     return jnp.concatenate([high.astype(F32), low.astype(F32)], axis=0).astype(BF16)
 
 
-def ordered_by_column(ranks, tile_rows, tokens):
-    line = ranks * tile_rows
-    narrow = tokens // line
-
-    def source(at):
-        column, rank, row = split_index(at, (narrow, ranks, tile_rows))
-        return rank * (tile_rows * narrow) + row * narrow + column
-
-    return one_hot_rows(tokens, source)
-
-
-def ordered_by_rank(ranks, tile_rows, tokens):
-    line = ranks * tile_rows
-    narrow = tokens // line
-
-    def source(at):
-        rank, row, column = split_index(at, (ranks, tile_rows, narrow))
-        return column * line + rank * tile_rows + row
-
-    return one_hot_rows(tokens, source)
-
-
-def blocks_of(line, tokens):
-    block = max(line, min(LANES, tokens))
-    return block, [slice(at, at + block) for at in range(0, tokens, block)]
-
-
-def long_lines(params, span, slots, line, block):
-    rows = jnp.transpose(params[span].astype(F32))
+def long_lines(params, slots, lines):
+    rows = jnp.transpose(params.astype(F32))
     rates = [
         rows[hi : hi + slots.pad] + rows[lo : lo + slots.pad]
         for hi, lo in zip(slots.rates, slots.lows)
     ]
-    return Lines(rows, rates, slots, line, block)
+    return Lines(rows, rates, slots, lines, params.shape[0])
 
 
 def halves_of(array):
@@ -312,87 +280,69 @@
     return high, (array - high.astype(F32)).astype(BF16)
 
 
-def reach_of(line, block):
-    at_t, at_u = iota((block, block), 0), iota((block, block), 1)
-    same = split_index(at_t, (block // line, line))[0] == (
-        split_index(at_u, (block // line, line))[0]
-    )
+def reach_of(lines, block):
+    at_t, line_t = split_index(iota((block, block), 0), (block // lines, lines))
+    at_u, line_u = split_index(iota((block, block), 1), (block // lines, lines))
+    same = line_t == line_u
     return same, (same & (at_t >= at_u), same & (at_t <= at_u))
 
 
 class Tables:
-    def __init__(self, slots, ranks, tile_rows, tokens, width):
-        line = ranks * tile_rows
-        block = blocks_of(line, tokens)[0]
-        self.slots, self.ranks, self.tile_rows = slots, ranks, tile_rows
-        self.tokens, self.width, self.line, self.block = tokens, width, line, block
-        self.shapes = [(tokens, tokens)] * 2
-        if line <= LONGEST_SHORT:
-            self.shapes += [(2 * block, block), (2 * LANES, 2 * width), (4 * width, LANES)]
+    def __init__(self, slots, lines, tokens, width):
+        self.slots, self.lines, self.tokens, self.width = slots, lines, tokens, width
+        self.short = tokens // lines <= LONGEST_SHORT
+        self.shapes = []
+        if self.short:
+            self.shapes = [(2 * tokens, tokens), (2 * LANES, 2 * width), (4 * width, LANES)]
 
     def fill(self, refs):
-        slots, width, block = self.slots, self.width, self.block
+        if not self.short:
+            return
+        slots, width, tokens = self.slots, self.width, self.tokens
         size = width // slots.heads
-        refs[0][...] = ordered_by_column(self.ranks, self.tile_rows, self.tokens)
-        refs[1][...] = ordered_by_rank(self.ranks, self.tile_rows, self.tokens)
-        if self.line > LONGEST_SHORT:
-            return
-        same, reach = reach_of(self.line, block)
+        same, reach = reach_of(self.lines, tokens)
         half = jnp.where(same, 0.5, 0.0)
         for way in (0, 1):
-            refs[2][way * block : (way + 1) * block, :] = (
+            refs[0][way * tokens : (way + 1) * tokens, :] = (
                 reach[way].astype(F32) - half
             ).astype(BF16)
             at = iota((LANES, width), 0)
             head = split_index(iota((LANES, width), 1), (slots.heads, size))[0]
             spread = (at == head + slots.rates[way]).astype(F32).astype(BF16)
             lanes = slice(way * width, (way + 1) * width)
-            refs[3][:LANES, lanes] = spread
-            refs[3][LANES:, lanes] = spread
+            refs[1][:LANES, lanes] = spread
+            refs[1][LANES:, lanes] = spread
             at = iota((width, LANES), 1)
             head = split_index(iota((width, LANES), 0), (slots.heads, size))[0]
             gather = (at == head + slots.rates[way]).astype(F32).astype(BF16)
-            refs[4][way * width : (way + 1) * width, :] = gather
-            refs[4][(2 + way) * width : (3 + way) * width, :] = gather
+            refs[2][way * width : (way + 1) * width, :] = gather
+            refs[2][(2 + way) * width : (3 + way) * width, :] = gather
 
 
 class ShortLines:
-    def __init__(self, params, slots, line, block, spans, width, tables):
-        self.slots, self.spans, self.block = slots, spans, block
-        self.tables = tables
-        self.reach = reach_of(line, block)[1]
-        tokens = params.shape[0]
+    def __init__(self, params, slots, lines, width, tables):
+        self.slots, self.tables = slots, tables
+        tokens = self.tokens = params.shape[0]
+        self.reach = reach_of(lines, tokens)[1]
         lane = iota((tokens, LANES), 1)
         states = slots.states
-        ways = tables[2][...]
-        sums = [nn(ways, params[span]) for span in spans]
+        sums = nn(tables[0][...], params)
         low_up = lane >= slots.lows[1]
         self.up_lane = ((lane >= slots.rates[1]) & (lane < slots.lows[0])) | low_up
-        sums = jnp.where(
-            self.up_lane,
-            jnp.concatenate([both[block:] for both in sums], axis=0),
-            jnp.concatenate([both[:block] for both in sums], axis=0),
-        )
+        sums = jnp.where(self.up_lane, sums[tokens:], sums[:tokens])
         wide = params.astype(F32)
         turned = pltpu.roll(wide, LANES - slots.reads[0], 1)
         first, second = lane < states, (lane >= states) & (lane < 2 * states)
         self.inputs = [jnp.where(mask, wide, 0.0).astype(BF16) for mask in (first, second)]
         self.reads = [jnp.where(mask, turned, 0.0).astype(BF16) for mask in (first, second)]
-        scores = [
-            nt(jnp.concatenate([read[span] for read in self.reads], axis=0), params[span])
-            for span in spans
-        ]
         self.scores = [
-            [
-                jnp.where(self.reach[way], both[way * block : (way + 1) * block], 0.0).astype(BF16)
-                for both in scores
-            ]
+            jnp.where(self.reach[way], nt(self.reads[way], params), 0.0).astype(BF16)
             for way in (0, 1)
         ]
         sums = sums + pltpu.roll(sums, LANES - (slots.lows[0] - slots.rates[0]), 1)
         rated = (lane >= slots.rates[0]) & (lane < slots.lows[0])
         sums = jnp.where(rated, sums, 0.0)
-        spread = tables[3][...]
+        spread = tables[1][...]
 
         def widen(narrow):
             wide = nn(jnp.concatenate(halves_of(narrow), axis=1), spread)
@@ -400,19 +350,10 @@
 
         self.losses, self.gains = widen(jnp.exp(sums)), widen(jnp.exp(-sums))
 
-    def per_block(self, way, product, right):
-        return jnp.concatenate(
-            [
-                product(score, right[span])
-                for score, span in zip(self.scores[way], self.spans)
-            ],
-            axis=0,
-        )
-
     def values(self, feats):
         wide = feats.astype(F32)
         self.lost = [(wide * loss).astype(BF16) for loss in self.losses]
-        self.mixed = [self.per_block(way, nn, self.lost[way]) for way in (0, 1)]
+        self.mixed = [nn(self.scores[way], self.lost[way]) for way in (0, 1)]
 
     def forward(self, feats):
         self.values(feats)
@@ -420,19 +361,14 @@
 
     def backward(self, feats, grads):
         self.values(feats)
-        slots, spans = self.slots, self.spans
+        slots, tokens = self.slots, self.tokens
         wide = grads.astype(F32)
         gained = [(wide * gain).astype(BF16) for gain in self.gains]
-        back = [self.per_block(way, tn, gained[way]) for way in (0, 1)]
+        back = [tn(self.scores[way], gained[way]) for way in (0, 1)]
         gx = self.losses[0] * back[0] + self.losses[1] * back[1]
         score_grads = [
-            [
-                jnp.where(
-                    self.reach[way], nt(gained[way][span], self.lost[way][span]), 0.0
-                ).astype(BF16)
-                for way in (0, 1)
-            ]
-            for span in spans
+            jnp.where(self.reach[way], nt(gained[way], self.lost[way]), 0.0).astype(BF16)
+            for way in (0, 1)
         ]
         change = jnp.concatenate(
             [
@@ -441,99 +377,58 @@
             ],
             axis=1,
         )
-        heads = nn(jnp.concatenate(halves_of(change), axis=1), self.tables[4][...])
-        read_grads = [
-            nn(
-                jnp.concatenate(score_grads[at], axis=1),
-                jnp.concatenate([part[span] for part in self.inputs], axis=0),
-            )
-            for at, span in enumerate(spans)
-        ]
-        input_grads = [
-            tn(
-                jnp.concatenate(score_grads[at], axis=0),
-                jnp.concatenate([part[span] for part in self.reads], axis=0),
-            )
-            for at, span in enumerate(spans)
-        ]
+        heads = nn(jnp.concatenate(halves_of(change), axis=1), self.tables[2][...])
+        read_grads = nn(score_grads[0], self.inputs[0]) + nn(score_grads[1], self.inputs[1])
+        input_grads = tn(score_grads[0], self.reads[0]) + tn(score_grads[1], self.reads[1])
         since, till = (mask.astype(F32).astype(BF16) for mask in self.reach)
-        both = jnp.concatenate(
-            [jnp.concatenate([till, till], axis=1), jnp.concatenate([since, since], axis=1)], axis=0
+        high, low = halves_of(heads)
+        both = jnp.concatenate([high, low], axis=1)
+        down, up = nn(till, both), nn(since, both)
+        rates = jnp.where(
+            self.up_lane, up[:, :LANES] + up[:, LANES:], down[:, :LANES] + down[:, LANES:]
         )
-        high, low = halves_of(heads)
-        reached = [
-            nn(both, jnp.concatenate([high[span], low[span]], axis=0)) for span in spans
-        ]
-        rates = jnp.where(
-            self.up_lane,
-            jnp.concatenate([pair[self.block :] for pair in reached], axis=0),
-            jnp.concatenate([pair[: self.block] for pair in reached], axis=0),
-        )
-        smalls = jnp.concatenate(input_grads, axis=0) + pltpu.roll(
-            jnp.concatenate(read_grads, axis=0), slots.reads[0], 1
-        )
-        lane = iota(smalls.shape, 1)
+        smalls = input_grads + pltpu.roll(read_grads, slots.reads[0], 1)
+        lane = iota((tokens, LANES), 1)
         return gx, jnp.where(lane >= slots.rates[0], rates, smalls)
 
 
 LONGEST_SHORT = 64
 
 
-def forward_kernel(slots, ranks, tile_rows, recv_ref, part_ref, *refs):
-    *tables, mine_ref, other_ref, order_ref = refs
+def forward_kernel(slots, lines, recv_ref, part_ref, *refs):
+    *tables, mine_ref, other_ref = refs
     width, model = part_ref.shape
     tokens = recv_ref.shape[0]
-    line = ranks * tile_rows
-    block, spans = blocks_of(line, tokens)
-    order = tables[0][...]
-    params = nn(order, recv_ref[:, width + model :]).astype(BF16)
-    feats = nn(order, recv_ref[:, :width]).astype(BF16)
-    cots = nn(order, recv_ref[:, width : width + model]).astype(BF16)
-    order_ref[:, width + model :] = params
-    order_ref[:, :width] = feats
-    order_ref[:, width : width + model] = cots
-    if line <= LONGEST_SHORT:
-        lines = ShortLines(params, slots, line, block, spans, width, tables)
-        down = lines.forward(feats).astype(BF16)
+    feats, cots = recv_ref[:, :width], recv_ref[:, width : width + model]
+    params = recv_ref[:, width + model :]
+    if tokens // lines <= LONGEST_SHORT:
+        down = ShortLines(params, slots, lines, width, tables).forward(feats)
     else:
-        outs = []
-        for span in spans:
-            lines = long_lines(params, span, slots, line, block)
-            outs.append(scan_block(feats[span], None, lines, slots, None, None, True, False)[0])
-        down = jnp.concatenate(outs, axis=0).astype(BF16)
-    total = part_ref[...] + tn(down, cots)
+        masks = long_lines(params, slots, lines)
+        down = scan_block(feats, None, masks, slots, None, None, True, False)[0]
+    total = part_ref[...] + tn(down.astype(BF16), cots)
     even = lax.rem(lax.axis_index("row"), 2) == 0
     half = width // 2
     mine_ref[...] = jnp.where(even, total[:half], total[half:])
     other_ref[...] = jnp.where(even, total[half:], total[:half]).astype(BF16)
 
 
-def backward_kernel(slots, ranks, tile_rows, chunk, order_ref, weight_ref, skip_ref, *refs):
+def backward_kernel(slots, ranks, lines, chunk, recv_ref, weight_ref, skip_ref, *refs):
     *tables, back_ref, small_ref = refs
     width, model = weight_ref.shape
-    tokens = order_ref.shape[0]
-    line = ranks * tile_rows
-    block, spans = blocks_of(line, tokens)
-    params = order_ref[:, width + model :]
-    feats = order_ref[:, :width]
-    grads = nt(order_ref[:, width : width + model], weight_ref[...]).astype(BF16)
-    if line <= LONGEST_SHORT:
-        lines = ShortLines(params, slots, line, block, spans, width, tables)
-        gx, small = lines.backward(feats, grads)
-        gx, small = gx.astype(BF16), small.astype(BF16)
+    tokens = recv_ref.shape[0]
+    feats = recv_ref[:, :width]
+    params = recv_ref[:, width + model :]
+    grads = nt(recv_ref[:, width : width + model], weight_ref[...]).astype(BF16)
+    if tokens // lines <= LONGEST_SHORT:
+        gx, small = ShortLines(params, slots, lines, width, tables).backward(feats, grads)
     else:
         small_ref[...] = jnp.zeros_like(small_ref)
-        gxs = []
-        for span in spans:
-            lines = long_lines(params, span, slots, line, block)
-            gxs.append(
-                scan_block(feats[span], grads[span], lines, slots, small_ref, span, False, True)[1]
-            )
-        gx = jnp.concatenate(gxs, axis=0).astype(BF16)
-        small = jnp.transpose(small_ref[...]).astype(BF16)
-    order_back = tables[1][...]
-    back_ref[:, :width] = nn(order_back, gx).astype(BF16)
-    small = nn(order_back, small)
+        masks = long_lines(params, slots, lines)
+        span = slice(0, tokens)
+        gx = scan_block(feats, grads, masks, slots, small_ref, span, False, True)[1]
+        small = jnp.transpose(small_ref[...])
+    back_ref[:, :width] = gx.astype(BF16)
     if chunk is not None:
         small = small + jnp.concatenate([skip_ref[...]] * ranks, axis=0)
     back_ref[:, width:] = small.astype(BF16)
@@ -558,29 +453,31 @@
         return self.places[self.starts[rank] : self.starts[rank + 1]]
 
 
-def merge_kernel(ranks, mine_ref, theirs_ref, back_ref, out_ref):
+def lay_out(out_ref, rank, pieces):
+    at = 0
+    for piece in pieces:
+        out_ref[rank, at : at + piece.shape[0], :] = piece
+        at += piece.shape[0]
+    if at < out_ref.shape[1]:
+        out_ref[rank, at:, :] = jnp.zeros((out_ref.shape[1] - at, LANES), BF16)
+
+
+def merge_kernel(ranks, early, mine_ref, theirs_ref, back_ref, out_ref):
     total = mine_ref[...] + theirs_ref[...].astype(F32)
-    tokens = back_ref.shape[0] // ranks
+    group = back_ref.shape[0] // ranks
     tiles = Tiles(*mine_ref.shape, ranks)
-    unit = tiles.unit
     for rank in range(ranks):
-        at = 0
-        for piece in strip(back_ref[rank * tokens : (rank + 1) * tokens, :]):
-            out_ref[rank, at : at + tokens, :] = piece
-            at += tokens
-        end = at + tiles.size
-        for row, lane in tiles.of(rank):
-            out_ref[rank, at : at + unit, :] = total[row : row + unit, lane : lane + LANES].astype(
-                BF16
-            )
-            at += unit
-        while at < end:
-            out_ref[rank, at : at + unit, :] = jnp.zeros((unit, LANES), BF16)
-            at += unit
-
-
-def sum_kernel(recv_ref, out_ref):
-    ranks, size = out_ref.shape[:2]
+        strips = strip(back_ref[rank * group : (rank + 1) * group, :])[:early]
+        blocks = [
+            total[row : row + tiles.unit, lane : lane + LANES].astype(BF16)
+            for row, lane in tiles.of(rank)
+        ]
+        lay_out(out_ref, rank, strips + blocks)
+
+
+def sum_kernel(early, size, recv_ref, back_ref, out_ref):
+    ranks = out_ref.shape[0]
+    group = back_ref.shape[0] // ranks
     own = slice(recv_ref.shape[1] - size, recv_ref.shape[1])
     for half in (0, 1):
         total = recv_ref[half, own, :].astype(F32)
@@ -588,7 +485,13 @@
             total = total + recv_ref[rank, own, :].astype(F32)
         total = total.astype(BF16)
         for rank in range(half, ranks, 2):
-            out_ref[rank] = total
+            strips = strip(back_ref[rank * group : (rank + 1) * group, :])[early:]
+            lay_out(out_ref, rank, strips + [total])
+
+
+def half_kernel(recv_ref, out_ref):
+    size = out_ref.shape[1]
+    out_ref[...] = recv_ref[:, recv_ref.shape[1] - size :, :]
 
 
 def weight_kernel(mine_ref, theirs_ref, out_ref):
@@ -609,7 +512,7 @@
 
 
 def finish_kernel(
-    slots, ranks, chunk, recv_ref, gx_ref, small_ref,
+    slots, ranks, chunk, early, early_ref, late_ref, gx_ref, small_ref,
     feat_out, rate_out, input_out, read_out, *skip_out,
 ):
     tile_rows, columns, width = feat_out.shape
@@ -618,7 +521,8 @@
     lanes = width // LANES
 
     def part_of(part):
-        return recv_ref[:, part * group : (part + 1) * group, :].astype(F32)
+        ref, part = (early_ref, part) if part < early else (late_ref, part - early)
+        return ref[:, part * group : (part + 1) * group, :].astype(F32)
 
     def row_of(array, row):
         return jnp.concatenate(
@@ -695,7 +599,8 @@
     )
     received = exchange(packed)
     skip_shape = (1, width) if chunk is None else (chunk, LANES)
-    tables = Tables(slots, ranks, tile_rows, tokens, width)
+    lines = columns // ranks
+    tables = Tables(slots, lines, tokens, width)
     gx_rows, small_rows, partial, skip_part, *table = call(
         functools.partial(rows_kernel, slots, chunk, tables), "rows",
         (
@@ -714,38 +619,43 @@
     )
     half = width // 2
     partners = [(rank, rank ^ 1) for rank in range(ranks)]
-    mine, other, ordered = call(
-        functools.partial(forward_kernel, slots, ranks, tile_rows), "forward",
+    mine, other = call(
+        functools.partial(forward_kernel, slots, lines), "forward",
         (
             shape((half, model), F32),
             shape((half, model), BF16),
-            shape(received.shape, BF16),
         ),
         (received, partial, *table),
         flops=2 * tokens * width * (2 * model + columns), moved=8 * tokens * width,
     )
     theirs = lax.ppermute(other, "row", partners)
     back = call(
-        functools.partial(backward_kernel, slots, ranks, tile_rows, chunk), "backward",
-        shape((tokens, width + LANES), BF16), (ordered, out_weight, skip_part, *table),
+        functools.partial(backward_kernel, slots, ranks, lines, chunk), "backward",
+        shape((tokens, width + LANES), BF16), (received, out_weight, skip_part, *table),
         [pltpu.VMEM((LANES, tokens), F32)],
         flops=2 * tokens * width * (2 * model + 3 * columns), moved=8 * tokens * width,
     )
     group = tokens // ranks
     size = Tiles(half, model, ranks).size
+    strips = width // LANES + 1
+    early = strips // 2
     merged = call(
-        functools.partial(merge_kernel, ranks), "merge",
-        shape((ranks, (width // LANES + 1) * group + size, LANES), BF16), (mine, theirs, back),
+        functools.partial(merge_kernel, ranks, early), "merge",
+        shape((ranks, early * group + size, LANES), BF16), (mine, theirs, back),
         flops=width * model, moved=2 * width * model,
     )
     returned = exchange(merged)
     summed = call(
-        sum_kernel, "sum", shape((ranks, size, LANES), BF16), (returned,),
+        functools.partial(sum_kernel, early, size), "sum",
+        shape((ranks, (strips - early) * group + size, LANES), BF16), (returned, back),
         flops=width * model, moved=2 * width * model,
     )
-    held = exchange(summed)
+    last = exchange(summed)
+    held = call(
+        half_kernel, "half", shape((ranks, size, LANES), BF16), (last,),
+        flops=width * model, moved=2 * width * model,
+    )
     swapped = lax.ppermute(held, "row", partners)
-    returned, held = lax.optimization_barrier((returned, held))
     outs = [
         shape(features.shape, BF16),
         shape(decay_rate.shape, F32),
@@ -755,8 +665,8 @@
     if chunk is not None:
         outs.append(shape((width,), F32))
     done = call(
-        functools.partial(finish_kernel, slots, ranks, chunk), "finish",
-        tuple(outs), (returned, gx_rows, small_rows),
+        functools.partial(finish_kernel, slots, ranks, chunk, early), "finish",
+        tuple(outs), (returned, last, gx_rows, small_rows),
         flops=2 * tokens * tokens * width, moved=8 * tokens * width,
     )
     grad_weight = call(

time: 57.8 us -> 57 us (0.986)
  blocking collectives: 28.4 us -> 27.8 us
    all_to_all x2, blocking collectives: 28.4 us -> 27.8 us  [exchange(): return lax.all_to_all(array, 'row', split_axis=0, concat_axis=0, tiled=True)]
    pallas_call x8 -> x9, Pallas kernels: 10.2 us -> 10.1 us  [call(): pl.pallas_call(kernel, name=name, out_shape=out_shape, in_specs=[pl.Block...]
where the time goes in v4:
time: 57 us; the launch traced here: 56.7 us
  blocking collectives  27.8 us (49%)
  Pallas kernels  10.1 us (18%)
  waiting for transfers between devices  10.1 us (18%)
  starting transfers between devices  7.91 us (14%)
  between operations  0.78 us (1%)
    all_to_all x2, blocking collectives, exchange(): return lax.all_to_all(array, 'row', split_axis=0, concat_axis=0, tiled=True)  27.8 us
    pallas_call x9, Pallas kernels, call(): pl.pallas_call(kernel, name=name, out_shape=out_shape, in_specs=[pl.Block...  10.1 us
    all_to_all x1, waiting for transfers between devices, exchange(): return lax.all_to_all(array, 'row', split_axis=0, concat_axis=0, tiled=True)  9.85 us
    all_to_all x1, starting transfers between devices, exchange(): return lax.all_to_all(array, 'row', split_axis=0, concat_axis=0, tiled=True)  7.56 us
  transfers between devices with their start and end apart: 3, of which 2 were waited for; matrix products, arithmetic and copies ran while one was open for 0% of the time, Pallas kernels for 11%

profile of v4, /device:TPU:0, one launch (start us, length us, event | category | flops | bytes accessed | tf_op | source)
XLA Modules:
  0.0 56.7 jit_solution(18419383039480733411)
XLA Ops:
  0.6 2.0 %pack.1 = bf16[256,896]{1,0:T(8,128)(2,1)} custom-call(bf16[2,128,384]{2,1,0:T(8,128)(2,1)} %feat_ref.3, bf16[2,128,384]{2,1,0:T(8,128)(2,1)} %cot_ref.3, f32[4,6,2,128]{3,2,1,0:T(2,128)} %rate_ref.3, f32[4,16,2,128]{3,2,1,0:T(2,128)} %input_ref.3, f32[4,16,2,128]{3,2,1,0:T(2,128)} %read_ref.3), custom_call_target="tpu_custom_call" | custom-call | flops 100663296 | bytes 786432 | tf_op jit(solution)/shard_map/pack/pallas_call | solution.py:566
  2.6 0.0 copy-start.6
  2.6 0.0 copy-start
  2.6 0.0 copy-start.1
  2.6 0.0 copy-start.2
  2.6 0.0 copy-start.3
  2.7 0.0 copy-start.4
  2.7 0.0 copy-start.5
  2.7 7.6 %all-to-all-start = ((bf16[16,16,896]{2,1,0:T(8,128)(2,1)}), bf16[16,16,896]{2,1,0:T(8,128)(2,1)S(1)}, u32[]{:S(2)}, u32[]{:S(2)}) async-start(bf16[16,16,896]{2,1,0:T(8,128)(2,1)} %bitcast.4), calls=%async_computation | async-start | bytes 917504 | tf_op jit(solution)/shard_map/all_to_all | solution.py:591
  10.2 0.0 copy-done.6
  10.3 0.0 copy-done
  10.3 0.0 copy-done.1
  10.3 0.0 copy-done.2
  10.3 0.0 copy-done.3
  10.3 0.0 copy-done.4
  10.3 0.0 copy-done.5
  10.3 3.3 %rows.1 = (f32[256,384]{1,0:T(8,128)S(1)}, f32[128,256]{1,0:T(8,128)S(1)}, f32[384,384]{1,0:T(8,128)S(1)}, f32[16,128]{1,0:T(8,128)S(1)}, bf16[512,256]{1,0:T(8,...) custom-call(bf16[2,128,384]{2,1,0:T(8,128)(2,1)S(1)} %copy-done.1, ...), custom_call_target="tpu_custom_call" | custom-call | flops 226492416 | bytes 786432 | tf_op jit(solution)/shard_map/rows/pallas_call | solution.py:566
  13.6 9.8 %all-to-all-done = bf16[16,16,896]{2,1,0:T(8,128)(2,1)S(1)} async-done(((bf16[16,16,896]{2,1,0:T(8,128)(2,1)}), bf16[16,16,896]{2,1,0:T(8,128)(2,1)S(1)}, u32[]{:S(2)}, u32[]{:S(2)}) %all-to-all-start) | async-done | bytes 458784 | tf_op jit(solution)/shard_map/all_to_all | solution.py:591
  23.5 1.1 %forward.1 = (f32[192,384]{1,0:T(8,128)S(1)}, bf16[192,384]{1,0:T(8,128)(2,1)S(1)}) custom-call(bf16[256,896]{1,0:T(8,128)(2,1)S(1)} %bitcast.2, f32[384,384]{1,0:T(8,128)S(1)} %get-tuple-element.20.part_ref, bf16[512,256]{1,0:T(8,128)(2,1)S(1)} %get-tuple-element.21.refs_0_, bf16[256,768]{1,0:T(8,128)(2,1)S(1)} %get-tuple-element.22.refs_1_, ...), custom_call_target="tpu_custom_call" | custom-call | flops 176160768 | bytes 786432 | tf_op jit(solution)/shard_map/forward/pallas_call | solution.py:566
  24.5 0.2 collective-permute-start
  24.7 1.7 %backward.1.back_ref = bf16[256,512]{1,0:T(8,128)(2,1)S(1)} custom-call(bf16[256,896]{1,0:T(8,128)(2,1)S(1)} %bitcast.3, bf16[384,384]{1,0:T(8,128)(2,1)S(1)} %copy-done, f32[16,128]{1,0:T(8,128)S(1)} %get-tuple-element.26.skip_ref, bf16[512,256]{1,0:T(8,128)(2,1)S(1)} %get-tuple-element.21.refs_0_, bf16[256,768]{1,0:T(8,128)(2,1)S(1)} %get-tuple-element.22.refs_1_, ...), custom_call_target="tpu_custom_call" | custom-call | flops 226492416 | bytes 786432 | tf_op jit(solution)/shard_map/backward/pallas_call | solution.py:566
  26.5 0.0 collective-permute-done.theirs_ref
  26.5 14.4 %all_to_all.21.recv_ref.early_ref = bf16[16,72,128]{2,1,0:T(8,128)(2,1)S(1)} all-to-all(bf16[16,72,128]{2,1,0:T(8,128)(2,1)S(1)} %merge.1), channel_id=1, replica_groups=mesh['grp'=2,'row'=16] {'row'}, dimensions={0} | all-to-all | bytes 589824 | tf_op jit(solution)/shard_map/all_to_all | solution.py:591
  41.0 13.3 %all_to_all.22.late_ref.recv_ref = bf16[16,72,128]{2,1,0:T(8,128)(2,1)S(1)} all-to-all(bf16[16,72,128]{2,1,0:T(8,128)(2,1)S(1)} %sum.1), channel_id=1, replica_groups=mesh['grp'=2,'row'=16] {'row'}, dimensions={0} | all-to-all | bytes 589824 | tf_op jit(solution)/shard_map/all_to_all | solution.py:591
  54.3 0.2 collective-permute-start.1
  54.5 1.0 %finish.1 = (bf16[2,128,384]{2,1,0:T(8,128)(2,1)}, f32[4,6,2,128]{3,2,1,0:T(2,128)}, f32[4,16,2,128]{3,2,1,0:T(2,128)}, f32[4,16,2,128]{3,2,1,0:T(2,128)}, f32[384]{0:T(512)}) custom-call(bf16[16,72,128]{2,1,0:T(8,128)(2,1)S(1)} %all_to_all.21.recv_ref.early_ref, bf16[16,72,128]{2,1,0:T(8,128)(2,1)S(1)} %all_to_all.22.late_ref.recv_ref, ...), custom_call_target="tpu_custom_call" | custom-call | flops 50331648 | bytes 786432 | tf_op jit(solution)/shard_map/finish/pallas_call | solution.py:566
  55.5 0.3 collective-permute-done.1.theirs_ref
  55.8 0.9 %weight.1 = f32[384,384]{1,0:T(8,128)} custom-call(bf16[16,40,128]{2,1,0:T(8,128)(2,1)S(1)} %half.1.mine_ref, bf16[16,40,128]{2,1,0:T(8,128)(2,1)S(1)} %collective-permute-done.1.theirs_ref), custom_call_target="tpu_custom_call" | custom-call | flops 147456 | bytes 884736 | tf_op jit(solution)/shard_map/weight/pallas_call | solution.py:566
  (4 shorter events, 0.1 us)
Async XLA Ops:
  2.6 7.6 %copy-start.6 = (f32[384]{0:T(512)S(1)}, f32[384]{0:T(512)}, u32[]{:S(2)}) copy-start(f32[384]{0:T(512)} %param.11) | copy-start | bytes 4612
  2.6 7.6 %copy-start = (bf16[384,384]{1,0:T(8,128)(2,1)S(1)}, bf16[384,384]{1,0:T(8,128)(2,1)}, u32[]{:S(2)}) copy-start(bf16[384,384]{1,0:T(8,128)(2,1)} %weight_ref.3) | copy-start | bytes 884740
  2.6 7.6 %copy-start.1 = (bf16[2,128,384]{2,1,0:T(8,128)(2,1)S(1)}, bf16[2,128,384]{2,1,0:T(8,128)(2,1)}, u32[]{:S(2)}) copy-start(bf16[2,128,384]{2,1,0:T(8,128)(2,1)} %feat_ref.3) | copy-start | bytes 589828
  2.6 7.7 %copy-start.2 = (bf16[2,128,384]{2,1,0:T(8,128)(2,1)S(1)}, bf16[2,128,384]{2,1,0:T(8,128)(2,1)}, u32[]{:S(2)}) copy-start(bf16[2,128,384]{2,1,0:T(8,128)(2,1)} %cot_ref.3) | copy-start | bytes 589828
  2.6 7.7 %copy-start.3 = (f32[4,16,2,128]{3,2,1,0:T(2,128)S(1)}, f32[4,16,2,128]{3,2,1,0:T(2,128)}, u32[]{:S(2)}) copy-start(f32[4,16,2,128]{3,2,1,0:T(2,128)} %input_ref.3) | copy-start | bytes 196612
  2.7 7.7 %copy-start.4 = (f32[4,16,2,128]{3,2,1,0:T(2,128)S(1)}, f32[4,16,2,128]{3,2,1,0:T(2,128)}, u32[]{:S(2)}) copy-start(f32[4,16,2,128]{3,2,1,0:T(2,128)} %read_ref.3) | copy-start | bytes 196612
  2.7 7.7 %copy-start.5 = (f32[4,6,2,128]{3,2,1,0:T(2,128)S(1)}, f32[4,6,2,128]{3,2,1,0:T(2,128)}, u32[]{:S(2)}) copy-start(f32[4,6,2,128]{3,2,1,0:T(2,128)} %rate_ref.3) | copy-start | bytes 73732
  2.7 20.8 %all-to-all-start = ((bf16[16,16,896]{2,1,0:T(8,128)(2,1)}), bf16[16,16,896]{2,1,0:T(8,128)(2,1)S(1)}, u32[]{:S(2)}, u32[]{:S(2)}) async-start(bf16[16,16,896]{2,1,0:T(8,128)(2,1)} %bitcast.4), calls=%async_computation | async-start | bytes 917504 | tf_op jit(solution)/shard_map/all_to_all | solution.py:591
  24.5 1.9 %collective-permute-start = (bf16[192,384]{1,0:T(8,128)(2,1)S(1)}, bf16[192,384]{1,0:T(8,128)(2,1)S(1)}, u32[]{:S(2)}, u32[]{:S(2)}) collective-permute-start(bf16[192,384]{1,0:T(8,128)(2,1)S(1)} %get-tuple-element.25), channel_id=1, source_target_pairs={{0,1},{1,0},{2,3},{3,2},{4,5},{5,4},{6,7},{7,6},{8,9},{9,8},{10,11... | collective-permute-start | bytes 442376 | tf_op jit(solution)/shard_map/ppermute | solution.py:631
  54.3 1.5 %collective-permute-start.1 = (bf16[16,40,128]{2,1,0:T(8,128)(2,1)S(1)}, bf16[16,40,128]{2,1,0:T(8,128)(2,1)S(1)}, u32[]{:S(2)}, u32[]{:S(2)}) collective-permute-start(bf16[16,40,128]{2,1,0:T(8,128)(2,1)S(1)} %half.1.mine_ref), channel_id=1, source_target_pairs={{0,1},{1,0},{2,3},{3,2},{4,5},{5,4},{6,7},{7,6},{8,9},{9,8},{10,11... | collective-permute-start | bytes 491528 | tf_op jit(solution)/shard_map/ppermute | solution.py:658

commit v5 on v4

--- a/solution.py
+++ b/solution.py
@@ -292,7 +292,13 @@
         self.slots, self.lines, self.tokens, self.width = slots, lines, tokens, width
         self.short = tokens // lines <= LONGEST_SHORT
         self.shapes = []
+        self.kept = []
         if self.short:
+            values = ((2, tokens, width), F32)
+            self.kept = [
+                ((2, tokens, 2 * LANES), BF16), ((2, tokens, width), BF16), values,
+                ((2, tokens, tokens), BF16),
+            ]
             self.shapes = [(2 * tokens, tokens), (2 * LANES, 2 * width), (4 * width, LANES)]
 
     def fill(self, refs):
@@ -315,94 +321,96 @@
             at = iota((width, LANES), 1)
             head = split_index(iota((width, LANES), 0), (slots.heads, size))[0]
             gather = (at == head + slots.rates[way]).astype(F32).astype(BF16)
-            refs[2][way * width : (way + 1) * width, :] = gather
-            refs[2][(2 + way) * width : (3 + way) * width, :] = gather
+            refs[2][2 * way * width : (2 * way + 1) * width, :] = gather
+            refs[2][(2 * way + 1) * width : (2 * way + 2) * width, :] = gather
 
 
 class ShortLines:
-    def __init__(self, params, slots, lines, width, tables):
-        self.slots, self.tables = slots, tables
+    def __init__(self, params, slots, lines, tables):
+        self.slots, self.tables, self.params = slots, tables, params
         tokens = self.tokens = params.shape[0]
         self.reach = reach_of(lines, tokens)[1]
-        lane = iota((tokens, LANES), 1)
+        self.lane = lane = iota((tokens, LANES), 1)
+        self.up_lane = ((lane >= slots.rates[1]) & (lane < slots.lows[0])) | (
+            lane >= slots.lows[1]
+        )
         states = slots.states
-        sums = nn(tables[0][...], params)
-        low_up = lane >= slots.lows[1]
-        self.up_lane = ((lane >= slots.rates[1]) & (lane < slots.lows[0])) | low_up
-        sums = jnp.where(self.up_lane, sums[tokens:], sums[:tokens])
         wide = params.astype(F32)
         turned = pltpu.roll(wide, LANES - slots.reads[0], 1)
         first, second = lane < states, (lane >= states) & (lane < 2 * states)
         self.inputs = [jnp.where(mask, wide, 0.0).astype(BF16) for mask in (first, second)]
         self.reads = [jnp.where(mask, turned, 0.0).astype(BF16) for mask in (first, second)]
-        self.scores = [
-            jnp.where(self.reach[way], nt(self.reads[way], params), 0.0).astype(BF16)
-            for way in (0, 1)
-        ]
+
+    def factors(self, width, narrows):
+        spread = self.tables[1][...]
+        pairs = [nn(narrows[at], spread) for at in (0, 1)]
+        return [(pair[:, :width], pair[:, width:]) for pair in pairs]
+
+    def forward(self, feats, kept):
+        slots, tokens, lane = self.slots, self.tokens, self.lane
+        width = feats.shape[1]
+        narrows, lost, mixed, scores = kept
+        sums = nn(self.tables[0][...], self.params)
+        sums = jnp.where(self.up_lane, sums[tokens:], sums[:tokens])
         sums = sums + pltpu.roll(sums, LANES - (slots.lows[0] - slots.rates[0]), 1)
         rated = (lane >= slots.rates[0]) & (lane < slots.lows[0])
         sums = jnp.where(rated, sums, 0.0)
-        spread = tables[1][...]
-
-        def widen(narrow):
-            wide = nn(jnp.concatenate(halves_of(narrow), axis=1), spread)
-            return wide[:, :width], wide[:, width:]
-
-        self.losses, self.gains = widen(jnp.exp(sums)), widen(jnp.exp(-sums))
-
-    def values(self, feats):
+        for at, narrow in enumerate((jnp.exp(sums), jnp.exp(-sums))):
+            narrows[at] = jnp.concatenate(halves_of(narrow), axis=1)
+        losses, gains = self.factors(width, narrows)
         wide = feats.astype(F32)
-        self.lost = [(wide * loss).astype(BF16) for loss in self.losses]
-        self.mixed = [nn(self.scores[way], self.lost[way]) for way in (0, 1)]
-
-    def forward(self, feats):
-        self.values(feats)
-        return self.gains[0] * self.mixed[0] + self.gains[1] * self.mixed[1]
-
-    def backward(self, feats, grads):
-        self.values(feats)
-        slots, tokens = self.slots, self.tokens
+        out = None
+        for way in (0, 1):
+            score = jnp.where(self.reach[way], nt(self.reads[way], self.params), 0.0).astype(BF16)
+            scores[way] = score
+            held = (wide * losses[way]).astype(BF16)
+            lost[way] = held
+            mix = nn(score, held)
+            mixed[way] = mix
+            part = gains[way] * mix
+            out = part if out is None else out + part
+        return out
+
+    def backward(self, grads, kept):
+        slots = self.slots
+        width = grads.shape[1]
+        narrows, lost, mixed, scores = kept
+        losses, gains = self.factors(width, narrows)
         wide = grads.astype(F32)
-        gained = [(wide * gain).astype(BF16) for gain in self.gains]
-        back = [tn(self.scores[way], gained[way]) for way in (0, 1)]
-        gx = self.losses[0] * back[0] + self.losses[1] * back[1]
-        score_grads = [
-            jnp.where(self.reach[way], nt(gained[way], self.lost[way]), 0.0).astype(BF16)
-            for way in (0, 1)
-        ]
-        change = jnp.concatenate(
-            [
-                self.lost[way].astype(F32) * back[way] - gained[way].astype(F32) * self.mixed[way]
-                for way in (0, 1)
-            ],
-            axis=1,
-        )
-        heads = nn(jnp.concatenate(halves_of(change), axis=1), self.tables[2][...])
-        read_grads = nn(score_grads[0], self.inputs[0]) + nn(score_grads[1], self.inputs[1])
-        input_grads = tn(score_grads[0], self.reads[0]) + tn(score_grads[1], self.reads[1])
+        gx = heads = read_grads = input_grads = 0.0
+        for way in (0, 1):
+            gained = (wide * gains[way]).astype(BF16)
+            back = tn(scores[way], gained)
+            gx = gx + losses[way] * back
+            held = lost[way]
+            score_grad = jnp.where(self.reach[way], nt(gained, held), 0.0).astype(BF16)
+            change = held.astype(F32) * back - gained.astype(F32) * mixed[way]
+            places = self.tables[2][2 * way * width : 2 * (way + 1) * width, :]
+            heads = heads + nn(jnp.concatenate(halves_of(change), axis=1), places)
+            read_grads = read_grads + nn(score_grad, self.inputs[way])
+            input_grads = input_grads + tn(score_grad, self.reads[way])
         since, till = (mask.astype(F32).astype(BF16) for mask in self.reach)
-        high, low = halves_of(heads)
-        both = jnp.concatenate([high, low], axis=1)
+        both = jnp.concatenate(halves_of(heads), axis=1)
         down, up = nn(till, both), nn(since, both)
         rates = jnp.where(
             self.up_lane, up[:, :LANES] + up[:, LANES:], down[:, :LANES] + down[:, LANES:]
         )
         smalls = input_grads + pltpu.roll(read_grads, slots.reads[0], 1)
-        lane = iota((tokens, LANES), 1)
-        return gx, jnp.where(lane >= slots.rates[0], rates, smalls)
-
-
-LONGEST_SHORT = 64
-
-
-def forward_kernel(slots, lines, recv_ref, part_ref, *refs):
-    *tables, mine_ref, other_ref = refs
+        return gx, jnp.where(self.lane >= slots.rates[0], rates, smalls)
+
+
+LONGEST_SHORT = 32
+
+
+def forward_kernel(slots, lines, sizes, recv_ref, part_ref, *refs):
+    tables, refs = refs[: len(sizes.shapes)], refs[len(sizes.shapes) :]
+    mine_ref, other_ref, *kept = refs
     width, model = part_ref.shape
     tokens = recv_ref.shape[0]
     feats, cots = recv_ref[:, :width], recv_ref[:, width : width + model]
     params = recv_ref[:, width + model :]
-    if tokens // lines <= LONGEST_SHORT:
-        down = ShortLines(params, slots, lines, width, tables).forward(feats)
+    if sizes.short:
+        down = ShortLines(params, slots, lines, tables).forward(feats, kept)
     else:
         masks = long_lines(params, slots, lines)
         down = scan_block(feats, None, masks, slots, None, None, True, False)[0]
@@ -413,15 +421,16 @@
     other_ref[...] = jnp.where(even, total[half:], total[:half]).astype(BF16)
 
 
-def backward_kernel(slots, ranks, lines, chunk, recv_ref, weight_ref, skip_ref, *refs):
-    *tables, back_ref, small_ref = refs
+def backward_kernel(slots, ranks, lines, chunk, sizes, recv_ref, weight_ref, skip_ref, *refs):
+    tables, refs = refs[: len(sizes.shapes)], refs[len(sizes.shapes) :]
+    *kept, back_ref, small_ref = refs
     width, model = weight_ref.shape
     tokens = recv_ref.shape[0]
     feats = recv_ref[:, :width]
     params = recv_ref[:, width + model :]
     grads = nt(recv_ref[:, width : width + model], weight_ref[...]).astype(BF16)
-    if tokens // lines <= LONGEST_SHORT:
-        gx, small = ShortLines(params, slots, lines, width, tables).backward(feats, grads)
+    if sizes.short:
+        gx, small = ShortLines(params, slots, lines, tables).backward(grads, kept)
     else:
         small_ref[...] = jnp.zeros_like(small_ref)
         masks = long_lines(params, slots, lines)
@@ -439,18 +448,27 @@
 
 
 class Tiles:
-    def __init__(self, rows, model, ranks):
-        self.unit = 8
-        steps = rows // self.unit
-        self.places = [
-            (at * self.unit, lane) for lane in range(0, model, LANES) for at in range(steps)
-        ]
+    def __init__(self, rows, model, ranks, group):
+        self.unit = unit = 8
+        steps = rows // unit
+        self.places = [(at * unit, lane) for lane in range(0, model, LANES) for at in range(steps)]
         count = len(self.places)
+        per = 2 * count // ranks
+        self.split = 2 * count % ranks == 0 and per % 2 == 1 and ranks % 2 == 0 and group > 4
+        self.per = per
+        self.full = per // 2 if self.split else -(-count // ranks)
         self.starts = [count * rank // ranks for rank in range(ranks + 1)]
-        self.size = self.unit * -(-count // ranks)
+        self.moved = unit // 2 if self.split else 0
+        self.size = unit * (self.full + self.split)
 
     def of(self, rank):
-        return self.places[self.starts[rank] : self.starts[rank + 1]]
+        if not self.split:
+            return self.places[self.starts[rank] : self.starts[rank + 1]]
+        first = self.per * (rank // 2) + (rank % 2) * (self.full + 1)
+        return self.places[first : first + self.full]
+
+    def shared(self, rank):
+        return self.places[self.per * (rank // 2) + self.full]
 
 
 def lay_out(out_ref, rank, pieces):
@@ -458,63 +476,98 @@
     for piece in pieces:
         out_ref[rank, at : at + piece.shape[0], :] = piece
         at += piece.shape[0]
-    if at < out_ref.shape[1]:
-        out_ref[rank, at:, :] = jnp.zeros((out_ref.shape[1] - at, LANES), BF16)
 
 
 def merge_kernel(ranks, early, mine_ref, theirs_ref, back_ref, out_ref):
     total = mine_ref[...] + theirs_ref[...].astype(F32)
     group = back_ref.shape[0] // ranks
-    tiles = Tiles(*mine_ref.shape, ranks)
+    tiles = Tiles(*mine_ref.shape, ranks, group)
+    unit = tiles.unit
     for rank in range(ranks):
-        strips = strip(back_ref[rank * group : (rank + 1) * group, :])[:early]
+        pieces = strip(back_ref[rank * group : (rank + 1) * group, :])
         blocks = [
-            total[row : row + tiles.unit, lane : lane + LANES].astype(BF16)
+            total[row : row + unit, lane : lane + LANES].astype(BF16)
             for row, lane in tiles.of(rank)
         ]
-        lay_out(out_ref, rank, strips + blocks)
-
-
-def sum_kernel(early, size, recv_ref, back_ref, out_ref):
+        blocks += [jnp.zeros((unit, LANES), BF16)] * (tiles.full - len(blocks))
+        if tiles.split:
+            row, lane = tiles.shared(rank)
+            half = unit // 2
+            row += (rank % 2) * half
+            moved = pieces[-1].astype(F32)[group - tiles.moved :]
+            blocks.append(
+                jnp.concatenate([total[row : row + half, lane : lane + LANES], moved], axis=0)
+                .astype(BF16)
+            )
+        lay_out(out_ref, rank, pieces[:early] + blocks)
+
+
+def sum_kernel(early, recv_ref, back_ref, out_ref, tiles):
     ranks = out_ref.shape[0]
     group = back_ref.shape[0] // ranks
-    own = slice(recv_ref.shape[1] - size, recv_ref.shape[1])
+    unit = tiles.unit
+    own = slice(recv_ref.shape[1] - tiles.size, recv_ref.shape[1])
+    whole = tiles.full * unit
     for half in (0, 1):
         total = recv_ref[half, own, :].astype(F32)
         for rank in range(half + 2, ranks, 2):
             total = total + recv_ref[rank, own, :].astype(F32)
-        total = total.astype(BF16)
         for rank in range(half, ranks, 2):
-            strips = strip(back_ref[rank * group : (rank + 1) * group, :])[early:]
-            lay_out(out_ref, rank, strips + [total])
-
-
-def half_kernel(recv_ref, out_ref):
-    size = out_ref.shape[1]
-    out_ref[...] = recv_ref[:, recv_ref.shape[1] - size :, :]
-
-
-def weight_kernel(mine_ref, theirs_ref, out_ref):
-    ranks = mine_ref.shape[0]
-    width, model = out_ref.shape
-    tiles = Tiles(width // 2, model, ranks)
+            pieces = strip(back_ref[rank * group : (rank + 1) * group, :])
+            small = pieces[-1]
+            if tiles.split:
+                small = jnp.concatenate(
+                    [total[whole : whole + unit // 2], small.astype(F32)[: group - tiles.moved]],
+                    axis=0,
+                ).astype(BF16)
+            lay_out(out_ref, rank, pieces[early:-1] + [total[:whole].astype(BF16), small])
+
+
+def half_kernel(start, recv_ref, out_ref):
+    out_ref[...] = recv_ref[:, start : start + out_ref.shape[1], :]
+
+
+def widen_half(halves_ref, store, tiles):
+    ranks = halves_ref.shape[0]
     unit = tiles.unit
-    even = lax.rem(lax.axis_index("row"), 2) == 0
-    mine, theirs = mine_ref[...].astype(F32), theirs_ref[...].astype(F32)
-    pair = (jnp.where(even, mine, theirs), jnp.where(even, theirs, mine))
-    for half in (0, 1):
-        for rank in range(ranks):
-            for step, (row, lane) in enumerate(tiles.of(rank)):
-                row += half * (width // 2)
-                out_ref[row : row + unit, lane : lane + LANES] = pair[half][
-                    rank, step * unit : (step + 1) * unit, :
-                ]
+    for rank in range(ranks):
+        for step, (row, lane) in enumerate(tiles.of(rank)):
+            store(row, lane, halves_ref[rank, step * unit : (step + 1) * unit, :].astype(F32))
+    if tiles.split:
+        at = tiles.full * unit
+        for rank in range(0, ranks, 2):
+            pair = [
+                halves_ref[rank + side, at : at + unit, :].astype(F32)[: unit // 2]
+                for side in (0, 1)
+            ]
+            store(*tiles.shared(rank), jnp.concatenate(pair, axis=0))
+
+
+def weight_kernel(tiles, theirs_ref, weight_in, weight_out, wide_ref, done):
+    rows, model = wide_ref.shape
+
+    def store(row, lane, block):
+        wide_ref[row : row + block.shape[0], lane : lane + LANES] = block
+
+    widen_half(theirs_ref, store, tiles)
+    half = lax.rem(lax.axis_index("row") + 1, 2)
+    start = pl.multiple_of(half * rows, 8)
+    copy = pltpu.make_async_copy(wide_ref, weight_out.at[pl.ds(start, rows), :], done)
+    copy.start()
+    copy.wait()
 
 
 def finish_kernel(
-    slots, ranks, chunk, early, early_ref, late_ref, gx_ref, small_ref,
-    feat_out, rate_out, input_out, read_out, *skip_out,
+    slots, ranks, chunk, early, tiles, early_ref, late_ref, gx_ref, small_ref, held_ref,
+    weight_out, feat_out, rate_out, input_out, read_out, *skip_out,
 ):
+    rows = weight_out.shape[0] // 2
+    start = pl.multiple_of(lax.rem(lax.axis_index("row"), 2) * rows, 8)
+
+    def store(row, lane, block):
+        weight_out[pl.ds(start + row, block.shape[0]), lane : lane + LANES] = block
+
+    widen_half(held_ref, store, tiles)
     tile_rows, columns, width = feat_out.shape
     narrow = columns // ranks
     group = tile_rows * narrow
@@ -535,7 +588,10 @@
         for row in range(tile_rows):
             span = slice(row * columns, (row + 1) * columns)
             feat_out[row, :, lane] = (gx_ref[span, lane] + row_of(back, row)).astype(BF16)
-    back = part_of(lanes)
+    back = late_ref[:, late_ref.shape[1] - group :, :].astype(F32)
+    if tiles.split:
+        tail = early_ref[:, early_ref.shape[1] - tiles.unit :, :].astype(F32)
+        back = jnp.concatenate([back[:, tiles.moved :], tail[:, tiles.unit - tiles.moved :]], axis=1)
     for row in range(tile_rows):
         span = slice(row * columns, (row + 1) * columns)
         held = jnp.transpose(row_of(back, row))
@@ -562,14 +618,23 @@
         skip_out[0][...] = jnp.sum(jnp.where(owned, spread, 0.0), axis=0)
 
 
-def call(kernel, name, out_shape, operands, scratch=(), flops=0, moved=0, grant=VMEM_GRANT):
+def call(
+    kernel, name, out_shape, operands, scratch=(), flops=0, moved=0, grant=VMEM_GRANT,
+    whole=(), aliases=None,
+):
+    def spec(side, at):
+        return pl.BlockSpec(memory_space=pl.ANY if (side, at) in whole else pltpu.VMEM)
+
+    many = isinstance(out_shape, tuple)
+    outs = tuple(spec("out", at) for at in range(len(out_shape) if many else 1))
     return pl.pallas_call(
         kernel,
         name=name,
         out_shape=out_shape,
-        in_specs=[pl.BlockSpec(memory_space=pltpu.VMEM)] * len(operands),
-        out_specs=jax.tree.map(lambda leaf: pl.BlockSpec(memory_space=pltpu.VMEM), out_shape),
+        in_specs=[spec("in", at) for at in range(len(operands))],
+        out_specs=outs if many else outs[0],
         scratch_shapes=list(scratch),
+        input_output_aliases=aliases or {},
         compiler_params=pltpu.CompilerParams(vmem_limit_bytes=grant),
         cost_estimate=pl.CostEstimate(flops=flops, bytes_accessed=moved, transcendentals=0),
     )(*operands)
@@ -619,44 +684,49 @@
     )
     half = width // 2
     partners = [(rank, rank ^ 1) for rank in range(ranks)]
-    mine, other = call(
-        functools.partial(forward_kernel, slots, lines), "forward",
+    mine, other, *kept = call(
+        functools.partial(forward_kernel, slots, lines, tables), "forward",
         (
             shape((half, model), F32),
             shape((half, model), BF16),
+            *(shape(*leaf) for leaf in tables.kept),
         ),
         (received, partial, *table),
         flops=2 * tokens * width * (2 * model + columns), moved=8 * tokens * width,
     )
     theirs = lax.ppermute(other, "row", partners)
     back = call(
-        functools.partial(backward_kernel, slots, ranks, lines, chunk), "backward",
-        shape((tokens, width + LANES), BF16), (received, out_weight, skip_part, *table),
+        functools.partial(backward_kernel, slots, ranks, lines, chunk, tables), "backward",
+        shape((tokens, width + LANES), BF16), (received, out_weight, skip_part, *table, *kept),
         [pltpu.VMEM((LANES, tokens), F32)],
         flops=2 * tokens * width * (2 * model + 3 * columns), moved=8 * tokens * width,
     )
     group = tokens // ranks
-    size = Tiles(half, model, ranks).size
+    tiles = Tiles(half, model, ranks, group)
     strips = width // LANES + 1
     early = strips // 2
     merged = call(
         functools.partial(merge_kernel, ranks, early), "merge",
-        shape((ranks, early * group + size, LANES), BF16), (mine, theirs, back),
+        shape((ranks, early * group + tiles.size, LANES), BF16), (mine, theirs, back),
         flops=width * model, moved=2 * width * model,
     )
     returned = exchange(merged)
+    whole = tiles.full * tiles.unit
+    late_rows = (strips - early) * group + whole
     summed = call(
-        functools.partial(sum_kernel, early, size), "sum",
-        shape((ranks, (strips - early) * group + size, LANES), BF16), (returned, back),
+        functools.partial(sum_kernel, early, tiles=tiles), "sum",
+        shape((ranks, late_rows, LANES), BF16), (returned, back),
         flops=width * model, moved=2 * width * model,
     )
     last = exchange(summed)
     held = call(
-        half_kernel, "half", shape((ranks, size, LANES), BF16), (last,),
+        functools.partial(half_kernel, (strips - early - 1) * group), "half",
+        shape((ranks, tiles.size, LANES), BF16), (last,),
         flops=width * model, moved=2 * width * model,
     )
     swapped = lax.ppermute(held, "row", partners)
     outs = [
+        shape((width, model), F32),
         shape(features.shape, BF16),
         shape(decay_rate.shape, F32),
         shape(input_proj.shape, F32),
@@ -665,19 +735,22 @@
     if chunk is not None:
         outs.append(shape((width,), F32))
     done = call(
-        functools.partial(finish_kernel, slots, ranks, chunk, early), "finish",
-        tuple(outs), (returned, last, gx_rows, small_rows),
+        functools.partial(finish_kernel, slots, ranks, chunk, early, tiles), "finish",
+        tuple(outs), (returned, last, gx_rows, small_rows, held),
         flops=2 * tokens * tokens * width, moved=8 * tokens * width,
     )
     grad_weight = call(
-        weight_kernel, "weight", shape((width, model), F32), (held, swapped),
+        functools.partial(weight_kernel, tiles), "weight", shape((width, model), F32),
+        (swapped, done[0]),
+        [pltpu.VMEM((half, model), F32), pltpu.SemaphoreType.DMA(())],
         flops=width * model, moved=6 * width * model,
+        whole=[("in", 1), ("out", 0)], aliases={1: 0},
     )
     if chunk is None:
         grad_skip = lax.psum(skip_part, "row").reshape(width)
     else:
-        grad_skip = done[4]
-    return (*done[:4], grad_skip, grad_weight)
+        grad_skip = done[5]
+    return (*done[1:5], grad_skip, grad_weight)
 
 
 def solution(mesh):

time: 57 us -> 56.2 us (0.986)
  blocking collectives: 27.8 us -> 27.2 us
  transfers between devices with their start and end apart: 3 -> 3, of which waited for: 2 -> 2; matrix products, arithmetic and copies ran while one was open for 0% -> 0% of each run, Pallas kernels for 11% -> 10%
where the time goes in v5:
time: 56.2 us; the launch traced here: 55.9 us
  blocking collectives  27.2 us (48%)
  waiting for transfers between devices  10 us (18%)
  Pallas kernels  9.97 us (18%)
  starting transfers between devices  7.81 us (14%)
  between operations  0.78 us (1%)
    all_to_all x2, blocking collectives, exchange(): return lax.all_to_all(array, 'row', split_axis=0, concat_axis=0, tiled=True)  27.2 us
    pallas_call x9, Pallas kernels, call(): pl.pallas_call(kernel, name=name, out_shape=out_shape, in_specs=[spec('in...  9.97 us
    all_to_all x1, waiting for transfers between devices, exchange(): return lax.all_to_all(array, 'row', split_axis=0, concat_axis=0, tiled=True)  9.85 us
    all_to_all x1, starting transfers between devices, exchange(): return lax.all_to_all(array, 'row', split_axis=0, concat_axis=0, tiled=True)  7.56 us
  transfers between devices with their start and end apart: 3, of which 2 were waited for; matrix products, arithmetic and copies ran while one was open for 0% of the time, Pallas kernels for 10%

profile of v5, /device:TPU:0, one launch (start us, length us, event | category | flops | bytes accessed | tf_op | source)
XLA Modules:
  0.0 55.9 jit_solution(4521859366698667020)
XLA Ops:
  0.6 2.0 %pack.1 = bf16[256,896]{1,0:T(8,128)(2,1)} custom-call(bf16[2,128,384]{2,1,0:T(8,128)(2,1)} %feat_ref.3, bf16[2,128,384]{2,1,0:T(8,128)(2,1)} %cot_ref.3, f32[4,6,2,128]{3,2,1,0:T(2,128)} %rate_ref.3, f32[4,16,2,128]{3,2,1,0:T(2,128)} %input_ref.3, f32[4,16,2,128]{3,2,1,0:T(2,128)} %read_ref.3), custom_call_target="tpu_custom_call" | custom-call | flops 100663296 | bytes 786432 | tf_op jit(solution)/shard_map/pack/pallas_call | solution.py:630
  2.6 0.0 copy-start.6
  2.6 0.0 copy-start
  2.6 0.0 copy-start.1
  2.6 0.0 copy-start.2
  2.6 0.0 copy-start.3
  2.7 0.0 copy-start.4
  2.7 0.0 copy-start.5
  2.7 7.6 %all-to-all-start = ((bf16[16,16,896]{2,1,0:T(8,128)(2,1)}), bf16[16,16,896]{2,1,0:T(8,128)(2,1)S(1)}, u32[]{:S(2)}, u32[]{:S(2)}) async-start(bf16[16,16,896]{2,1,0:T(8,128)(2,1)} %bitcast.4), calls=%async_computation | async-start | bytes 917504 | tf_op jit(solution)/shard_map/all_to_all | solution.py:656
  10.2 0.0 copy-done.6
  10.3 0.0 copy-done
  10.3 0.0 copy-done.1
  10.3 0.0 copy-done.2
  10.3 0.0 copy-done.3
  10.3 0.0 copy-done.4
  10.3 0.0 copy-done.5
  10.3 3.3 %rows.1 = (f32[256,384]{1,0:T(8,128)S(1)}, f32[128,256]{1,0:T(8,128)S(1)}, f32[384,384]{1,0:T(8,128)S(1)}, f32[16,128]{1,0:T(8,128)S(1)}, bf16[512,256]{1,0:T(8,...) custom-call(bf16[2,128,384]{2,1,0:T(8,128)(2,1)S(1)} %copy-done.1, ...), custom_call_target="tpu_custom_call" | custom-call | flops 226492416 | bytes 786432 | tf_op jit(solution)/shard_map/rows/pallas_call | solution.py:630
  13.6 9.8 %all-to-all-done = bf16[16,16,896]{2,1,0:T(8,128)(2,1)S(1)} async-done(((bf16[16,16,896]{2,1,0:T(8,128)(2,1)}), bf16[16,16,896]{2,1,0:T(8,128)(2,1)S(1)}, u32[]{:S(2)}, u32[]{:S(2)}) %all-to-all-start) | async-done | bytes 458784 | tf_op jit(solution)/shard_map/all_to_all | solution.py:656
  23.5 1.3 %forward.1 = (f32[192,384]{1,0:T(8,128)S(1)}, bf16[192,384]{1,0:T(8,128)(2,1)S(1)}, bf16[2,256,256]{2,1,0:T(8,128)(2,1)S(1)}, bf16[2,256,384]{2,1,0:T(8,128)(2,1...) custom-call(bf16[256,896]{1,0:T(8,128)(2,1)S(1)} %bitcast.2, ...), custom_call_target="tpu_custom_call" | custom-call | flops 176160768 | bytes 786432 | tf_op jit(solution)/shard_map/forward/pallas_call | solution.py:630
  24.8 0.2 collective-permute-start
  24.9 1.4 %backward.1.back_ref = bf16[256,512]{1,0:T(8,128)(2,1)S(1)} custom-call(bf16[256,896]{1,0:T(8,128)(2,1)S(1)} %bitcast.3, bf16[384,384]{1,0:T(8,128)(2,1)S(1)} %copy-done, f32[16,128]{1,0:T(8,128)S(1)} %get-tuple-element.31.skip_ref, bf16[512,256]{1,0:T(8,128)(2,1)S(1)} %get-tuple-element.26.refs_0_, bf16[256,768]{1,0:T(8,128)(2,1)S(1)} %get-tuple-element.27.refs_1_, ...), custom_call_target="tpu_custom_call" | custom-call | flops 226492416 | bytes 786432 | tf_op jit(solution)/shard_map/backward/pallas_call | solution.py:630
  26.3 0.0 collective-permute-done.theirs_ref
  26.4 14.4 %all_to_all.21.recv_ref.early_ref = bf16[16,72,128]{2,1,0:T(8,128)(2,1)S(1)} all-to-all(bf16[16,72,128]{2,1,0:T(8,128)(2,1)S(1)} %merge.1), channel_id=1, replica_groups=mesh['grp'=2,'row'=16] {'row'}, dimensions={0} | all-to-all | bytes 589824 | tf_op jit(solution)/shard_map/all_to_all | solution.py:656
  40.8 12.8 %all_to_all.22.recv_ref.late_ref = bf16[16,64,128]{2,1,0:T(8,128)(2,1)S(1)} all-to-all(bf16[16,64,128]{2,1,0:T(8,128)(2,1)S(1)} %sum.1), channel_id=1, replica_groups=mesh['grp'=2,'row'=16] {'row'}, dimensions={0} | all-to-all | bytes 524288 | tf_op jit(solution)/shard_map/all_to_all | solution.py:656
  53.7 0.1 collective-permute-start.1
  53.8 1.2 %finish.1 = (f32[384,384]{1,0:T(8,128)}, bf16[2,128,384]{2,1,0:T(8,128)(2,1)}, f32[4,6,2,128]{3,2,1,0:T(2,128)}, f32[4,16,2,128]{3,2,1,0:T(2,128)}, f32[4,16,2,128]{3,2,1,0:T(2,128)}, /*index=5*/f32[384]{0:T(512)}) custom-call(bf16[16,72,128]{2,1,0:T(8,128)(2,1)S(1)} %all_to_all.21.recv_ref.early_ref, bf16[16,64,128]{2,1,0:T(8,128)(2,1)S(1)} %all_to_all.22.recv_ref.late_ref, ...), custom_call_target="tpu_custom_call" | custom-call | flops 50331648 | bytes 786432 | tf_op jit(solution)/shard_map/finish/pallas_call | solution.py:630
  54.9 0.2 collective-permute-done.1.theirs_ref
  55.1 0.7 %weight.1 = f32[384,384]{1,0:T(8,128)} custom-call(bf16[16,40,128]{2,1,0:T(8,128)(2,1)S(1)} %collective-permute-done.1.theirs_ref, f32[384,384]{1,0:T(8,128)} %get-tuple-element.43.weight_in), custom_call_target="tpu_custom_call", output_to_operand_aliasing={{}: (1, {})} | custom-call | flops 147456 | bytes 884736 | tf_op jit(solution)/shard_map/weight/pallas_call | solution.py:630
  (4 shorter events, 0.1 us)
Async XLA Ops:
  2.6 7.6 %copy-start.6 = (f32[384]{0:T(512)S(1)}, f32[384]{0:T(512)}, u32[]{:S(2)}) copy-start(f32[384]{0:T(512)} %param.11) | copy-start | bytes 4612
  2.6 7.6 %copy-start = (bf16[384,384]{1,0:T(8,128)(2,1)S(1)}, bf16[384,384]{1,0:T(8,128)(2,1)}, u32[]{:S(2)}) copy-start(bf16[384,384]{1,0:T(8,128)(2,1)} %weight_ref.3) | copy-start | bytes 884740
  2.6 7.6 %copy-start.1 = (bf16[2,128,384]{2,1,0:T(8,128)(2,1)S(1)}, bf16[2,128,384]{2,1,0:T(8,128)(2,1)}, u32[]{:S(2)}) copy-start(bf16[2,128,384]{2,1,0:T(8,128)(2,1)} %feat_ref.3) | copy-start | bytes 589828
  2.6 7.7 %copy-start.2 = (bf16[2,128,384]{2,1,0:T(8,128)(2,1)S(1)}, bf16[2,128,384]{2,1,0:T(8,128)(2,1)}, u32[]{:S(2)}) copy-start(bf16[2,128,384]{2,1,0:T(8,128)(2,1)} %cot_ref.3) | copy-start | bytes 589828
  2.6 7.7 %copy-start.3 = (f32[4,16,2,128]{3,2,1,0:T(2,128)S(1)}, f32[4,16,2,128]{3,2,1,0:T(2,128)}, u32[]{:S(2)}) copy-start(f32[4,16,2,128]{3,2,1,0:T(2,128)} %input_ref.3) | copy-start | bytes 196612
  2.7 7.7 %copy-start.4 = (f32[4,16,2,128]{3,2,1,0:T(2,128)S(1)}, f32[4,16,2,128]{3,2,1,0:T(2,128)}, u32[]{:S(2)}) copy-start(f32[4,16,2,128]{3,2,1,0:T(2,128)} %read_ref.3) | copy-start | bytes 196612
  2.7 7.7 %copy-start.5 = (f32[4,6,2,128]{3,2,1,0:T(2,128)S(1)}, f32[4,6,2,128]{3,2,1,0:T(2,128)}, u32[]{:S(2)}) copy-start(f32[4,6,2,128]{3,2,1,0:T(2,128)} %rate_ref.3) | copy-start | bytes 73732
  2.7 20.8 %all-to-all-start = ((bf16[16,16,896]{2,1,0:T(8,128)(2,1)}), bf16[16,16,896]{2,1,0:T(8,128)(2,1)S(1)}, u32[]{:S(2)}, u32[]{:S(2)}) async-start(bf16[16,16,896]{2,1,0:T(8,128)(2,1)} %bitcast.4), calls=%async_computation | async-start | bytes 917504 | tf_op jit(solution)/shard_map/all_to_all | solution.py:656
  24.8 1.6 %collective-permute-start = (bf16[192,384]{1,0:T(8,128)(2,1)S(1)}, bf16[192,384]{1,0:T(8,128)(2,1)S(1)}, u32[]{:S(2)}, u32[]{:S(2)}) collective-permute-start(bf16[192,384]{1,0:T(8,128)(2,1)S(1)} %get-tuple-element.30), channel_id=1, source_target_pairs={{0,1},{1,0},{2,3},{3,2},{4,5},{5,4},{6,7},{7,6},{8,9},{9,8},{10,11... | collective-permute-start | bytes 442376 | tf_op jit(solution)/shard_map/ppermute | solution.py:697
  53.7 1.5 %collective-permute-start.1 = (bf16[16,40,128]{2,1,0:T(8,128)(2,1)S(1)}, bf16[16,40,128]{2,1,0:T(8,128)(2,1)S(1)}, u32[]{:S(2)}, u32[]{:S(2)}) collective-permute-start(bf16[16,40,128]{2,1,0:T(8,128)(2,1)S(1)} %half.1.held_ref), channel_id=1, source_target_pairs={{0,1},{1,0},{2,3},{3,2},{4,5},{5,4},{6,7},{7,6},{8,9},{9,8},{10,11... | collective-permute-start | bytes 491528 | tf_op jit(solution)/shard_map/ppermute | solution.py:727

commit v6 on v5

--- a/solution.py
+++ b/solution.py
@@ -299,7 +299,7 @@
                 ((2, tokens, 2 * LANES), BF16), ((2, tokens, width), BF16), values,
                 ((2, tokens, tokens), BF16),
             ]
-            self.shapes = [(2 * tokens, tokens), (2 * LANES, 2 * width), (4 * width, LANES)]
+            self.shapes = [(tokens, tokens), (2 * LANES, 2 * width), (4 * width, LANES)]
 
     def fill(self, refs):
         if not self.short:
@@ -308,10 +308,8 @@
         size = width // slots.heads
         same, reach = reach_of(self.lines, tokens)
         half = jnp.where(same, 0.5, 0.0)
+        refs[0][...] = (reach[0].astype(F32) - half).astype(BF16)
         for way in (0, 1):
-            refs[0][way * tokens : (way + 1) * tokens, :] = (
-                reach[way].astype(F32) - half
-            ).astype(BF16)
             at = iota((LANES, width), 0)
             head = split_index(iota((LANES, width), 1), (slots.heads, size))[0]
             spread = (at == head + slots.rates[way]).astype(F32).astype(BF16)
@@ -347,11 +345,14 @@
         return [(pair[:, :width], pair[:, width:]) for pair in pairs]
 
     def forward(self, feats, kept):
-        slots, tokens, lane = self.slots, self.tokens, self.lane
+        slots, lane = self.slots, self.lane
         width = feats.shape[1]
         narrows, lost, mixed, scores = kept
+        for way in (0, 1):
+            score = nt(self.reads[way], self.params)
+            scores[way] = jnp.where(self.reach[way], score, 0.0).astype(BF16)
         sums = nn(self.tables[0][...], self.params)
-        sums = jnp.where(self.up_lane, sums[tokens:], sums[:tokens])
+        sums = jnp.where(self.up_lane, self.params.astype(F32) - sums, sums)
         sums = sums + pltpu.roll(sums, LANES - (slots.lows[0] - slots.rates[0]), 1)
         rated = (lane >= slots.rates[0]) & (lane < slots.lows[0])
         sums = jnp.where(rated, sums, 0.0)
@@ -361,11 +362,9 @@
         wide = feats.astype(F32)
         out = None
         for way in (0, 1):
-            score = jnp.where(self.reach[way], nt(self.reads[way], self.params), 0.0).astype(BF16)
-            scores[way] = score
             held = (wide * losses[way]).astype(BF16)
             lost[way] = held
-            mix = nn(score, held)
+            mix = nn(scores[way], held)
             mixed[way] = mix
             part = gains[way] * mix
             out = part if out is None else out + part

time: 56.2 us -> 56 us (level)
  no operation moved by 1% of the time
where the time goes in v6:
time: 56 us; the launch traced here: 55.7 us
  blocking collectives  27.2 us (49%)
  waiting for transfers between devices  10.1 us (18%)
  Pallas kernels  9.73 us (17%)
  starting transfers between devices  7.81 us (14%)
  between operations  0.78 us (1%)
    all_to_all x2, blocking collectives, exchange(): return lax.all_to_all(array, 'row', split_axis=0, concat_axis=0, tiled=True)  27.2 us
    all_to_all x1, waiting for transfers between devices, exchange(): return lax.all_to_all(array, 'row', split_axis=0, concat_axis=0, tiled=True)  9.89 us
    pallas_call x9, Pallas kernels, call(): pl.pallas_call(kernel, name=name, out_shape=out_shape, in_specs=[spec('in...  9.73 us
    all_to_all x1, starting transfers between devices, exchange(): return lax.all_to_all(array, 'row', split_axis=0, concat_axis=0, tiled=True)  7.56 us
  transfers between devices with their start and end apart: 3, of which 2 were waited for; matrix products, arithmetic and copies ran while one was open for 0% of the time, Pallas kernels for 10%

profile of v6, /device:TPU:0, one launch (start us, length us, event | category | flops | bytes accessed | tf_op | source)
XLA Modules:
  0.0 55.7 jit_solution(4129988050001642771)
XLA Ops:
  0.6 2.0 %pack.1 = bf16[256,896]{1,0:T(8,128)(2,1)} custom-call(bf16[2,128,384]{2,1,0:T(8,128)(2,1)} %feat_ref.3, bf16[2,128,384]{2,1,0:T(8,128)(2,1)} %cot_ref.3, f32[4,6,2,128]{3,2,1,0:T(2,128)} %rate_ref.3, f32[4,16,2,128]{3,2,1,0:T(2,128)} %input_ref.3, f32[4,16,2,128]{3,2,1,0:T(2,128)} %read_ref.3), custom_call_target="tpu_custom_call" | custom-call | flops 100663296 | bytes 786432 | tf_op jit(solution)/shard_map/pack/pallas_call | solution.py:629
  2.6 0.0 copy-start.6
  2.6 0.0 copy-start
  2.6 0.0 copy-start.1
  2.6 0.0 copy-start.2
  2.6 0.0 copy-start.3
  2.7 0.0 copy-start.4
  2.7 0.0 copy-start.5
  2.7 7.6 %all-to-all-start = ((bf16[16,16,896]{2,1,0:T(8,128)(2,1)}), bf16[16,16,896]{2,1,0:T(8,128)(2,1)S(1)}, u32[]{:S(2)}, u32[]{:S(2)}) async-start(bf16[16,16,896]{2,1,0:T(8,128)(2,1)} %bitcast.4), calls=%async_computation | async-start | bytes 917504 | tf_op jit(solution)/shard_map/all_to_all | solution.py:655
  10.2 0.0 copy-done.6
  10.3 0.0 copy-done
  10.3 0.0 copy-done.1
  10.3 0.0 copy-done.2
  10.3 0.0 copy-done.3
  10.3 0.0 copy-done.4
  10.3 0.0 copy-done.5
  10.3 3.2 %rows.1 = (f32[256,384]{1,0:T(8,128)S(1)}, f32[128,256]{1,0:T(8,128)S(1)}, f32[384,384]{1,0:T(8,128)S(1)}, f32[16,128]{1,0:T(8,128)S(1)}, bf16[256,256]{1,0:T(8,...) custom-call(bf16[2,128,384]{2,1,0:T(8,128)(2,1)S(1)} %copy-done.1, ...), custom_call_target="tpu_custom_call" | custom-call | flops 226492416 | bytes 786432 | tf_op jit(solution)/shard_map/rows/pallas_call | solution.py:629
  13.6 9.9 %all-to-all-done = bf16[16,16,896]{2,1,0:T(8,128)(2,1)S(1)} async-done(((bf16[16,16,896]{2,1,0:T(8,128)(2,1)}), bf16[16,16,896]{2,1,0:T(8,128)(2,1)S(1)}, u32[]{:S(2)}, u32[]{:S(2)}) %all-to-all-start) | async-done | bytes 458784 | tf_op jit(solution)/shard_map/all_to_all | solution.py:655
  23.5 1.1 %forward.1 = (f32[192,384]{1,0:T(8,128)S(1)}, bf16[192,384]{1,0:T(8,128)(2,1)S(1)}, bf16[2,256,256]{2,1,0:T(8,128)(2,1)S(1)}, bf16[2,256,384]{2,1,0:T(8,128)(2,1...) custom-call(bf16[256,896]{1,0:T(8,128)(2,1)S(1)} %bitcast.2, ...), custom_call_target="tpu_custom_call" | custom-call | flops 176160768 | bytes 786432 | tf_op jit(solution)/shard_map/forward/pallas_call | solution.py:629
  24.6 0.2 collective-permute-start
  24.8 1.4 %backward.1.back_ref = bf16[256,512]{1,0:T(8,128)(2,1)S(1)} custom-call(bf16[256,896]{1,0:T(8,128)(2,1)S(1)} %bitcast.3, bf16[384,384]{1,0:T(8,128)(2,1)S(1)} %copy-done, f32[16,128]{1,0:T(8,128)S(1)} %get-tuple-element.31.skip_ref, bf16[256,256]{1,0:T(8,128)(2,1)S(1)} %get-tuple-element.26.refs_0_, bf16[256,768]{1,0:T(8,128)(2,1)S(1)} %get-tuple-element.27.refs_1_, ...), custom_call_target="tpu_custom_call" | custom-call | flops 226492416 | bytes 786432 | tf_op jit(solution)/shard_map/backward/pallas_call | solution.py:629
  26.1 0.0 collective-permute-done.theirs_ref
  26.2 14.4 %all_to_all.21.recv_ref.early_ref = bf16[16,72,128]{2,1,0:T(8,128)(2,1)S(1)} all-to-all(bf16[16,72,128]{2,1,0:T(8,128)(2,1)S(1)} %merge.1), channel_id=1, replica_groups=mesh['grp'=2,'row'=16] {'row'}, dimensions={0} | all-to-all | bytes 589824 | tf_op jit(solution)/shard_map/all_to_all | solution.py:655
  40.6 12.8 %all_to_all.22.recv_ref.late_ref = bf16[16,64,128]{2,1,0:T(8,128)(2,1)S(1)} all-to-all(bf16[16,64,128]{2,1,0:T(8,128)(2,1)S(1)} %sum.1), channel_id=1, replica_groups=mesh['grp'=2,'row'=16] {'row'}, dimensions={0} | all-to-all | bytes 524288 | tf_op jit(solution)/shard_map/all_to_all | solution.py:655
  53.5 0.1 collective-permute-start.1
  53.6 1.2 %finish.1 = (f32[384,384]{1,0:T(8,128)}, bf16[2,128,384]{2,1,0:T(8,128)(2,1)}, f32[4,6,2,128]{3,2,1,0:T(2,128)}, f32[4,16,2,128]{3,2,1,0:T(2,128)}, f32[4,16,2,128]{3,2,1,0:T(2,128)}, /*index=5*/f32[384]{0:T(512)}) custom-call(bf16[16,72,128]{2,1,0:T(8,128)(2,1)S(1)} %all_to_all.21.recv_ref.early_ref, bf16[16,64,128]{2,1,0:T(8,128)(2,1)S(1)} %all_to_all.22.recv_ref.late_ref, ...), custom_call_target="tpu_custom_call" | custom-call | flops 50331648 | bytes 786432 | tf_op jit(solution)/shard_map/finish/pallas_call | solution.py:629
  54.8 0.2 collective-permute-done.1.theirs_ref
  54.9 0.7 %weight.1 = f32[384,384]{1,0:T(8,128)} custom-call(bf16[16,40,128]{2,1,0:T(8,128)(2,1)S(1)} %collective-permute-done.1.theirs_ref, f32[384,384]{1,0:T(8,128)} %get-tuple-element.43.weight_in), custom_call_target="tpu_custom_call", output_to_operand_aliasing={{}: (1, {})} | custom-call | flops 147456 | bytes 884736 | tf_op jit(solution)/shard_map/weight/pallas_call | solution.py:629
  (4 shorter events, 0.1 us)
Async XLA Ops:
  2.6 7.6 %copy-start.6 = (f32[384]{0:T(512)S(1)}, f32[384]{0:T(512)}, u32[]{:S(2)}) copy-start(f32[384]{0:T(512)} %param.11) | copy-start | bytes 4612
  2.6 7.6 %copy-start = (bf16[384,384]{1,0:T(8,128)(2,1)S(1)}, bf16[384,384]{1,0:T(8,128)(2,1)}, u32[]{:S(2)}) copy-start(bf16[384,384]{1,0:T(8,128)(2,1)} %weight_ref.3) | copy-start | bytes 884740
  2.6 7.6 %copy-start.1 = (bf16[2,128,384]{2,1,0:T(8,128)(2,1)S(1)}, bf16[2,128,384]{2,1,0:T(8,128)(2,1)}, u32[]{:S(2)}) copy-start(bf16[2,128,384]{2,1,0:T(8,128)(2,1)} %feat_ref.3) | copy-start | bytes 589828
  2.6 7.7 %copy-start.2 = (bf16[2,128,384]{2,1,0:T(8,128)(2,1)S(1)}, bf16[2,128,384]{2,1,0:T(8,128)(2,1)}, u32[]{:S(2)}) copy-start(bf16[2,128,384]{2,1,0:T(8,128)(2,1)} %cot_ref.3) | copy-start | bytes 589828
  2.6 7.7 %copy-start.3 = (f32[4,16,2,128]{3,2,1,0:T(2,128)S(1)}, f32[4,16,2,128]{3,2,1,0:T(2,128)}, u32[]{:S(2)}) copy-start(f32[4,16,2,128]{3,2,1,0:T(2,128)} %input_ref.3) | copy-start | bytes 196612
  2.7 7.7 %copy-start.4 = (f32[4,16,2,128]{3,2,1,0:T(2,128)S(1)}, f32[4,16,2,128]{3,2,1,0:T(2,128)}, u32[]{:S(2)}) copy-start(f32[4,16,2,128]{3,2,1,0:T(2,128)} %read_ref.3) | copy-start | bytes 196612
  2.7 7.7 %copy-start.5 = (f32[4,6,2,128]{3,2,1,0:T(2,128)S(1)}, f32[4,6,2,128]{3,2,1,0:T(2,128)}, u32[]{:S(2)}) copy-start(f32[4,6,2,128]{3,2,1,0:T(2,128)} %rate_ref.3) | copy-start | bytes 73732
  2.7 20.8 %all-to-all-start = ((bf16[16,16,896]{2,1,0:T(8,128)(2,1)}), bf16[16,16,896]{2,1,0:T(8,128)(2,1)S(1)}, u32[]{:S(2)}, u32[]{:S(2)}) async-start(bf16[16,16,896]{2,1,0:T(8,128)(2,1)} %bitcast.4), calls=%async_computation | async-start | bytes 917504 | tf_op jit(solution)/shard_map/all_to_all | solution.py:655
  24.6 1.6 %collective-permute-start = (bf16[192,384]{1,0:T(8,128)(2,1)S(1)}, bf16[192,384]{1,0:T(8,128)(2,1)S(1)}, u32[]{:S(2)}, u32[]{:S(2)}) collective-permute-start(bf16[192,384]{1,0:T(8,128)(2,1)S(1)} %get-tuple-element.30), channel_id=1, source_target_pairs={{0,1},{1,0},{2,3},{3,2},{4,5},{5,4},{6,7},{7,6},{8,9},{9,8},{10,11... | collective-permute-start | bytes 442376 | tf_op jit(solution)/shard_map/ppermute | solution.py:696
  53.5 1.5 %collective-permute-start.1 = (bf16[16,40,128]{2,1,0:T(8,128)(2,1)S(1)}, bf16[16,40,128]{2,1,0:T(8,128)(2,1)S(1)}, u32[]{:S(2)}, u32[]{:S(2)}) collective-permute-start(bf16[16,40,128]{2,1,0:T(8,128)(2,1)S(1)} %half.1.held_ref), channel_id=1, source_target_pairs={{0,1},{1,0},{2,3},{3,2},{4,5},{5,4},{6,7},{7,6},{8,9},{9,8},{10,11... | collective-permute-start | bytes 491528 | tf_op jit(solution)/shard_map/ppermute | solution.py:726

commit v7 on v6

--- a/solution.py
+++ b/solution.py
@@ -210,11 +210,28 @@
 
 
 def rows_kernel(
-    slots, chunk, tables, feat_ref, cot_ref, weight_ref, skip_ref, rate_ref, input_ref, read_ref,
+    slots, chunk, tables, feat_hbm, cot_hbm, weight_ref, skip_ref, rate_hbm, input_hbm, read_hbm,
     gx_ref, small_ref, part_ref, skip_out_ref, *refs,
 ):
-    *table_refs, rows_ref = refs
+    *table_refs, rows_ref, feat_ref, cot_ref, rate_ref, input_ref, read_ref, arrived = refs
+    ways = pl.ds(0, 2)
+    copies = [
+        pltpu.make_async_copy(source, target, arrived.at[at])
+        for at, (source, target) in enumerate(
+            [
+                (feat_hbm, feat_ref),
+                (cot_hbm, cot_ref),
+                (rate_hbm.at[ways], rate_ref),
+                (input_hbm.at[ways], input_ref),
+                (read_hbm.at[ways], read_ref),
+            ]
+        )
+    ]
+    for copy in copies:
+        copy.start()
     tables.fill(table_refs)
+    for copy in copies:
+        copy.wait()
     tile_rows, columns, width = feat_ref.shape
     tokens = tile_rows * columns
     skip = skip_ref[...]
@@ -622,7 +639,7 @@
     whole=(), aliases=None,
 ):
     def spec(side, at):
-        return pl.BlockSpec(memory_space=pl.ANY if (side, at) in whole else pltpu.VMEM)
+        return pl.BlockSpec(memory_space=pltpu.HBM if (side, at) in whole else pltpu.VMEM)
 
     many = isinstance(out_shape, tuple)
     outs = tuple(spec("out", at) for at in range(len(out_shape) if many else 1))
@@ -678,7 +695,16 @@
             features, out_cotangent, out_weight, skip_gain.reshape(1, width),
             decay_rate, input_proj, read_proj,
         ),
-        [pltpu.VMEM((LANES, columns), F32)],
+        [
+            pltpu.VMEM((LANES, columns), F32),
+            pltpu.VMEM(features.shape, BF16),
+            pltpu.VMEM(out_cotangent.shape, BF16),
+            pltpu.VMEM((2, *decay_rate.shape[1:]), F32),
+            pltpu.VMEM((2, *input_proj.shape[1:]), F32),
+            pltpu.VMEM((2, *read_proj.shape[1:]), F32),
+            pltpu.SemaphoreType.DMA((5,)),
+        ],
+        whole=[("in", at) for at in (0, 1, 4, 5, 6)],
         flops=2 * tokens * width * (2 * model + 3 * columns), moved=8 * tokens * width,
     )
     half = width // 2
@@ -703,7 +729,7 @@
     group = tokens // ranks
     tiles = Tiles(half, model, ranks, group)
     strips = width // LANES + 1
-    early = strips // 2
+    early = strips // 4
     merged = call(
         functools.partial(merge_kernel, ranks, early), "merge",
         shape((ranks, early * group + tiles.size, LANES), BF16), (mine, theirs, back),

time: 56 us -> 55.8 us (level)
  waiting for transfers between devices: 10.1 us -> 9.3 us
  Pallas kernels: 9.73 us -> 10.4 us
    all_to_all x1, waiting for transfers between devices: 9.89 us -> 9.2 us  [exchange(): return lax.all_to_all(array, 'row', split_axis=0, concat_axis=0, tiled=True)]
    pallas_call x9, Pallas kernels: 9.73 us -> 10.4 us  [call(): pl.pallas_call(kernel, name=name, out_shape=out_shape, in_specs=[spec('in...]
  transfers between devices with their start and end apart: 3 -> 3, of which waited for: 2 -> 2; matrix products, arithmetic and copies ran while one was open for 0% -> 0% of each run, Pallas kernels for 10% -> 12%
where the time goes in v7:
time: 55.8 us; the launch traced here: 55.5 us
  blocking collectives  27 us (48%)
  Pallas kernels  10.4 us (19%)
  waiting for transfers between devices  9.3 us (17%)
  starting transfers between devices  7.92 us (14%)
  between operations  0.78 us (1%)
    all_to_all x2, blocking collectives, exchange(): return lax.all_to_all(array, 'row', split_axis=0, concat_axis=0, tiled=True)  27 us
    pallas_call x9, Pallas kernels, call(): pl.pallas_call(kernel, name=name, out_shape=out_shape, in_specs=[spec('in...  10.4 us
    all_to_all x1, waiting for transfers between devices, exchange(): return lax.all_to_all(array, 'row', split_axis=0, concat_axis=0, tiled=True)  9.2 us
    all_to_all x1, starting transfers between devices, exchange(): return lax.all_to_all(array, 'row', split_axis=0, concat_axis=0, tiled=True)  7.56 us
  transfers between devices with their start and end apart: 3, of which 2 were waited for; matrix products, arithmetic and copies ran while one was open for 0% of the time, Pallas kernels for 12%

profile of v7, /device:TPU:0, one launch (start us, length us, event | category | flops | bytes accessed | tf_op | source)
XLA Modules:
  0.0 55.5 jit_solution(3899471690406362838)
XLA Ops:
  0.6 2.0 %pack.1 = bf16[256,896]{1,0:T(8,128)(2,1)} custom-call(bf16[2,128,384]{2,1,0:T(8,128)(2,1)} %feat_hbm.1, bf16[2,128,384]{2,1,0:T(8,128)(2,1)} %cot_hbm.1, f32[4,6,2,128]{3,2,1,0:T(2,128)} %rate_hbm.1, f32[4,16,2,128]{3,2,1,0:T(2,128)} %input_hbm.1, f32[4,16,2,128]{3,2,1,0:T(2,128)} %read_hbm.1), custom_call_target="tpu_custom_call" | custom-call | flops 100663296 | bytes 786432 | tf_op jit(solution)/shard_map/pack/pallas_call | solution.py:646
  2.6 0.0 copy-start.6
  2.6 0.0 copy-start
  2.6 0.0 copy-start.1
  2.6 0.0 copy-start.2
  2.6 0.0 copy-start.3
  2.7 0.0 copy-start.4
  2.7 0.0 copy-start.5
  2.7 7.6 %all-to-all-start = ((bf16[16,16,896]{2,1,0:T(8,128)(2,1)}), bf16[16,16,896]{2,1,0:T(8,128)(2,1)S(1)}, u32[]{:S(2)}, u32[]{:S(2)}) async-start(bf16[16,16,896]{2,1,0:T(8,128)(2,1)} %bitcast.4), calls=%async_computation | async-start | bytes 917504 | tf_op jit(solution)/shard_map/all_to_all | solution.py:672
  10.2 0.0 copy-done.6
  10.3 0.0 copy-done
  10.3 0.0 copy-done.1
  10.3 0.0 copy-done.2
  10.3 0.0 copy-done.3
  10.3 0.0 copy-done.4
  10.3 0.0 copy-done.5
  10.3 3.9 %rows.1 = (f32[256,384]{1,0:T(8,128)S(1)}, f32[128,256]{1,0:T(8,128)S(1)}, f32[384,384]{1,0:T(8,128)S(1)}, f32[16,128]{1,0:T(8,128)S(1)}, bf16[256,256]{1,0:T(8,...) custom-call(bf16[2,128,384]{2,1,0:T(8,128)(2,1)S(1)} %copy-done.1, ...), custom_call_target="tpu_custom_call" | custom-call | flops 226492416 | bytes 786432 | tf_op jit(solution)/shard_map/rows/pallas_call | solution.py:646
  14.3 9.2 %all-to-all-done = bf16[16,16,896]{2,1,0:T(8,128)(2,1)S(1)} async-done(((bf16[16,16,896]{2,1,0:T(8,128)(2,1)}), bf16[16,16,896]{2,1,0:T(8,128)(2,1)S(1)}, u32[]{:S(2)}, u32[]{:S(2)}) %all-to-all-start) | async-done | bytes 458784 | tf_op jit(solution)/shard_map/all_to_all | solution.py:672
  23.5 1.1 %forward.1 = (f32[192,384]{1,0:T(8,128)S(1)}, bf16[192,384]{1,0:T(8,128)(2,1)S(1)}, bf16[2,256,256]{2,1,0:T(8,128)(2,1)S(1)}, bf16[2,256,384]{2,1,0:T(8,128)(2,1...) custom-call(bf16[256,896]{1,0:T(8,128)(2,1)S(1)} %bitcast.2, ...), custom_call_target="tpu_custom_call" | custom-call | flops 176160768 | bytes 786432 | tf_op jit(solution)/shard_map/forward/pallas_call | solution.py:646
  24.6 0.2 collective-permute-start
  24.8 1.4 %backward.1.back_ref = bf16[256,512]{1,0:T(8,128)(2,1)S(1)} custom-call(bf16[256,896]{1,0:T(8,128)(2,1)S(1)} %bitcast.3, bf16[384,384]{1,0:T(8,128)(2,1)S(1)} %copy-done, f32[16,128]{1,0:T(8,128)S(1)} %get-tuple-element.31.skip_ref, bf16[256,256]{1,0:T(8,128)(2,1)S(1)} %get-tuple-element.26.refs_0_, bf16[256,768]{1,0:T(8,128)(2,1)S(1)} %get-tuple-element.27.refs_1_, ...), custom_call_target="tpu_custom_call" | custom-call | flops 226492416 | bytes 786432 | tf_op jit(solution)/shard_map/backward/pallas_call | solution.py:646
  26.1 0.0 collective-permute-done.theirs_ref
  26.2 13.4 %all_to_all.21.recv_ref.early_ref = bf16[16,56,128]{2,1,0:T(8,128)(2,1)S(1)} all-to-all(bf16[16,56,128]{2,1,0:T(8,128)(2,1)S(1)} %merge.1), channel_id=1, replica_groups=mesh['grp'=2,'row'=16] {'row'}, dimensions={0} | all-to-all | bytes 458752 | tf_op jit(solution)/shard_map/all_to_all | solution.py:672
  39.6 13.7 %all_to_all.22.recv_ref.late_ref = bf16[16,80,128]{2,1,0:T(8,128)(2,1)S(1)} all-to-all(bf16[16,80,128]{2,1,0:T(8,128)(2,1)S(1)} %sum.1), channel_id=1, replica_groups=mesh['grp'=2,'row'=16] {'row'}, dimensions={0} | all-to-all | bytes 655360 | tf_op jit(solution)/shard_map/all_to_all | solution.py:672
  53.3 0.2 collective-permute-start.1
  53.5 1.2 %finish.1 = (f32[384,384]{1,0:T(8,128)}, bf16[2,128,384]{2,1,0:T(8,128)(2,1)}, f32[4,6,2,128]{3,2,1,0:T(2,128)}, f32[4,16,2,128]{3,2,1,0:T(2,128)}, f32[4,16,2,128]{3,2,1,0:T(2,128)}, /*index=5*/f32[384]{0:T(512)}) custom-call(bf16[16,56,128]{2,1,0:T(8,128)(2,1)S(1)} %all_to_all.21.recv_ref.early_ref, bf16[16,80,128]{2,1,0:T(8,128)(2,1)S(1)} %all_to_all.22.recv_ref.late_ref, ...), custom_call_target="tpu_custom_call" | custom-call | flops 50331648 | bytes 786432 | tf_op jit(solution)/shard_map/finish/pallas_call | solution.py:646
  54.6 0.1 collective-permute-done.1.theirs_ref
  54.7 0.7 %weight.1 = f32[384,384]{1,0:T(8,128)} custom-call(bf16[16,40,128]{2,1,0:T(8,128)(2,1)S(1)} %collective-permute-done.1.theirs_ref, f32[384,384]{1,0:T(8,128)} %get-tuple-element.43.weight_in), custom_call_target="tpu_custom_call", output_to_operand_aliasing={{}: (1, {})} | custom-call | flops 147456 | bytes 884736 | tf_op jit(solution)/shard_map/weight/pallas_call | solution.py:646
  (4 shorter events, 0.1 us)
Async XLA Ops:
  2.6 7.6 %copy-start.6 = (f32[384]{0:T(512)S(1)}, f32[384]{0:T(512)}, u32[]{:S(2)}) copy-start(f32[384]{0:T(512)} %param.11) | copy-start | bytes 4612
  2.6 7.6 %copy-start = (bf16[384,384]{1,0:T(8,128)(2,1)S(1)}, bf16[384,384]{1,0:T(8,128)(2,1)}, u32[]{:S(2)}) copy-start(bf16[384,384]{1,0:T(8,128)(2,1)} %weight_ref.3) | copy-start | bytes 884740
  2.6 7.6 %copy-start.1 = (bf16[2,128,384]{2,1,0:T(8,128)(2,1)S(1)}, bf16[2,128,384]{2,1,0:T(8,128)(2,1)}, u32[]{:S(2)}) copy-start(bf16[2,128,384]{2,1,0:T(8,128)(2,1)} %feat_hbm.1) | copy-start | bytes 589828
  2.6 7.7 %copy-start.2 = (bf16[2,128,384]{2,1,0:T(8,128)(2,1)S(1)}, bf16[2,128,384]{2,1,0:T(8,128)(2,1)}, u32[]{:S(2)}) copy-start(bf16[2,128,384]{2,1,0:T(8,128)(2,1)} %cot_hbm.1) | copy-start | bytes 589828
  2.6 7.7 %copy-start.3 = (f32[4,16,2,128]{3,2,1,0:T(2,128)S(1)}, f32[4,16,2,128]{3,2,1,0:T(2,128)}, u32[]{:S(2)}) copy-start(f32[4,16,2,128]{3,2,1,0:T(2,128)} %input_hbm.1) | copy-start | bytes 196612
  2.7 7.7 %copy-start.4 = (f32[4,16,2,128]{3,2,1,0:T(2,128)S(1)}, f32[4,16,2,128]{3,2,1,0:T(2,128)}, u32[]{:S(2)}) copy-start(f32[4,16,2,128]{3,2,1,0:T(2,128)} %read_hbm.1) | copy-start | bytes 196612
  2.7 7.7 %copy-start.5 = (f32[4,6,2,128]{3,2,1,0:T(2,128)S(1)}, f32[4,6,2,128]{3,2,1,0:T(2,128)}, u32[]{:S(2)}) copy-start(f32[4,6,2,128]{3,2,1,0:T(2,128)} %rate_hbm.1) | copy-start | bytes 73732
  2.7 20.8 %all-to-all-start = ((bf16[16,16,896]{2,1,0:T(8,128)(2,1)}), bf16[16,16,896]{2,1,0:T(8,128)(2,1)S(1)}, u32[]{:S(2)}, u32[]{:S(2)}) async-start(bf16[16,16,896]{2,1,0:T(8,128)(2,1)} %bitcast.4), calls=%async_computation | async-start | bytes 917504 | tf_op jit(solution)/shard_map/all_to_all | solution.py:672
  24.6 1.6 %collective-permute-start = (bf16[192,384]{1,0:T(8,128)(2,1)S(1)}, bf16[192,384]{1,0:T(8,128)(2,1)S(1)}, u32[]{:S(2)}, u32[]{:S(2)}) collective-permute-start(bf16[192,384]{1,0:T(8,128)(2,1)S(1)} %get-tuple-element.30), channel_id=1, source_target_pairs={{0,1},{1,0},{2,3},{3,2},{4,5},{5,4},{6,7},{7,6},{8,9},{9,8},{10,11... | collective-permute-start | bytes 442376 | tf_op jit(solution)/shard_map/ppermute | solution.py:722
  53.3 1.5 %collective-permute-start.1 = (bf16[16,40,128]{2,1,0:T(8,128)(2,1)S(1)}, bf16[16,40,128]{2,1,0:T(8,128)(2,1)S(1)}, u32[]{:S(2)}, u32[]{:S(2)}) collective-permute-start(bf16[16,40,128]{2,1,0:T(8,128)(2,1)S(1)} %half.1.held_ref), channel_id=1, source_target_pairs={{0,1},{1,0},{2,3},{3,2},{4,5},{5,4},{6,7},{7,6},{8,9},{9,8},{10,11... | collective-permute-start | bytes 491528 | tf_op jit(solution)/shard_map/ppermute | solution.py:752

commit v8 on v6

--- a/solution.py
+++ b/solution.py
@@ -703,7 +703,7 @@
     group = tokens // ranks
     tiles = Tiles(half, model, ranks, group)
     strips = width // LANES + 1
-    early = strips // 2
+    early = strips // 4
     merged = call(
         functools.partial(merge_kernel, ranks, early), "merge",
         shape((ranks, early * group + tiles.size, LANES), BF16), (mine, theirs, back),

time: 56 us -> 55.8 us (level)
  no operation moved by 1% of the time
where the time goes in v8:
time: 55.8 us; the launch traced here: 55.5 us
  blocking collectives  27 us (48%)
  waiting for transfers between devices  9.99 us (18%)
  Pallas kernels  9.73 us (17%)
  starting transfers between devices  7.92 us (14%)
  between operations  0.77 us (1%)
    all_to_all x2, blocking collectives, exchange(): return lax.all_to_all(array, 'row', split_axis=0, concat_axis=0, tiled=True)  27 us
    all_to_all x1, waiting for transfers between devices, exchange(): return lax.all_to_all(array, 'row', split_axis=0, concat_axis=0, tiled=True)  9.89 us
    pallas_call x9, Pallas kernels, call(): pl.pallas_call(kernel, name=name, out_shape=out_shape, in_specs=[spec('in...  9.73 us
    all_to_all x1, starting transfers between devices, exchange(): return lax.all_to_all(array, 'row', split_axis=0, concat_axis=0, tiled=True)  7.56 us
  transfers between devices with their start and end apart: 3, of which 2 were waited for; matrix products, arithmetic and copies ran while one was open for 0% of the time, Pallas kernels for 10%

profile of v8, /device:TPU:0, one launch (start us, length us, event | category | flops | bytes accessed | tf_op | source)
XLA Modules:
  0.0 55.5 jit_solution(3221275836269423690)
XLA Ops:
  0.6 2.0 %pack.1 = bf16[256,896]{1,0:T(8,128)(2,1)} custom-call(bf16[2,128,384]{2,1,0:T(8,128)(2,1)} %feat_ref.3, bf16[2,128,384]{2,1,0:T(8,128)(2,1)} %cot_ref.3, f32[4,6,2,128]{3,2,1,0:T(2,128)} %rate_ref.3, f32[4,16,2,128]{3,2,1,0:T(2,128)} %input_ref.3, f32[4,16,2,128]{3,2,1,0:T(2,128)} %read_ref.3), custom_call_target="tpu_custom_call" | custom-call | flops 100663296 | bytes 786432 | tf_op jit(solution)/shard_map/pack/pallas_call | solution.py:629
  2.6 0.0 copy-start.6
  2.6 0.0 copy-start
  2.6 0.0 copy-start.1
  2.6 0.0 copy-start.2
  2.6 0.0 copy-start.3
  2.7 0.0 copy-start.4
  2.7 0.0 copy-start.5
  2.7 7.6 %all-to-all-start = ((bf16[16,16,896]{2,1,0:T(8,128)(2,1)}), bf16[16,16,896]{2,1,0:T(8,128)(2,1)S(1)}, u32[]{:S(2)}, u32[]{:S(2)}) async-start(bf16[16,16,896]{2,1,0:T(8,128)(2,1)} %bitcast.4), calls=%async_computation | async-start | bytes 917504 | tf_op jit(solution)/shard_map/all_to_all | solution.py:655
  10.2 0.0 copy-done.6
  10.3 0.0 copy-done
  10.3 0.0 copy-done.1
  10.3 0.0 copy-done.2
  10.3 0.0 copy-done.3
  10.3 0.0 copy-done.4
  10.3 0.0 copy-done.5
  10.3 3.2 %rows.1 = (f32[256,384]{1,0:T(8,128)S(1)}, f32[128,256]{1,0:T(8,128)S(1)}, f32[384,384]{1,0:T(8,128)S(1)}, f32[16,128]{1,0:T(8,128)S(1)}, bf16[256,256]{1,0:T(8,...) custom-call(bf16[2,128,384]{2,1,0:T(8,128)(2,1)S(1)} %copy-done.1, ...), custom_call_target="tpu_custom_call" | custom-call | flops 226492416 | bytes 786432 | tf_op jit(solution)/shard_map/rows/pallas_call | solution.py:629
  13.6 9.9 %all-to-all-done = bf16[16,16,896]{2,1,0:T(8,128)(2,1)S(1)} async-done(((bf16[16,16,896]{2,1,0:T(8,128)(2,1)}), bf16[16,16,896]{2,1,0:T(8,128)(2,1)S(1)}, u32[]{:S(2)}, u32[]{:S(2)}) %all-to-all-start) | async-done | bytes 458784 | tf_op jit(solution)/shard_map/all_to_all | solution.py:655
  23.5 1.1 %forward.1 = (f32[192,384]{1,0:T(8,128)S(1)}, bf16[192,384]{1,0:T(8,128)(2,1)S(1)}, bf16[2,256,256]{2,1,0:T(8,128)(2,1)S(1)}, bf16[2,256,384]{2,1,0:T(8,128)(2,1...) custom-call(bf16[256,896]{1,0:T(8,128)(2,1)S(1)} %bitcast.2, ...), custom_call_target="tpu_custom_call" | custom-call | flops 176160768 | bytes 786432 | tf_op jit(solution)/shard_map/forward/pallas_call | solution.py:629
  24.6 0.2 collective-permute-start
  24.8 1.4 %backward.1.back_ref = bf16[256,512]{1,0:T(8,128)(2,1)S(1)} custom-call(bf16[256,896]{1,0:T(8,128)(2,1)S(1)} %bitcast.3, bf16[384,384]{1,0:T(8,128)(2,1)S(1)} %copy-done, f32[16,128]{1,0:T(8,128)S(1)} %get-tuple-element.31.skip_ref, bf16[256,256]{1,0:T(8,128)(2,1)S(1)} %get-tuple-element.26.refs_0_, bf16[256,768]{1,0:T(8,128)(2,1)S(1)} %get-tuple-element.27.refs_1_, ...), custom_call_target="tpu_custom_call" | custom-call | flops 226492416 | bytes 786432 | tf_op jit(solution)/shard_map/backward/pallas_call | solution.py:629
  26.1 0.0 collective-permute-done.theirs_ref
  26.2 13.4 %all_to_all.21.recv_ref.early_ref = bf16[16,56,128]{2,1,0:T(8,128)(2,1)S(1)} all-to-all(bf16[16,56,128]{2,1,0:T(8,128)(2,1)S(1)} %merge.1), channel_id=1, replica_groups=mesh['grp'=2,'row'=16] {'row'}, dimensions={0} | all-to-all | bytes 458752 | tf_op jit(solution)/shard_map/all_to_all | solution.py:655
  39.6 13.7 %all_to_all.22.recv_ref.late_ref = bf16[16,80,128]{2,1,0:T(8,128)(2,1)S(1)} all-to-all(bf16[16,80,128]{2,1,0:T(8,128)(2,1)S(1)} %sum.1), channel_id=1, replica_groups=mesh['grp'=2,'row'=16] {'row'}, dimensions={0} | all-to-all | bytes 655360 | tf_op jit(solution)/shard_map/all_to_all | solution.py:655
  53.3 0.2 collective-permute-start.1
  53.5 1.2 %finish.1 = (f32[384,384]{1,0:T(8,128)}, bf16[2,128,384]{2,1,0:T(8,128)(2,1)}, f32[4,6,2,128]{3,2,1,0:T(2,128)}, f32[4,16,2,128]{3,2,1,0:T(2,128)}, f32[4,16,2,128]{3,2,1,0:T(2,128)}, /*index=5*/f32[384]{0:T(512)}) custom-call(bf16[16,56,128]{2,1,0:T(8,128)(2,1)S(1)} %all_to_all.21.recv_ref.early_ref, bf16[16,80,128]{2,1,0:T(8,128)(2,1)S(1)} %all_to_all.22.recv_ref.late_ref, ...), custom_call_target="tpu_custom_call" | custom-call | flops 50331648 | bytes 786432 | tf_op jit(solution)/shard_map/finish/pallas_call | solution.py:629
  54.6 0.1 collective-permute-done.1.theirs_ref
  54.7 0.7 %weight.1 = f32[384,384]{1,0:T(8,128)} custom-call(bf16[16,40,128]{2,1,0:T(8,128)(2,1)S(1)} %collective-permute-done.1.theirs_ref, f32[384,384]{1,0:T(8,128)} %get-tuple-element.43.weight_in), custom_call_target="tpu_custom_call", output_to_operand_aliasing={{}: (1, {})} | custom-call | flops 147456 | bytes 884736 | tf_op jit(solution)/shard_map/weight/pallas_call | solution.py:629
  (4 shorter events, 0.1 us)
Async XLA Ops:
  2.6 7.6 %copy-start.6 = (f32[384]{0:T(512)S(1)}, f32[384]{0:T(512)}, u32[]{:S(2)}) copy-start(f32[384]{0:T(512)} %param.11) | copy-start | bytes 4612
  2.6 7.6 %copy-start = (bf16[384,384]{1,0:T(8,128)(2,1)S(1)}, bf16[384,384]{1,0:T(8,128)(2,1)}, u32[]{:S(2)}) copy-start(bf16[384,384]{1,0:T(8,128)(2,1)} %weight_ref.3) | copy-start | bytes 884740
  2.6 7.6 %copy-start.1 = (bf16[2,128,384]{2,1,0:T(8,128)(2,1)S(1)}, bf16[2,128,384]{2,1,0:T(8,128)(2,1)}, u32[]{:S(2)}) copy-start(bf16[2,128,384]{2,1,0:T(8,128)(2,1)} %feat_ref.3) | copy-start | bytes 589828
  2.6 7.7 %copy-start.2 = (bf16[2,128,384]{2,1,0:T(8,128)(2,1)S(1)}, bf16[2,128,384]{2,1,0:T(8,128)(2,1)}, u32[]{:S(2)}) copy-start(bf16[2,128,384]{2,1,0:T(8,128)(2,1)} %cot_ref.3) | copy-start | bytes 589828
  2.6 7.7 %copy-start.3 = (f32[4,16,2,128]{3,2,1,0:T(2,128)S(1)}, f32[4,16,2,128]{3,2,1,0:T(2,128)}, u32[]{:S(2)}) copy-start(f32[4,16,2,128]{3,2,1,0:T(2,128)} %input_ref.3) | copy-start | bytes 196612
  2.7 7.7 %copy-start.4 = (f32[4,16,2,128]{3,2,1,0:T(2,128)S(1)}, f32[4,16,2,128]{3,2,1,0:T(2,128)}, u32[]{:S(2)}) copy-start(f32[4,16,2,128]{3,2,1,0:T(2,128)} %read_ref.3) | copy-start | bytes 196612
  2.7 7.7 %copy-start.5 = (f32[4,6,2,128]{3,2,1,0:T(2,128)S(1)}, f32[4,6,2,128]{3,2,1,0:T(2,128)}, u32[]{:S(2)}) copy-start(f32[4,6,2,128]{3,2,1,0:T(2,128)} %rate_ref.3) | copy-start | bytes 73732
  2.7 20.8 %all-to-all-start = ((bf16[16,16,896]{2,1,0:T(8,128)(2,1)}), bf16[16,16,896]{2,1,0:T(8,128)(2,1)S(1)}, u32[]{:S(2)}, u32[]{:S(2)}) async-start(bf16[16,16,896]{2,1,0:T(8,128)(2,1)} %bitcast.4), calls=%async_computation | async-start | bytes 917504 | tf_op jit(solution)/shard_map/all_to_all | solution.py:655
  24.6 1.6 %collective-permute-start = (bf16[192,384]{1,0:T(8,128)(2,1)S(1)}, bf16[192,384]{1,0:T(8,128)(2,1)S(1)}, u32[]{:S(2)}, u32[]{:S(2)}) collective-permute-start(bf16[192,384]{1,0:T(8,128)(2,1)S(1)} %get-tuple-element.30), channel_id=1, source_target_pairs={{0,1},{1,0},{2,3},{3,2},{4,5},{5,4},{6,7},{7,6},{8,9},{9,8},{10,11... | collective-permute-start | bytes 442376 | tf_op jit(solution)/shard_map/ppermute | solution.py:696
  53.3 1.5 %collective-permute-start.1 = (bf16[16,40,128]{2,1,0:T(8,128)(2,1)S(1)}, bf16[16,40,128]{2,1,0:T(8,128)(2,1)S(1)}, u32[]{:S(2)}, u32[]{:S(2)}) collective-permute-start(bf16[16,40,128]{2,1,0:T(8,128)(2,1)S(1)} %half.1.held_ref), channel_id=1, source_target_pairs={{0,1},{1,0},{2,3},{3,2},{4,5},{5,4},{6,7},{7,6},{8,9},{9,8},{10,11... | collective-permute-start | bytes 491528 | tf_op jit(solution)/shard_map/ppermute | solution.py:726
